TPU v7x, 32 devices: a whole 2x2x4 slice. The times are simulated.
32 devices in a mesh: seq: 8 (over z, y), row: 2 (over core), col: 2 (over x).
Axes of the slice: x: 2, y: 2, z: 4, core: 2. Of those that a mesh axis runs over, the one named last changes fastest.
Arguments:
- tokens_in: bfloat16 [4096, 1024], P('seq'), may hold values from -6 to 6
- teacher: bfloat16 [4096, 1024], P('seq', 'col'), may hold values from -6 to 6
- norm_gain: bfloat16 [1024], P('col'), may hold values from 0.5 to 1.5
- in_weight: bfloat16 [1024, 2, 2048], P('col', None, 'row'), may hold values from -0.1875 to 0.1875
- conv_weight: bfloat16 [4, 2048], P(None, ('row', 'col')), may hold values from -3 to 3
- conv_bias: bfloat16 [2048], P(('row', 'col')), may hold values from -3 to 3
- select_weight: bfloat16 [2048, 96], P(('row', 'col')), may hold values from -0.125 to 0.125
- step_weight: bfloat16 [64, 2048], P(None, ('row', 'col')), may hold values from -0.75 to 0.75
- step_bias: bfloat16 [2048], P(('row', 'col')), may hold values from -9 to -2.5
- decay_log: float32 [16, 2048], P(None, ('row', 'col')), may hold values from -4 to 2.5
- skip_gain: bfloat16 [2048], P(('row', 'col')), may hold values from 0.5 to 1.5
- out_weight: bfloat16 [2048, 1024], P('row', 'col'), may hold values from -0.25 to 0.25
- parents: int32 [8], replicated, may hold values from -1 to 5, as said below
- lengths: int32 [8], replicated, may hold values from 256 to 512, as said below
- valid_rows: int32 [8], replicated, may hold values from 1 to 512, as said below
Outputs:
- output: bfloat16 [4096, 1024], P(('seq', 'row'), 'col')
- tokens_grad: float32 [4096, 1024], P(('seq', 'row'), 'col')
- gain_grad: float32 [1024], P('col')
- in_grad: float32 [1024, 2, 2048], P('col', None, 'row')
- conv_grad: float32 [4, 2048], P(None, ('row', 'col'))
- conv_bias_grad: float32 [2048], P(('row', 'col'))
- select_grad: float32 [2048, 96], P(('row', 'col'))
- step_grad: float32 [64, 2048], P(None, ('row', 'col'))
- step_bias_grad: float32 [2048], P(('row', 'col'))
- decay_grad: float32 [16, 2048], P(None, ('row', 'col'))
- skip_grad: float32 [2048], P(('row', 'col'))
- out_grad: float32 [2048, 1024], P('row', 'col')
Inputs may be any that keep to these rules, and one draw needn't show every extreme that they name: parents[0] = -1 and is the only root; for i >= 1, 0 <= parents[i] < i; the last segment's parent is the root. `lengths`: one segment has exactly 512 live slots and another exactly 256. valid_rows[i] <= lengths[i]; one segment has 512 and another 1.
All inputs are finite; a program needn't handle non-finite values.
Results may differ from a plain program's by a relative error of at most 0.014.
Values may be sent and summed in bfloat16 or wider, within the bound.
A program may use at most 192 MiB of HBM per device.

v0:
```python
import functools

import jax
import jax.numpy as jnp
from jax import lax
from jax.experimental import pallas as pl
from jax.experimental.pallas import tpu as pltpu
from jax.sharding import PartitionSpec as P

MESH = pl.DeviceIdType.MESH
F32 = jnp.float32
BF16 = jnp.bfloat16
norm_epsilon = 1e-05
spans = 8
lanes = 128
log2e = 1.4426950408889634
vmem_bytes = 60 * 1024 * 1024


def vmem_spec():
    return pl.BlockSpec(memory_space=pltpu.VMEM)


def smem_spec():
    return pl.BlockSpec(memory_space=pltpu.SMEM)


def struct(shape, dtype):
    return jax.ShapeDtypeStruct(shape, dtype)


def dot(a, b):
    return jnp.dot(a, b, preferred_element_type=F32)


def dot_tn(a, b):
    return lax.dot_general(a, b, (((0,), (0,)), ((), ())), preferred_element_type=F32)


def dot_nt(a, b):
    return lax.dot_general(a, b, (((1,), (1,)), ((), ())), preferred_element_type=F32)


def sigmoid(v):
    return 1.0 / (1.0 + jnp.exp(-v))


def slope_of(v, sigma):
    return sigma * (1.0 + v * (1.0 - sigma))


def to_steps(rows, steps):
    place = lax.broadcasted_iota(jnp.int32, (rows, rows), 0)
    token = lax.broadcasted_iota(jnp.int32, (rows, rows), 1)
    return (token == (place % spans) * steps + place // spans).astype(F32).astype(BF16)


def to_tokens(rows, steps):
    token = lax.broadcasted_iota(jnp.int32, (rows, rows), 0)
    place = lax.broadcasted_iota(jnp.int32, (rows, rows), 1)
    return (token == (place % spans) * steps + place // spans).astype(F32).astype(BF16)


def step_tokens(rows, steps):
    place = lax.broadcasted_iota(jnp.int32, (rows, 1), 0)
    return (place % spans) * steps + place // spans


def spread_matrix(states):
    row = lax.broadcasted_iota(jnp.int32, (2 * states, states * lanes), 0)
    col = lax.broadcasted_iota(jnp.int32, (2 * states, states * lanes), 1)
    return (row % states == col // lanes).astype(F32).astype(BF16)


def gather_matrix(states):
    row = lax.broadcasted_iota(jnp.int32, (states * lanes, states), 0)
    col = lax.broadcasted_iota(jnp.int32, (states * lanes, states), 1)
    return (row // lanes == col).astype(F32).astype(BF16)


def spread(values, states):
    high = values.astype(BF16)
    rest = (values - high.astype(F32)).astype(BF16)
    return dot(jnp.concatenate([high, rest], axis=1), spread_matrix(states))


def shift_spans(values, amount):
    return jnp.roll(values, amount, axis=values.ndim - 2)


def span_index(shape):
    return lax.broadcasted_iota(jnp.int32, shape, len(shape) - 2)


def run_kernel(kernel, outs, args, name, scratch=(), specs=None, flops=0, collective=None):
    params = dict(vmem_limit_bytes=vmem_bytes)
    if collective is not None:
        params.update(collective_id=collective, has_side_effects=True)
    return pl.pallas_call(
        kernel,
        out_shape=outs,
        in_specs=[
            smem_spec() if a.dtype == jnp.int32 else vmem_spec() for a in args
        ],
        out_specs=jax.tree.map(lambda _: vmem_spec(), outs),
        scratch_shapes=list(scratch),
        compiler_params=pltpu.CompilerParams(**params),
        cost_estimate=pl.CostEstimate(
            flops=int(flops),
            transcendentals=0,
            bytes_accessed=int(sum(a.size * a.dtype.itemsize for a in args)),
        ),
        name=name,
    )(*args)


def barrier_with(peers):
    barrier = pltpu.get_barrier_semaphore()
    for peer in peers:
        pl.semaphore_signal(barrier, inc=1, device_id=peer, device_id_type=MESH)
    pl.semaphore_wait(barrier, len(peers))


def remote(src, dst, send, recv, peer):
    return pltpu.make_async_remote_copy(
        src_ref=src, dst_ref=dst, send_sem=send, recv_sem=recv, device_id=peer, device_id_type=MESH
    )


def row_peer():
    return {"row": 1 - lax.axis_index("row")}


def col_peer():
    return {"col": 1 - lax.axis_index("col")}


def entry_kernel(tail_ref, wi_ref, gain_ref, tails_ref, wo_ref, gain_o_ref, tsend, trecv, csend, crecv):
    count = tails_ref.shape[0]
    me = lax.axis_index("seq")
    peers = [{"seq": lax.rem(me + j, count)} for j in range(1, count)]
    barrier_with([col_peer()] + peers)
    copies = []
    for j, peer in enumerate(peers):
        copies.append(remote(tail_ref, tails_ref.at[me], tsend.at[j], trecv.at[j], peer))
    copies.append(remote(gain_ref, gain_o_ref, csend.at[0], crecv.at[0], col_peer()))
    copies.append(remote(wi_ref, wo_ref, csend.at[1], crecv.at[1], col_peer()))
    for copy in copies:
        copy.start()
    tails_ref[me] = tail_ref[...]
    for copy in copies:
        copy.wait()


def entry_exchange(tail, wi_send, gain_send, count):
    return run_kernel(
        entry_kernel,
        (
            struct((count,) + tail.shape, tail.dtype),
            struct(wi_send.shape, wi_send.dtype),
            struct(gain_send.shape, gain_send.dtype),
        ),
        (tail, wi_send, gain_send),
        "entry_exchange",
        scratch=[
            pltpu.SemaphoreType.DMA((count,)),
            pltpu.SemaphoreType.DMA((count,)),
            pltpu.SemaphoreType.DMA((2,)),
            pltpu.SemaphoreType.DMA((2,)),
        ],
        collective=0,
    )


def seq_gather_kernel(x_ref, o_ref, send, recv):
    count = o_ref.shape[0]
    me = lax.axis_index("seq")
    peers = [{"seq": lax.rem(me + j, count)} for j in range(1, count)]
    barrier_with(peers)
    copies = [
        remote(x_ref, o_ref.at[me], send.at[j], recv.at[j], peer) for j, peer in enumerate(peers)
    ]
    for copy in copies:
        copy.start()
    o_ref[me] = x_ref[...]
    for copy in copies:
        copy.wait()


def seq_gather(x, count, collective, name):
    return run_kernel(
        seq_gather_kernel,
        struct((count,) + x.shape, x.dtype),
        (x,),
        name,
        scratch=[pltpu.SemaphoreType.DMA((count,)), pltpu.SemaphoreType.DMA((count,))],
        collective=collective,
    )


def quad_sum_kernel(x_ref, o_ref, from_row, to_col, from_col, send, recv):
    barrier_with([row_peer(), col_peer()])
    first = remote(x_ref, from_row, send.at[0], recv.at[0], row_peer())
    first.start()
    first.wait()
    pair = x_ref[...] + from_row[...]
    to_col[...] = pair.astype(BF16)
    second = remote(to_col, from_col, send.at[1], recv.at[1], col_peer())
    second.start()
    o_ref[...] = pair
    second.wait()
    o_ref[...] += from_col[...].astype(F32)


def quad_sum(x, collective, name):
    return run_kernel(
        quad_sum_kernel,
        struct(x.shape, F32),
        (x,),
        name,
        scratch=[
            pltpu.VMEM(x.shape, F32),
            pltpu.VMEM(x.shape, BF16),
            pltpu.VMEM(x.shape, BF16),
            pltpu.SemaphoreType.DMA((2,)),
            pltpu.SemaphoreType.DMA((2,)),
        ],
        collective=collective,
    )


def middle_kernel(
    part_ref, tok_ref, teach_ref, ints_ref, scale_ref,
    out_ref, cot_ref, low_ref,
    from_row, to_col, from_col, send, recv,
):
    half = tok_ref.shape[0]
    row = lax.axis_index("row")
    mine = pl.multiple_of(row * half, half)
    other = pl.multiple_of((1 - row) * half, half)
    barrier_with([row_peer(), col_peer()])
    first = [
        remote(part_ref.at[h, pl.ds(other, half), :], from_row.at[h], send.at[h], recv.at[h], row_peer())
        for h in (1, 0)
    ]
    for copy in first:
        copy.start()
    first[0].wait()
    to_col[...] = (
        part_ref[1, pl.ds(mine, half), :].astype(F32) + from_row[1].astype(F32)
    ).astype(BF16)
    second = remote(to_col, from_col, send.at[2], recv.at[2], col_peer())
    second.start()
    first[1].wait()
    tile = part_ref[0, pl.ds(mine, half), :].astype(F32) + from_row[0].astype(F32)
    tile = tile + tok_ref[...].astype(F32)
    second.wait()
    result = tile + from_col[...].astype(F32)
    out_ref[...] = result.astype(BF16)
    positions = mine + lax.broadcasted_iota(jnp.int32, (half, 1), 0)
    counted = (positions < ints_ref[0]).astype(F32) * scale_ref[0:1, 0:1]
    cot = (result - teach_ref[...].astype(F32)) * counted
    cot_ref[...] = cot
    low_ref[0, pl.ds(mine, half), :] = cot.astype(BF16)
    third = [
        remote(low_ref.at[0, pl.ds(mine, half), :], low_ref.at[1, pl.ds(mine, half), :], send.at[3], recv.at[3], col_peer()),
        remote(low_ref.at[0, pl.ds(mine, half), :], low_ref.at[0, pl.ds(mine, half), :], send.at[4], recv.at[4], row_peer()),
    ]
    for copy in third:
        copy.start()
    third[0].wait()
    fourth = remote(low_ref.at[1, pl.ds(mine, half), :], low_ref.at[1, pl.ds(mine, half), :], send.at[5], recv.at[5], row_peer())
    fourth.start()
    third[1].wait()
    fourth.wait()


def middle_exchange(part, tok_tile, teach_tile, my_valid, scale):
    _, rows, width = part.shape
    half = rows // 2
    return run_kernel(
        middle_kernel,
        (struct((half, width), BF16), struct((half, width), F32), struct((2, rows, width), BF16)),
        (part, tok_tile, teach_tile, my_valid, scale),
        "middle_exchange",
        scratch=[
            pltpu.VMEM((2, half, width), BF16),
            pltpu.VMEM((half, width), BF16),
            pltpu.VMEM((half, width), BF16),
            pltpu.SemaphoreType.DMA((6,)),
            pltpu.SemaphoreType.DMA((6,)),
        ],
        collective=3,
    )


def hidden_kernel(part_ref, tail_ref, out_ref, tout_ref, from_row, trow, to_col, from_col, tcol, tfrom, send, recv):
    half = out_ref.shape[0]
    row = lax.axis_index("row")
    mine = pl.multiple_of(row * half, half)
    other = pl.multiple_of((1 - row) * half, half)
    barrier_with([row_peer(), col_peer()])
    first = [
        remote(part_ref.at[h, pl.ds(other, half), :], from_row.at[h], send.at[h], recv.at[h], row_peer())
        for h in (1, 0)
    ]
    first.append(remote(tail_ref, trow, send.at[2], recv.at[2], row_peer()))
    for copy in (first[2], first[0], first[1]):
        copy.start()
    first[2].wait()
    tails = tail_ref[...] + trow[...]
    tcol[...] = tails[1]
    last = remote(tcol, tfrom, send.at[3], recv.at[3], col_peer())
    last.start()
    first[0].wait()
    to_col[...] = (
        part_ref[1, pl.ds(mine, half), :].astype(F32) + from_row[1].astype(F32)
    ).astype(BF16)
    second = remote(to_col, from_col, send.at[4], recv.at[4], col_peer())
    second.start()
    first[1].wait()
    out_ref[...] = part_ref[0, pl.ds(mine, half), :].astype(F32) + from_row[0].astype(F32)
    last.wait()
    tout_ref[...] = tails[0] + tfrom[...]
    second.wait()
    out_ref[...] += from_col[...].astype(F32)


def hidden_exchange(part, tail):
    _, rows, width = part.shape
    half = rows // 2
    return run_kernel(
        hidden_kernel,
        (struct((half, width), F32), struct(tail.shape[1:], F32)),
        (part, tail),
        "hidden_exchange",
        scratch=[
            pltpu.VMEM((2, half, width), BF16),
            pltpu.VMEM(tail.shape, F32),
            pltpu.VMEM((half, width), BF16),
            pltpu.VMEM((half, width), BF16),
            pltpu.VMEM(tail.shape[1:], F32),
            pltpu.VMEM(tail.shape[1:], F32),
            pltpu.SemaphoreType.DMA((5,)),
            pltpu.SemaphoreType.DMA((5,)),
        ],
        collective=5,
    )


def finish_kernel(
    hid_ref, tails_ref, tok_ref, toko_ref, gain_ref, cot_ref, parents_ref, lengths_ref,
    tg_ref, gg_ref, mean_out, mean_in, gain_out, gain_in, send, recv, *, width
):
    half = tok_ref.shape[0]
    count, margin8 = tails_ref.shape[0], tails_ref.shape[1]
    row = lax.axis_index("row")
    me = lax.axis_index("seq")
    barrier_with([row_peer(), col_peer()])
    positions = row * half + lax.broadcasted_iota(jnp.int32, (half, margin8), 0)
    slot = lax.broadcasted_iota(jnp.int32, (half, margin8), 1)
    hidden = hid_ref[...]
    length = lengths_ref[me]
    own_tail = jnp.zeros(tails_ref.shape[1:], F32)
    for child in range(count):
        is_child = (parents_ref[child] == me).astype(F32)
        own_tail = own_tail + is_child * tails_ref[child].astype(F32)
    place = ((positions == length - 3 + slot) & (slot < 3)).astype(F32)
    hidden = hidden + jnp.dot(place, own_tail, preferred_element_type=F32, precision=lax.Precision.HIGHEST)
    tok = tok_ref[...].astype(F32)
    toko = toko_ref[...].astype(F32)
    total = jnp.sum(tok * tok, axis=1, keepdims=True) + jnp.sum(toko * toko, axis=1, keepdims=True)
    inv = lax.rsqrt(total / width + norm_epsilon)
    normed = tok * inv
    gain_out[...] = jnp.broadcast_to(jnp.sum(hidden * normed, axis=0, keepdims=True), gain_out.shape)
    scaled = hidden * gain_ref[0:1, :].astype(F32)
    mean = jnp.sum(scaled * normed, axis=1, keepdims=True)
    ones = jnp.ones((8, lanes), F32)
    mean_out[...] = lax.dot_general(
        ones, jnp.broadcast_to(mean / lanes, (half, lanes)), (((1,), (1,)), ((), ())),
        preferred_element_type=F32, precision=lax.Precision.HIGHEST,
    )
    copies = [
        remote(mean_out, mean_in, send.at[0], recv.at[0], col_peer()),
        remote(gain_out, gain_in, send.at[1], recv.at[1], row_peer()),
    ]
    for copy in copies:
        copy.start()
    for copy in copies:
        copy.wait()
    other = lax.dot_general(
        mean_in[...], jnp.full((8, lanes), 0.125, F32), (((0,), (0,)), ((), ())),
        preferred_element_type=F32, precision=lax.Precision.HIGHEST,
    )
    mean = (mean + other[:, 0:1]) / width
    tg_ref[...] = cot_ref[...] + inv * (scaled - normed * mean)
    gg_ref[...] = gain_out[...] + gain_in[...]


def finish_exchange(hid, tails, tok, toko, gain, cot, parents, lengths, width):
    half, cols = hid.shape
    return run_kernel(
        functools.partial(finish_kernel, width=width),
        (struct((half, cols), F32), struct((8, cols), F32)),
        (hid, tails, tok, toko, gain, cot, parents, lengths),
        "finish_exchange",
        scratch=[
            pltpu.VMEM((8, half), F32),
            pltpu.VMEM((8, half), F32),
            pltpu.VMEM((8, cols), F32),
            pltpu.VMEM((8, cols), F32),
            pltpu.SemaphoreType.DMA((2,)),
            pltpu.SemaphoreType.DMA((2,)),
        ],
        collective=6,
    )


def forward_in_kernel(
    tok_ref, toko_ref, tails_ref, tailso_ref, gain_ref, gaino_ref, wi_ref, wio_ref,
    cw_ref, cb_ref, sw_ref, ints_ref,
    hid_ref, hidt_ref, ext_ref, act_ref, sel_ref,
):
    rows, half = tok_ref.shape
    steps = rows // spans
    width = 2 * half
    parent = jnp.maximum(ints_ref[0], 0)
    present = (ints_ref[0] >= 0).astype(F32)
    gain = gain_ref[0:1, :].astype(F32)
    gaino = gaino_ref[0:1, :].astype(F32)

    def hidden_of(own, other):
        own = own.astype(F32)
        other = other.astype(F32)
        total = jnp.sum(own * own, axis=1, keepdims=True) + jnp.sum(other * other, axis=1, keepdims=True)
        inv = lax.rsqrt(total / width + norm_epsilon)
        return (own * inv * gain).astype(BF16), (other * inv * gaino).astype(BF16)

    hid, hido = hidden_of(tok_ref[...], toko_ref[...])
    order = to_steps(rows, steps)
    hid = dot(order, hid).astype(BF16)
    hido = dot(order, hido).astype(BF16)
    hid_ref[0] = hid
    hid_ref[1] = hido
    inner = dot(hid, wi_ref[...]) + dot(hido, wio_ref[...])
    tail, tailo = hidden_of(tails_ref[parent], tailso_ref[parent])
    hidt_ref[0] = tail
    hidt_ref[1] = tailo
    tail_inner = (dot(tail, wi_ref[...]) + dot(tailo, wio_ref[...])) * present
    last = inner[rows - 3 * spans :]
    first_span = lax.broadcasted_iota(jnp.int32, (spans, half), 0) == 0
    for j in range(3):
        block = jnp.roll(last[j * spans : (j + 1) * spans], 1, axis=0)
        ext_ref[j * spans : (j + 1) * spans, :] = jnp.where(
            first_span, jnp.broadcast_to(tail_inner[5 + j : 6 + j, :], (spans, half)), block
        )
    ext_ref[3 * spans :, :] = inner
    taps = cw_ref[...].astype(F32)
    pre = jnp.broadcast_to(cb_ref[0:1, :].astype(F32), (rows, half))
    for k in range(4):
        pre = pre + taps[k : k + 1, :] * ext_ref[k * spans : k * spans + rows, :]
    act = (pre * sigmoid(pre)).astype(BF16)
    act_ref[...] = act
    sel_ref[...] = dot(act, sw_ref[...])


def conv_pre(ext_ref, cw_ref, cb_ref, rows, half):
    taps = cw_ref[...].astype(F32)
    pre = jnp.broadcast_to(cb_ref[0:1, :].astype(F32), (rows, half))
    for k in range(4):
        pre = pre + taps[k : k + 1, :] * ext_ref[k * spans : k * spans + rows, :]
    return pre


def group_ds(group):
    return pl.ds(pl.multiple_of(group * lanes, lanes), lanes)


def step_ds(step):
    return pl.ds(pl.multiple_of(step * spans, spans), spans)


def decay_rows(decay_log_ref, decay_b, scale):
    states, width = decay_log_ref.shape
    rate = -jnp.exp(decay_log_ref[...]) * scale
    for n in range(states):
        decay_b[n] = jnp.broadcast_to(rate[n : n + 1, :], (spans, width))


def span_sum_kernel_part(delta_ref, steps):
    total = delta_ref[0:spans, :]
    for s in range(1, steps):
        total = total + delta_ref[s * spans : (s + 1) * spans, :]
    return total


def forward_ends_kernel(
    sel_ref, tw_ref, tb_ref, dl_ref, act_ref, ints_ref,
    delta_ref, pre_ref, reach_ref, cum_ref, send_ref,
    drive, b_ref, rate_ref,
):
    rows, width = act_ref.shape
    steps = rows // spans
    states = dl_ref.shape[0]
    rank = tw_ref.shape[0]
    length = ints_ref[0]
    sel = sel_ref[...]
    step_pre = dot(sel[:, :rank].astype(BF16), tw_ref[...]) + tb_ref[0:1, :].astype(F32)
    pre_ref[...] = step_pre
    live = (step_tokens(rows, steps) < length).astype(F32)
    delta = (jnp.maximum(step_pre, 0.0) + jnp.log1p(jnp.exp(-jnp.abs(step_pre)))) * live
    delta_ref[...] = delta
    drive[...] = delta * act_ref[...].astype(F32)
    b_ref[...] = spread(sel[:, rank : rank + states], states)
    decay_rows(dl_ref, rate_ref, log2e)

    for group in range(width // lanes):
        here = slice(group * lanes, (group + 1) * lanes)

        def advance(step, carry):
            d = delta_ref[step_ds(step), here]
            w = drive[step_ds(step), here]
            out = []
            for n in range(states):
                a = jnp.exp2(d * rate_ref[n, :, here])
                out.append(a * carry[n] + w * b_ref[step_ds(step), n * lanes : (n + 1) * lanes])
            return tuple(out)

        ends = lax.fori_loop(0, steps, advance, (jnp.zeros((spans, lanes), F32),) * states)
        for n in range(states):
            reach_ref[n, :, here] = ends[n]

    total = span_sum_kernel_part(delta_ref, steps)
    index2 = span_index((spans, width))
    part = total
    shift = 1
    while shift < spans:
        inside = index2 >= shift
        for n in range(states):
            own = reach_ref[n]
            earlier = jnp.where(inside, shift_spans(own, shift), 0.0)
            reach_ref[n] = own + jnp.exp2(part * rate_ref[n]) * earlier
        part = part + jnp.where(inside, shift_spans(part, shift), 0.0)
        shift *= 2
    cum_ref[...] = part
    sums = part[spans - 1 : spans, :]
    high = sums.astype(BF16)
    mid = (sums - high.astype(F32)).astype(BF16)
    low = (sums - high.astype(F32) - mid.astype(F32)).astype(BF16)
    ends = jnp.concatenate([reach_ref[n, spans - 1 : spans, :] for n in range(states)], axis=0)
    extra = jnp.concatenate(
        [high.astype(F32), mid.astype(F32), low.astype(F32), jnp.zeros((5, width), F32)], axis=0
    )
    send_ref[...] = jnp.concatenate([ends, extra], axis=0).astype(BF16)


def segment_sum(table_ref, index, states):
    block = table_ref[index].astype(F32)
    return block[:states], block[states : states + 1] + block[states + 1 : states + 2] + block[states + 2 : states + 3]


def forward_out_kernel(
    table_ref, parents_ref, me_ref, dl_ref, reach_ref, cum_ref, delta_ref, act_ref, sel_ref,
    hid_ref, wg_ref, wgo_ref, skip_ref, ow_ref, owo_ref,
    starts_ref, mpre_ref, gate_ref, mixed_ref, part_ref,
    finals, drive, b_ref, c_ref, rate_ref,
):
    rows, width = act_ref.shape
    steps = rows // spans
    states = dl_ref.shape[0]
    rank = sel_ref.shape[1] - 2 * states
    count = table_ref.shape[0]
    me = me_ref[0]
    decay_rows(dl_ref, rate_ref, log2e)
    rate = -jnp.exp(dl_ref[...]) * log2e

    def start_of(target):
        above = parents_ref[target]
        return finals[jnp.maximum(above, 0)] * (above >= 0).astype(F32)

    def visit(target, carry):
        end, total = segment_sum(table_ref, target, states)
        finals[target] = jnp.exp2(rate * total) * start_of(target) + end
        return carry

    finals[0] = jnp.zeros(finals.shape[1:], F32)
    lax.fori_loop(0, count, visit, 0)
    start = start_of(me)
    sel = sel_ref[...]
    drive[...] = delta_ref[...] * act_ref[...].astype(F32)
    b_ref[...] = spread(sel[:, rank : rank + states], states)
    c_ref[...] = spread(sel[:, rank + states :], states)
    index2 = span_index((spans, width))
    cum = jnp.where(index2 >= 1, shift_spans(cum_ref[...], 1), 0.0)
    for n in range(states):
        earlier = jnp.where(index2 >= 1, shift_spans(reach_ref[n], 1), 0.0)
        starts_ref[n] = jnp.exp2(cum * rate_ref[n]) * start[n : n + 1, :] + earlier

    for group in range(width // lanes):
        here = slice(group * lanes, (group + 1) * lanes)

        def advance(step, carry):
            d = delta_ref[step_ds(step), here]
            w = drive[step_ds(step), here]
            out = []
            reads = [None] * 4
            for n in range(states):
                a = jnp.exp2(d * rate_ref[n, :, here])
                now = a * carry[n] + w * b_ref[step_ds(step), n * lanes : (n + 1) * lanes]
                out.append(now)
                term = c_ref[step_ds(step), n * lanes : (n + 1) * lanes] * now
                reads[n % 4] = term if reads[n % 4] is None else reads[n % 4] + term
            mpre_ref[step_ds(step), here] = (reads[0] + reads[1]) + (reads[2] + reads[3])
            return tuple(out)

        lax.fori_loop(0, steps, advance, tuple(starts_ref[n, :, here] for n in range(states)))

    gate = dot(hid_ref[0], wg_ref[...]) + dot(hid_ref[1], wgo_ref[...])
    gate_ref[...] = gate
    mixed_pre = mpre_ref[...] + skip_ref[0:1, :].astype(F32) * act_ref[...].astype(F32)
    mpre_ref[...] = mixed_pre
    mixed = (mixed_pre * (gate * sigmoid(gate))).astype(BF16)
    mixed_ref[...] = mixed
    natural = dot(to_tokens(rows, steps), mixed).astype(BF16)
    part_ref[0] = dot(natural, ow_ref[...]).astype(BF16)
    part_ref[1] = dot(natural, owo_ref[...]).astype(BF16)


def backward_in_kernel(
    cot_ref, mixed_ref, ow_ref, owo_ref, gate_ref, mpre_ref, act_ref, skip_ref, sel_ref,
    delta_ref, dl_ref, cum_ref, hid_ref,
    og_ref, ggrad_ref, ig_ref, pgrad_ref, sgrad_ref, back_ref, flow_ref,
    c_ref, rate_ref,
):
    rows, width = act_ref.shape
    steps = rows // spans
    states = dl_ref.shape[0]
    rank = sel_ref.shape[1] - 2 * states
    order = to_steps(rows, steps)
    cot = dot(order, cot_ref[0]).astype(BF16)
    coto = dot(order, cot_ref[1]).astype(BF16)
    mixed_grad = dot_nt(cot, ow_ref[...]) + dot_nt(coto, owo_ref[...])
    gate = gate_ref[...]
    sigma = sigmoid(gate)
    pre_grad = mixed_grad * (gate * sigma)
    pgrad_ref[...] = pre_grad
    gate_grad = (mixed_grad * mpre_ref[...] * slope_of(gate, sigma)).astype(BF16)
    ggrad_ref[...] = gate_grad
    sgrad_ref[...] = jnp.broadcast_to(
        jnp.sum(pre_grad * act_ref[...].astype(F32), axis=0, keepdims=True), sgrad_ref.shape
    )
    c_ref[...] = spread(sel_ref[:, rank + states :], states)
    decay_rows(dl_ref, rate_ref, log2e)

    for group in range(width // lanes):
        here = slice(group * lanes, (group + 1) * lanes)

        def retreat(back, carry):
            step = steps - 1 - back
            d = delta_ref[step_ds(step), here]
            p = pgrad_ref[step_ds(step), here]
            out = []
            for n in range(states):
                a = jnp.exp2(d * rate_ref[n, :, here])
                out.append(a * (c_ref[step_ds(step), n * lanes : (n + 1) * lanes] * p + carry[n]))
            return tuple(out)

        flows = lax.fori_loop(0, steps, retreat, (jnp.zeros((spans, lanes), F32),) * states)
        for n in range(states):
            back_ref[n, :, here] = flows[n]

    index2 = span_index((spans, width))
    cum = cum_ref[...]
    part = cum - jnp.where(index2 >= 1, shift_spans(cum, 1), 0.0)
    shift = 1
    while shift < spans:
        inside = index2 < spans - shift
        for n in range(states):
            own = back_ref[n]
            later = jnp.where(inside, shift_spans(own, -shift), 0.0)
            back_ref[n] = own + jnp.exp2(part * rate_ref[n]) * later
        part = part + jnp.where(inside, shift_spans(part, -shift), 0.0)
        shift *= 2
    flow_ref[...] = jnp.concatenate(
        [back_ref[n, 0:1, :] for n in range(states)], axis=0
    ).astype(BF16)
    og_ref[0] = dot_tn(mixed_ref[...], cot).astype(BF16)
    og_ref[1] = dot_tn(mixed_ref[...], coto).astype(BF16)
    ig_ref[0] = dot_tn(hid_ref[0], gate_grad).astype(BF16)
    ig_ref[1] = dot_tn(hid_ref[1], gate_grad).astype(BF16)


def backward_scan_kernel(
    table_ref, flows_ref, parents_ref, me_ref, length_ref, dl_ref, starts_ref, back_ref, cum_ref,
    delta_ref, act_ref, sel_ref, pgrad_ref, pre_ref, tw_ref,
    selg_ref, agrad_ref, small_ref, stepg_ref, dgrad_ref,
    grads, drive, b_ref, c_ref, rate_ref, decay_buf, state_buf, b_sum, c_sum, dg_ref,
):
    rows, width = act_ref.shape
    steps = rows // spans
    states = dl_ref.shape[0]
    rank = tw_ref.shape[0]
    count = table_ref.shape[0]
    me = me_ref[0]
    rate = -jnp.exp(dl_ref[...]) * log2e
    decay_rows(dl_ref, rate_ref, log2e)
    grads[...] = jnp.zeros(grads.shape, F32)

    def visit(visited, carry):
        target = count - 1 - visited
        _, total = segment_sum(table_ref, target, states)
        flow = flows_ref[target].astype(F32) + jnp.exp2(rate * total) * grads[target]
        above = parents_ref[target]
        slot = jnp.maximum(above, 0)
        grads[slot] = grads[slot] + flow * (above >= 0).astype(F32)
        return carry

    lax.fori_loop(0, count - 1, visit, 0)
    end_grad = grads[me]
    sel = sel_ref[...]
    drive[...] = delta_ref[...] * act_ref[...].astype(F32)
    b_ref[...] = spread(sel[:, rank : rank + states], states)
    c_ref[...] = spread(sel[:, rank + states :], states)
    index2 = span_index((spans, width))
    cum = cum_ref[...]
    after = cum[spans - 1 : spans, :] - cum
    inside = index2 < spans - 1

    for group in range(width // lanes):
        here = slice(group * lanes, (group + 1) * lanes)

        def advance(step, carry):
            d = delta_ref[step_ds(step), here]
            w = drive[step_ds(step), here]
            out = []
            for n in range(states):
                state_buf[n, step_ds(step), :] = carry[n]
                a = jnp.exp2(d * rate_ref[n, :, here])
                decay_buf[n, step_ds(step), :] = a
                out.append(a * carry[n] + w * b_ref[step_ds(step), n * lanes : (n + 1) * lanes])
            return tuple(out)

        finals = lax.fori_loop(0, steps, advance, tuple(starts_ref[n, :, here] for n in range(states)))
        for n in range(states):
            state_buf[n, rows : rows + spans, :] = finals[n]

        later = []
        for n in range(states):
            flow = jnp.where(inside[:, here], shift_spans(back_ref[n, :, here], -1), 0.0)
            later.append(flow + jnp.exp2(after[:, here] * rate_ref[n, :, here]) * end_grad[n : n + 1, here])

        def retreat(back, carry):
            step = steps - 1 - back
            at = step_ds(step)
            d = delta_ref[at, here]
            p = pgrad_ref[at, here]
            w = drive[at, here]
            flows, sums = carry
            new_flows, new_sums = [], []
            weighted = [None, None]
            decayed = [None, None]
            for n in range(states):
                cols = slice(n * lanes, (n + 1) * lanes)
                a = decay_buf[n, at, :]
                adjoint = c_ref[at, cols] * p + flows[n]
                moved = a * adjoint
                growth = moved * state_buf[n, at, :]
                new_flows.append(moved)
                new_sums.append(sums[n] + growth * d)
                term = adjoint * b_ref[at, cols]
                weighted[n % 2] = term if weighted[n % 2] is None else weighted[n % 2] + term
                term = growth * rate_ref[n, :, here]
                decayed[n % 2] = term if decayed[n % 2] is None else decayed[n % 2] + term
                b_term = adjoint * w
                c_term = state_buf[n, step_ds(step + 1), :] * p
                if group == 0:
                    b_sum[at, cols] = b_term
                    c_sum[at, cols] = c_term
                else:
                    b_sum[at, cols] += b_term
                    c_sum[at, cols] += c_term
            bw = weighted[0] + weighted[1]
            dg_ref[at, here] = (decayed[0] + decayed[1]) * (1.0 / log2e) + act_ref[at, here].astype(F32) * bw
            agrad_ref[at, here] = bw * d
            return (tuple(new_flows), tuple(new_sums))

        zero = jnp.zeros((spans, lanes), F32)
        _, sums = lax.fori_loop(0, steps, retreat, (tuple(later), (zero,) * states))
        for n in range(states):
            dgrad_ref[n : n + 1, here] = (
                jnp.sum(sums[n], axis=0, keepdims=True) * rate[n : n + 1, here] * (1.0 / log2e)
            )

    live = (step_tokens(rows, steps) < length_ref[0]).astype(F32)
    step_pre_grad = dg_ref[...] * live * sigmoid(pre_ref[...])
    small_ref[...] = jnp.broadcast_to(jnp.sum(step_pre_grad, axis=0, keepdims=True), small_ref.shape)
    low = step_pre_grad.astype(BF16)
    stepg_ref[...] = dot_tn(sel[:, :rank].astype(BF16), low)
    gather = gather_matrix(states)
    selg_ref[...] = jnp.concatenate(
        [dot_nt(low, tw_ref[...]), dot(b_sum[...].astype(BF16), gather), dot(c_sum[...].astype(BF16), gather)],
        axis=1,
    )


def backward_out_kernel(
    selg_ref, act_ref, sw_ref, agrad_ref, skip_ref, pgrad_ref, ext_ref, cw_ref, cb_ref,
    hid_ref, hidt_ref, wi_ref, wio_ref, wg_ref, wgo_ref, ggrad_ref,
    ig_ref, part_ref, tpart_ref, selw_ref, cgrad_ref,
    cig_ref,
):
    rows, width = act_ref.shape
    steps = rows // spans
    selg = selg_ref[...].astype(BF16)
    selw_ref[...] = dot_tn(selg, act_ref[...])
    active_grad = (
        agrad_ref[...] + skip_ref[0:1, :].astype(F32) * pgrad_ref[...] + dot_nt(selg, sw_ref[...])
    )
    pre = conv_pre(ext_ref, cw_ref, cb_ref, rows, width)
    conv_in = active_grad * slope_of(pre, sigmoid(pre))
    cig_ref[0:rows, :] = conv_in
    last_span = lax.broadcasted_iota(jnp.int32, (spans, width), 0) == spans - 1
    for j in range(3):
        block = jnp.roll(conv_in[j * spans : (j + 1) * spans], -1, axis=0)
        cig_ref[rows + j * spans : rows + (j + 1) * spans, :] = jnp.where(last_span, 0.0, block)
    taps = cw_ref[...].astype(F32)
    sums = [
        jnp.sum(conv_in * ext_ref[k * spans : k * spans + rows, :], axis=0, keepdims=True)
        for k in range(4)
    ]
    sums.append(jnp.sum(conv_in, axis=0, keepdims=True))
    sums.append(jnp.zeros((3, width), F32))
    cgrad_ref[...] = jnp.concatenate(sums, axis=0)
    inner_grad = jnp.zeros((rows, width), F32)
    for k in range(4):
        inner_grad = inner_grad + taps[k : k + 1, :] * cig_ref[(3 - k) * spans : (3 - k) * spans + rows, :]
    inner_low = inner_grad.astype(BF16)
    tails = [jnp.zeros((5, width), F32)]
    for i in range(3):
        row = jnp.zeros((1, width), F32)
        for k in range(i + 1):
            row = row + taps[k : k + 1, :] * conv_in[(i - k) * spans : (i - k) * spans + 1, :]
        tails.append(row)
    tail_low = jnp.concatenate(tails, axis=0).astype(BF16)
    order = to_tokens(rows, steps)
    natural = dot(order, inner_low).astype(BF16)
    naturalg = dot(order, ggrad_ref[...]).astype(BF16)
    for h, (wi, wg) in enumerate(((wi_ref, wg_ref), (wio_ref, wgo_ref))):
        part_ref[h] = (dot_nt(natural, wi[...]) + dot_nt(naturalg, wg[...])).astype(BF16)
        tpart_ref[h] = dot_nt(tail_low, wi[...])
        ig_ref[h] = (dot_tn(hid_ref[h], inner_low) + dot_tn(hidt_ref[h], tail_low)).astype(BF16)


def seq_bits(count):
    bits = []
    mask = 1
    while mask < count:
        bits.append(mask)
        mask *= 2
    return bits


def sum_scatter(value, count):
    me = lax.axis_index("seq")
    for mask in seq_bits(count):
        half = value.shape[0] // 2
        mine = (me // mask) % 2
        keep = lax.dynamic_slice_in_dim(value, mine * half, half, 0)
        give = lax.dynamic_slice_in_dim(value, (1 - mine) * half, half, 0)
        got = lax.ppermute(give, "seq", [(i, i ^ mask) for i in range(count)])
        value = (keep.astype(F32) + got.astype(F32)).astype(value.dtype)
    return value


def gather_back(value, count):
    me = lax.axis_index("seq")
    for mask in reversed(seq_bits(count)):
        mine = (me // mask) % 2
        got = lax.ppermute(value, "seq", [(i, i ^ mask) for i in range(count)])
        low = jnp.where(mine == 0, value, got)
        high = jnp.where(mine == 0, got, value)
        value = jnp.concatenate([low, high], axis=0)
    return value


def on_device(
    tokens_in, teacher, norm_gain, in_weight, conv_weight, conv_bias, select_weight, step_weight,
    step_bias, decay_log, skip_gain, out_weight, parents, lengths, valid_rows,
):
    rows, width = tokens_in.shape
    half = norm_gain.shape[0]
    inner = decay_log.shape[1]
    states = decay_log.shape[0]
    rank = step_weight.shape[0]
    selects = rank + 2 * states
    steps = rows // spans
    count = lax.axis_size("seq")
    row_len = rows // lax.axis_size("row")
    row = lax.axis_index("row")
    col = lax.axis_index("col")
    me = lax.axis_index("seq")
    my_len = lengths[me][None]
    my_parent = parents[me][None]
    my_valid = valid_rows[me][None]
    me1 = me.astype(jnp.int32)[None]
    scale = jnp.full((8, lanes), 1.0, F32) * (rows * count / jnp.sum(valid_rows).astype(F32))

    def halves(value, axis):
        size = value.shape[axis] // 2
        own = lax.dynamic_slice_in_dim(value, col * size, size, axis)
        other = lax.dynamic_slice_in_dim(value, (1 - col) * size, size, axis)
        return own, other

    def rows8(value):
        return jnp.broadcast_to(value[None, :], (8, value.shape[0]))

    swap = [(0, 1), (1, 0)]
    tok, toko = halves(tokens_in, 1)
    tail = lax.dynamic_slice_in_dim(tokens_in, my_len[0] - 8, 8, 0)
    w_own, w_send = halves(in_weight, 2)
    wi, wg = w_own[:, 0], w_own[:, 1]
    wi_send, wg_send = w_send[:, 0], w_send[:, 1]
    ow, ow_send = halves(out_weight, 0)
    gain = rows8(norm_gain)
    skip = rows8(skip_gain)
    conv_b = rows8(conv_bias)
    step_b = rows8(step_bias)

    tails, wio, gaino = entry_exchange(tail, wi_send, gain, count)
    wg_send, ow_send, wio = lax.optimization_barrier((wg_send, ow_send, wio))
    wgo = lax.ppermute(wg_send, "col", swap)
    owo = lax.ppermute(ow_send, "col", swap)
    tails_own, tails_oth = halves(tails, 2)

    hid, hid_tail, ext, act, sel_part = run_kernel(
        forward_in_kernel,
        (
            struct((2, rows, half), BF16),
            struct((2, 8, half), BF16),
            struct((rows + 3 * spans, inner), F32),
            struct((rows, inner), BF16),
            struct((rows, selects), F32),
        ),
        (tok, toko, tails_own, tails_oth, gain, gaino, wi, wio, conv_weight, conv_b, select_weight, my_parent),
        "forward_in",
        flops=2e9,
    )
    sel = quad_sum(sel_part, 1, "select_sum")
    delta, step_pre, reach, cum, seg_map = run_kernel(
        forward_ends_kernel,
        (
            struct((rows, inner), F32),
            struct((rows, inner), F32),
            struct((states, spans, inner), F32),
            struct((spans, inner), F32),
            struct((states + 8, inner), BF16),
        ),
        (sel, step_weight, step_b, decay_log, act, my_len),
        "forward_ends",
        scratch=[
            pltpu.VMEM((rows, inner), F32),
            pltpu.VMEM((rows, states * lanes), F32),
            pltpu.VMEM((states, spans, inner), F32),
        ],
        flops=2e9,
    )
    table = seq_gather(seg_map, count, 2, "state_gather")
    starts, mixed_pre, gate, mixed, part = run_kernel(
        forward_out_kernel,
        (
            struct((states, spans, inner), F32),
            struct((rows, inner), F32),
            struct((rows, inner), F32),
            struct((rows, inner), BF16),
            struct((2, rows, half), BF16),
        ),
        (
            table, parents, me1, decay_log, reach, cum, delta, act, sel, hid, wg, wgo, skip, ow, owo,
        ),
        "forward_out",
        scratch=[
            pltpu.VMEM((count, states, inner), F32),
            pltpu.VMEM((rows, inner), F32),
            pltpu.VMEM((rows, states * lanes), F32),
            pltpu.VMEM((rows, states * lanes), F32),
            pltpu.VMEM((states, spans, inner), F32),
        ],
        flops=4e9,
    )
    tok_tile = lax.dynamic_slice_in_dim(tok, row * row_len, row_len, 0)
    toko_tile = lax.dynamic_slice_in_dim(toko, row * row_len, row_len, 0)
    teach_tile = lax.dynamic_slice_in_dim(teacher, row * row_len, row_len, 0)
    output, cot_tile, cot = middle_exchange(part, tok_tile, teach_tile, my_valid, scale)
    out_part, gate_grad, ig_gate, pre_grad, skip_part, back, flow = run_kernel(
        backward_in_kernel,
        (
            struct((2, inner, half), BF16),
            struct((rows, inner), BF16),
            struct((2, half, inner), BF16),
            struct((rows, inner), F32),
            struct((8, inner), F32),
            struct((states, spans, inner), F32),
            struct((states, inner), BF16),
        ),
        (cot, mixed, ow, owo, gate, mixed_pre, act, skip, sel, delta, decay_log, cum, hid),
        "backward_in",
        scratch=[
            pltpu.VMEM((rows, states * lanes), F32),
            pltpu.VMEM((states, spans, inner), F32),
        ],
        flops=4e9,
    )
    flows = seq_gather(flow, count, 4, "flow_gather")
    selg_part, active_grad, step_bias_part, step_part, decay_part = run_kernel(
        backward_scan_kernel,
        (
            struct((rows, selects), F32),
            struct((rows, inner), F32),
            struct((8, inner), F32),
            struct((rank, inner), F32),
            struct((states, inner), F32),
        ),
        (
            table, flows, parents, me1, my_len, decay_log, starts, back, cum, delta, act, sel,
            pre_grad, step_pre, step_weight,
        ),
        "backward_scan",
        scratch=[
            pltpu.VMEM((count, states, inner), F32),
            pltpu.VMEM((rows, inner), F32),
            pltpu.VMEM((rows, states * lanes), F32),
            pltpu.VMEM((rows, states * lanes), F32),
            pltpu.VMEM((states, spans, inner), F32),
            pltpu.VMEM((states, rows, lanes), F32),
            pltpu.VMEM((states, rows + spans, lanes), F32),
            pltpu.VMEM((rows, states * lanes), F32),
            pltpu.VMEM((rows, states * lanes), F32),
            pltpu.VMEM((rows, inner), F32),
        ],
        flops=8e9,
    )
    selg = quad_sum(selg_part, 7, "select_grad_sum")
    ig_inner, hid_part, tail_part, select_part, conv_part = run_kernel(
        backward_out_kernel,
        (
            struct((2, half, inner), BF16),
            struct((2, rows, half), BF16),
            struct((2, 8, half), F32),
            struct((selects, inner), F32),
            struct((8, inner), F32),
        ),
        (
            selg, act, select_weight, active_grad, skip, pre_grad, ext, conv_weight, conv_b,
            hid, hid_tail, wi, wio, wg, wgo, gate_grad,
        ),
        "backward_out",
        scratch=[pltpu.VMEM((rows + 3 * spans, inner), F32)],
        flops=6e9,
    )
    hid_tile, tail_tile = hidden_exchange(hid_part, tail_part)
    tail_table = seq_gather(
        jnp.concatenate([tail_tile[5:8], tail_tile[:5]], axis=0), count, 8, "tail_gather"
    )
    tokens_grad, gain_part = finish_exchange(
        hid_tile, tail_table, tok_tile, toko_tile, gain, cot_tile, parents, lengths, width
    )

    def flat(pair):
        return pair.reshape(-1, pair.shape[-1])

    small = jnp.concatenate(
        [
            step_part, decay_part, select_part, conv_part[:5], skip_part[:1], step_bias_part[:1],
            gain_part[:1],
        ],
        axis=0,
    )
    pad = -small.shape[0] % (8 * count)
    small = jnp.pad(small, ((0, pad), (0, 0)))
    first = jnp.concatenate([flat(out_part), flat(ig_gate)], axis=0)
    first = gather_back(sum_scatter(first, count), count)
    second = gather_back(sum_scatter(flat(ig_inner), count), count)
    small = gather_back(sum_scatter(small, count), count)
    og = first[: 2 * inner].reshape(2, inner, half)
    igg = first[2 * inner :].reshape(2, half, inner)
    igi = second.reshape(2, half, inner)
    from_pair = lax.ppermute(jnp.stack([og[1], igg[1], igi[1]]), "col", swap)
    left = col == 0

    def beside(own, other, axis):
        return jnp.concatenate(
            [jnp.where(left, own, other), jnp.where(left, other, own)], axis=axis
        ).astype(F32)

    out_grad = beside(og[0], from_pair[0], 0)
    in_grad = jnp.stack([beside(igi[0], from_pair[2], 1), beside(igg[0], from_pair[1], 1)], axis=1)
    at = 0
    pieces = []
    for size in (rank, states, selects, 4, 1, 1, 1, 1):
        pieces.append(small[at : at + size])
        at += size
    step_grad, decay_grad, select_grad, conv_grad, conv_bias_grad, skip_grad, step_bias_grad, gain_grad = pieces
    return (
        output,
        tokens_grad,
        gain_grad[0],
        in_grad,
        conv_grad,
        conv_bias_grad[0],
        select_grad.T,
        step_grad,
        step_bias_grad[0],
        decay_grad,
        skip_grad[0],
        out_grad,
    )


def solution(mesh):
    placed = (
        P("seq", None),
        P("seq", "col"),
        P("col"),
        P("col", None, "row"),
        P(None, ("row", "col")),
        P(("row", "col")),
        P(("row", "col"), None),
        P(None, ("row", "col")),
        P(("row", "col")),
        P(None, ("row", "col")),
        P(("row", "col")),
        P("row", "col"),
        P(),
        P(),
        P(),
    )
    return jax.shard_map(
        on_device,
        mesh=mesh,
        in_specs=placed,
        out_specs=(
            P(("seq", "row"), "col"),
            P(("seq", "row"), "col"),
            P("col"),
            P("col", None, "row"),
            P(None, ("row", "col")),
            P(("row", "col")),
            P(("row", "col"), None),
            P(None, ("row", "col")),
            P(("row", "col")),
            P(None, ("row", "col")),
            P(("row", "col")),
            P("row", "col"),
        ),
        check_vma=False,
    )
```

profile of v0, /device:TPU:0, one launch (start us, length us, event | category | flops | bytes accessed | tf_op | source)
XLA Modules:
  0.0 381.1 jit_solution(13985788628403491562)
XLA Ops:
  4.6 2.9 constant_dynamic-slice_fusion.10
  7.5 5.1 %constant_dynamic-slice_fusion.12 = (bf16[512,1,512]{2,1,0:T(2,128)(2,1)S(1)}, bf16[512,1,512]{2,1,0:T(2,128)(2,1)S(1)}, bf16[512,1,512]{2,1,0:T(2,128)(2,1)S(1)}, bf16[512,1,512]{2,1,0:T(2,128)(2,1)S(1)}) fusion(bf16[512,2,1024]{2,1,0:T(2,128)(2,1)S(1)} %copy-done.2, s32[]{:T(128)S(6)} %add.183, s32[]{:T(128)S(6)} %select_n.283, s32[]{:T(128)S(6)} %select_n.284), kind=kLoop, calls=%fused_computation.74 | loop fusion | bytes 4194316 | tf_op jit(solution)/shard_map/slice | solution.py:921
  14.5 21.4 %entry_exchange.1 = (bf16[8,8,1024]{2,1,0:T(8,128)(2,1)}, bf16[512,512]{1,0:T(8,128)(2,1)}, bf16[8,512]{1,0:T(8,128)(2,1)}) custom-call(bf16[8,1024]{1,0:T(8,128)(2,1)} %constant_dynamic-slice_fusion.16.tail_ref, bf16[512,512]{1,0:T(8,128)(2,1)} %get-tuple-element.161.wi_ref, bf16[8,512]{1,0:T(8,128)(2,1)} %broadcast_in_dim.10.gain_ref), custom_call_target="tpu_custom_call" | custom-call | bytes 548864 | tf_op jit(solution)/shard_map/entry_exchange/pallas_call | solution.py:99
  42.8 5.6 %forward_in.1 = (bf16[2,512,512]{2,1,0:T(8,128)(2,1)}, bf16[2,8,512]{2,1,0:T(8,128)(2,1)}, f32[536,512]{1,0:T(8,128)}, bf16[512,512]{1,0:T(8,128)(2,1)}, f32[512,96]{1,0:T(8,128)}) custom-call(bf16[512,512]{1,0:T(8,128)(2,1)} %get-tuple-element.156.tok_ref, bf16[512,512]{1,0:T(8,128)(2,1)} %get-tuple-element.157.toko_ref, ...), custom_call_target="tpu_custom_call" | custom-call | flops 2000000000 | bytes 2355204 | tf_op jit(solution)/shard_map/forward_in/pallas_call | solution.py:99
  49.6 14.3 %select_sum.1.sel_ref = f32[512,96]{1,0:T(8,128)} custom-call(f32[512,96]{1,0:T(8,128)} %get-tuple-element.61.x_ref), custom_call_target="tpu_custom_call" | custom-call | bytes 196608 | tf_op jit(solution)/shard_map/select_sum/pallas_call | solution.py:99
  64.5 9.9 %forward_ends.1 = (f32[512,512]{1,0:T(8,128)}, f32[512,512]{1,0:T(8,128)}, f32[16,8,512]{2,1,0:T(8,128)}, f32[8,512]{1,0:T(8,128)}, bf16[24,512]{1,0:T(8,128)(2,1)}) custom-call(f32[512,96]{1,0:T(8,128)} %select_sum.1.sel_ref, bf16[64,512]{1,0:T(8,128)(2,1)} %tw_ref.3, bf16[8,512]{1,0:T(8,128)(2,1)} %broadcast_in_dim.12.tb_ref, f32[16,512]{1,0:T(8,128)} %dl_ref.7, ...), custom_call_target="tpu_custom_call" | custom-call | flops 2000000000 | bytes 827396 | tf_op jit(solution)/shard_map/forward_ends/pallas_call | solution.py:99
  74.3 8.2 %state_gather.1.table_ref = bf16[8,24,512]{2,1,0:T(8,128)(2,1)} custom-call(bf16[24,512]{1,0:T(8,128)(2,1)} %get-tuple-element.63.x_ref), custom_call_target="tpu_custom_call" | custom-call | bytes 24576 | tf_op jit(solution)/shard_map/state_gather/pallas_call | solution.py:99
  85.7 13.5 %forward_out.1 = (f32[16,8,512]{2,1,0:T(8,128)}, f32[512,512]{1,0:T(8,128)}, f32[512,512]{1,0:T(8,128)}, bf16[512,512]{1,0:T(8,128)(2,1)}, bf16[2,512,512]{2,1,0:T(8,128)(2,1)}) custom-call(bf16[8,24,512]{2,1,0:T(8,128)(2,1)} %state_gather.1.table_ref, s32[8]{0:T(128)} %parents_ref.5, s32[1]{0:T(128)} %bitcast.5.me_ref, f32[16,512]{1,0:T(8,128)} %dl_ref.7, ...), custom_call_target="tpu_custom_call" | custom-call | flops 4000000000 | bytes 5431332 | tf_op jit(solution)/shard_map/forward_out/pallas_call | solution.py:99
  99.8 21.6 %middle_exchange.1 = (bf16[256,512]{1,0:T(8,128)(2,1)}, f32[256,512]{1,0:T(8,128)}, bf16[2,512,512]{2,1,0:T(8,128)(2,1)}) custom-call(bf16[2,512,512]{2,1,0:T(8,128)(2,1)} %get-tuple-element.70.part_ref, bf16[256,512]{1,0:T(8,128)(2,1)} %get-tuple-element.133.tok_ref, bf16[256,512]{1,0:T(8,128)(2,1)} %constant_dynamic-slice_fusion.9.teach_ref, ...), custom_call_target="tpu_custom_call" | custom-call | bytes 1576964 | tf_op jit(solution)/shard_map/middle_exchange/pallas_call | solution.py:99
  121.4 13.0 %backward_in.1 = (bf16[2,512,512]{2,1,0:T(8,128)(2,1)}, bf16[512,512]{1,0:T(8,128)(2,1)}, bf16[2,512,512]{2,1,0:T(8,128)(2,1)}, f32[512,512]{1,0:T(8,128)}, f32[...) custom-call(bf16[2,512,512]{2,1,0:T(8,128)(2,1)} %get-tuple-element.72.cot_ref, ...), custom_call_target="tpu_custom_call" | custom-call | flops 4000000000 | bytes 7593984 | tf_op jit(solution)/shard_map/backward_in/pallas_call | solution.py:99
  137.3 26.8 %flow_gather.1.flows_ref = bf16[8,16,512]{2,1,0:T(8,128)(2,1)} custom-call(bf16[16,512]{1,0:T(8,128)(2,1)} %get-tuple-element.76.x_ref), custom_call_target="tpu_custom_call" | custom-call | bytes 16384 | tf_op jit(solution)/shard_map/flow_gather/pallas_call | solution.py:99
  164.1 24.5 %backward_scan.1 = (f32[512,96]{1,0:T(8,128)}, f32[512,512]{1,0:T(8,128)}, f32[8,512]{1,0:T(8,128)}, f32[64,512]{1,0:T(8,128)}, f32[16,512]{1,0:T(8,128)}) custom-call(bf16[8,24,512]{2,1,0:T(8,128)(2,1)} %state_gather.1.table_ref, bf16[8,16,512]{2,1,0:T(8,128)(2,1)} %flow_gather.1.flows_ref, s32[8]{0:T(128)} %parents_ref.5, s32[1]{0:T(128)} %bitcast.5.me_ref, ...), custom_call_target="tpu_custom_call" | custom-call | flops 8000000000 | bytes 4833320 | tf_op jit(solution)/shard_map/backward_scan/pallas_call | solution.py:99
  188.6 9.0 %select_grad_sum.1.selg_ref = f32[512,96]{1,0:T(8,128)} custom-call(f32[512,96]{1,0:T(8,128)} %get-tuple-element.81.x_ref), custom_call_target="tpu_custom_call" | custom-call | bytes 196608 | tf_op jit(solution)/shard_map/select_grad_sum/pallas_call | solution.py:99
  197.6 8.6 %backward_out.1 = (bf16[2,512,512]{2,1,0:T(8,128)(2,1)}, bf16[2,512,512]{2,1,0:T(8,128)(2,1)}, f32[2,8,512]{2,1,0:T(8,128)}, f32[96,512]{1,0:T(8,128)}, f32[8,512]{1,0:T(8,128)}) custom-call(f32[512,96]{1,0:T(8,128)} %select_grad_sum.1.selg_ref, bf16[512,512]{1,0:T(8,128)(2,1)} %get-tuple-element.62.act_ref, bf16[512,96]{1,0:T(8,128)(2,1)} %copy.29.sw_ref, ...), custom_call_target="tpu_custom_call" | custom-call | flops 6000000000 | bytes 7720960 | tf_op jit(solution)/shard_map/backward_out/pallas_call | solution.py:99
  208.9 3.0 add_convert_fusion
  213.2 12.4 %hidden_exchange.1 = (f32[256,512]{1,0:T(8,128)}, f32[8,512]{1,0:T(8,128)}) custom-call(bf16[2,512,512]{2,1,0:T(8,128)(2,1)} %get-tuple-element.86.part_ref, f32[2,8,512]{2,1,0:T(8,128)} %get-tuple-element.87.tail_ref), custom_call_target="tpu_custom_call" | custom-call | bytes 1081344 | tf_op jit(solution)/shard_map/hidden_exchange/pallas_call | solution.py:99
  227.6 8.0 %tail_gather.1.tails_ref = f32[8,8,512]{2,1,0:T(8,128)} custom-call(f32[8,512]{1,0:T(8,128)} %pad_maximum_fusion.8.x_ref), custom_call_target="tpu_custom_call" | custom-call | bytes 16384 | tf_op jit(solution)/shard_map/tail_gather/pallas_call | solution.py:99
  235.6 7.5 %finish_exchange.1 = (f32[256,512]{1,0:T(8,128)}, f32[8,512]{1,0:T(8,128)}) custom-call(f32[256,512]{1,0:T(8,128)} %get-tuple-element.88.hid_ref, f32[8,8,512]{2,1,0:T(8,128)} %tail_gather.1.tails_ref, bf16[256,512]{1,0:T(8,128)(2,1)} %get-tuple-element.133.tok_ref, bf16[256,512]{1,0:T(8,128)(2,1)} %get-tuple-element.132.toko_ref, ...), custom_call_target="tpu_custom_call" | custom-call | bytes 1712192 | tf_op jit(solution)/shard_map/finish_exchange/pallas_call | solution.py:99
  247.1 2.6 concatenate.63
  254.4 8.4 %collective-permute-done.9 = bf16[256,512]{1,0:T(8,128)(2,1)S(1)} collective-permute-done((bf16[256,512]{1,0:T(8,128)(2,1)S(1)}, bf16[256,512]{1,0:T(8,128)(2,1)S(1)}, u32[]{:S(2)}, u32[]{:S(2)}) %collective-permute-start.9) | collective-permute-done | bytes 262176 | tf_op jit(solution)/shard_map/ppermute | solution.py:870
  264.0 8.8 %collective-permute-done.16 = bf16[256,512]{1,0:T(8,128)(2,1)S(1)} collective-permute-done((bf16[256,512]{1,0:T(8,128)(2,1)S(1)}, bf16[256,512]{1,0:T(8,128)(2,1)S(1)}, u32[]{:S(2)}, u32[]{:S(2)}) %collective-permute-start.16) | collective-permute-done | bytes 262176 | tf_op jit(solution)/shard_map/ppermute | solution.py:870
  274.2 5.6 %collective-permute-done.10 = bf16[128,512]{1,0:T(8,128)(2,1)S(1)} collective-permute-done((bf16[128,512]{1,0:T(8,128)(2,1)S(1)}, bf16[128,512]{1,0:T(8,128)(2,1)S(1)}, u32[]{:S(2)}, u32[]{:S(2)}) %collective-permute-start.10) | collective-permute-done | bytes 131104 | tf_op jit(solution)/shard_map/ppermute | solution.py:870
  279.9 6.9 %collective-permute-done.17 = bf16[256,512]{1,0:T(8,128)(2,1)S(1)} collective-permute-done((bf16[256,512]{1,0:T(8,128)(2,1)S(1)}, bf16[256,512]{1,0:T(8,128)(2,1)S(1)}, u32[]{:S(2)}, u32[]{:S(2)}) %collective-permute-start.17) | collective-permute-done | bytes 262176 | tf_op jit(solution)/shard_map/ppermute | solution.py:879
  287.1 2.1 collective-permute-start.3
  289.3 12.5 %collective-permute-done.18 = bf16[512,512]{1,0:T(8,128)(2,1)S(1)} collective-permute-done((bf16[512,512]{1,0:T(8,128)(2,1)S(1)}, bf16[512,512]{1,0:T(8,128)(2,1)S(1)}, u32[]{:S(2)}, u32[]{:S(2)}) %collective-permute-start.18) | collective-permute-done | bytes 524320 | tf_op jit(solution)/shard_map/ppermute | solution.py:879
  303.7 3.7 collective-permute-done.12
  309.9 5.3 %collective-permute-done.4 = f32[24,512]{1,0:T(8,128)S(1)} collective-permute-done((f32[24,512]{1,0:T(8,128)S(1)}, f32[24,512]{1,0:T(8,128)S(1)}, u32[]{:S(2)}, u32[]{:S(2)}) %collective-permute-start.4) | collective-permute-done | bytes 49184 | tf_op jit(solution)/shard_map/ppermute | solution.py:870
  315.3 19.1 %collective-permute-done.13 = bf16[512,512]{1,0:T(8,128)(2,1)S(1)} collective-permute-done((bf16[512,512]{1,0:T(8,128)(2,1)}, bf16[512,512]{1,0:T(8,128)(2,1)S(1)}, u32[]{:S(2)}, u32[]{:S(2)}) %collective-permute-start.13) | collective-permute-done | bytes 524320 | tf_op jit(solution)/shard_map/ppermute | solution.py:879
  338.9 4.6 %collective-permute-done.6 = f32[48,512]{1,0:T(8,128)S(1)} collective-permute-done((f32[48,512]{1,0:T(8,128)S(1)}, f32[48,512]{1,0:T(8,128)S(1)}, u32[]{:S(2)}, u32[]{:S(2)}) %collective-permute-start.6) | collective-permute-done | bytes 98336 | tf_op jit(solution)/shard_map/ppermute | solution.py:879
  344.9 4.4 %collective-permute-done.7 = f32[96,512]{1,0:T(8,128)S(1)} collective-permute-done((f32[96,512]{1,0:T(8,128)S(1)}, f32[96,512]{1,0:T(8,128)S(1)}, u32[]{:S(2)}, u32[]{:S(2)}) %collective-permute-start.7) | collective-permute-done | bytes 196640 | tf_op jit(solution)/shard_map/ppermute | solution.py:879
  352.5 17.7 %collective-permute-done.20 = bf16[3,512,512]{2,1,0:T(8,128)(2,1)} collective-permute-done((bf16[3,512,512]{2,1,0:T(8,128)(2,1)}, bf16[3,512,512]{2,1,0:T(8,128)(2,1)}, u32[]{:S(2)}, u32[]{:S(2)}) %collective-permute-start.20) | collective-permute-done | bytes 1572896 | tf_op jit(solution)/shard_map/ppermute | solution.py:1087
  372.7 5.3 %copy.31 = f32[512,2,1024]{2,1,0:T(2,128)} copy(f32[512,2,1024]{2,0,1:T(8,128)S(1)} %maximum_convert_fusion) | data formatting | bytes 8388608
  (136 shorter events, 55.8 us)
Async XLA Ops:
  0.6 82.6 %copy-start = (bf16[512,512]{1,0:T(8,128)(2,1)S(1)}, bf16[512,512]{1,0:T(8,128)(2,1)}, u32[]{:S(2)}) copy-start(bf16[512,512]{1,0:T(8,128)(2,1)} %param.16) | copy-start | bytes 1572868
  12.6 26.9 %copy-start.18 = (s32[8]{0:T(128)S(1)}, s32[8]{0:T(128)}, u32[]{:S(2)}) copy-start(s32[8]{0:T(128)} %parents_ref.5) | copy-start | bytes 100
  12.7 27.5 %copy-start.12 = (bf16[512,96]{0,1:T(8,128)(2,1)S(1)}, bf16[512,96]{0,1:T(8,128)(2,1)}, u32[]{:S(2)}) copy-start(bf16[512,96]{0,1:T(8,128)(2,1)} %param.21) | copy-start | bytes 294916
  14.5 27.7 %copy-start.15 = (bf16[512]{0:T(512)(128)(2,1)S(1)}, bf16[512]{0:T(512)(128)(2,1)}, u32[]{:S(2)}) copy-start(bf16[512]{0:T(512)(128)(2,1)} %param.20) | copy-start | bytes 3076
  36.0 49.2 %collective-permute-start = (bf16[512,512]{1,0:T(8,128)(2,1)}, bf16[512,512]{1,0:T(8,128)(2,1)}, u32[]{:S(2)}, u32[]{:S(2)}) collective-permute-start(bf16[512,512]{1,0:T(8,128)(2,1)} %get-tuple-element.68), channel_id=1, source_target_pairs={{0,1},{1,0},{2,3},{3,2},{4,5},{5,4},{6,7},{7,6},{8,9},{9,8},{10,11... | collective-permute-start | bytes 1572872 | tf_op jit(solution)/shard_map/ppermute | solution.py:931
  36.6 48.6 %collective-permute-start.1 = (bf16[512,512]{1,0:T(8,128)(2,1)S(1)}, bf16[512,512]{1,0:T(8,128)(2,1)}, u32[]{:S(2)}, u32[]{:S(2)}) collective-permute-start(bf16[512,512]{1,0:T(8,128)(2,1)S(1)} %get-tuple-element.69), channel_id=1, source_target_pairs={{0,1},{1,0},{2,3},{3,2},{4,5},{5,4},{6,7},{7,6},{8,9},{9,8},{10,11... | collective-permute-start | bytes 1572872 | tf_op jit(solution)/shard_map/ppermute | solution.py:932
  42.8 21.1 %copy-start.16 = (bf16[512]{0:T(512)(128)(2,1)S(1)}, bf16[512]{0:T(512)(128)(2,1)}, u32[]{:S(2)}) copy-start(bf16[512]{0:T(512)(128)(2,1)} %param.23) | copy-start | bytes 3076
  64.5 19.6 %copy-start.7 = (bf16[512,1024]{1,0:T(8,128)(2,1)S(1)}, bf16[512,1024]{1,0:T(8,128)(2,1)}, u32[]{:S(2)}) copy-start(bf16[512,1024]{1,0:T(8,128)(2,1)} %param.15) | copy-start | bytes 3145732
  64.5 20.7 %copy-start.17 = (bf16[512]{0:T(512)(128)(2,1)S(1)}, bf16[512]{0:T(512)(128)(2,1)}, u32[]{:S(2)}) copy-start(bf16[512]{0:T(512)(128)(2,1)} %param.25) | copy-start | bytes 3076
  136.4 72.5 %collective-permute-start.14 = (bf16[1024,512]{1,0:T(8,128)(2,1)S(1)}, bf16[1024,512]{1,0:T(8,128)(2,1)}, u32[]{:S(2)}, u32[]{:S(2)}) collective-permute-start(bf16[1024,512]{1,0:T(8,128)(2,1)S(1)} %fusion), channel_id=1, source_target_pairs={{0,4},{4,0},{8,12},{12,8},{16,20},{20,16},{24,28},{28,24},{1,5},{5... | collective-permute-start | bytes 3145736 | tf_op jit(solution)/shard_map/ppermute | solution.py:870
  208.0 41.6 %collective-permute-start.8 = (bf16[512,512]{1,0:T(8,128)(2,1)}, bf16[512,512]{1,0:T(8,128)(2,1)}, u32[]{:S(2)}, u32[]{:S(2)}) collective-permute-start(bf16[512,512]{1,0:T(8,128)(2,1)} %constant_dynamic-slice_fusion.6), channel_id=1, source_target_pairs={{0,4},{4,0},{8,12},{12,8},{16,20},{20,16},{24,28},{28,24},{1,5},{5... | collective-permute-start | bytes 1572872 | tf_op jit(solution)/shard_map/ppermute | solution.py:870
  211.9 35.2 %copy-start.13 = (f32[16,512]{1,0:T(8,128)S(1)}, f32[16,512]{1,0:T(8,128)}, u32[]{:S(2)}) copy-start(f32[16,512]{1,0:T(8,128)} %get-tuple-element.93) | copy-start | bytes 98308
  212.0 37.7 %copy-start.9 = (bf16[2,512,512]{2,1,0:T(8,128)(2,1)S(1)}, bf16[2,512,512]{2,1,0:T(8,128)(2,1)}, u32[]{:S(2)}) copy-start(bf16[2,512,512]{2,1,0:T(8,128)(2,1)} %get-tuple-element.99) | copy-start | bytes 3145732
  212.0 40.2 %collective-permute-start.15 = (bf16[512,512]{1,0:T(8,128)(2,1)S(1)}, bf16[512,512]{1,0:T(8,128)(2,1)S(1)}, u32[]{:S(2)}, u32[]{:S(2)}) collective-permute-start(bf16[512,512]{1,0:T(8,128)(2,1)S(1)} %constant_dynamic-slice_fusion.3), channel_id=1, source_target_pairs={{0,8},{4,12},{8,0},{12,4},{16,24},{20,28},{24,16},{28,20},{1,9},{5... | collective-permute-start | bytes 1572872 | tf_op jit(solution)/shard_map/ppermute | solution.py:870
  250.9 11.8 %collective-permute-start.9 = (bf16[256,512]{1,0:T(8,128)(2,1)S(1)}, bf16[256,512]{1,0:T(8,128)(2,1)S(1)}, u32[]{:S(2)}, u32[]{:S(2)}) collective-permute-start(bf16[256,512]{1,0:T(8,128)(2,1)S(1)} %constant_dynamic-slice_fusion.5), channel_id=1, source_target_pairs={{0,8},{4,12},{8,0},{12,4},{16,24},{20,28},{24,16},{28,20},{1,9},{5... | collective-permute-start | bytes 786440 | tf_op jit(solution)/shard_map/ppermute | solution.py:870
  252.4 20.4 %collective-permute-start.16 = (bf16[256,512]{1,0:T(8,128)(2,1)S(1)}, bf16[256,512]{1,0:T(8,128)(2,1)S(1)}, u32[]{:S(2)}, u32[]{:S(2)}) collective-permute-start(bf16[256,512]{1,0:T(8,128)(2,1)S(1)} %constant_dynamic-slice_fusion.2), channel_id=1, source_target_pairs={{0,16},{4,20},{8,24},{12,28},{16,0},{20,4},{24,8},{28,12},{1,17},{... | collective-permute-start | bytes 786440 | tf_op jit(solution)/shard_map/ppermute | solution.py:870
  262.9 17.0 %collective-permute-start.10 = (bf16[128,512]{1,0:T(8,128)(2,1)S(1)}, bf16[128,512]{1,0:T(8,128)(2,1)S(1)}, u32[]{:S(2)}, u32[]{:S(2)}) collective-permute-start(bf16[128,512]{1,0:T(8,128)(2,1)S(1)} %constant_dynamic-slice_fusion.4), channel_id=1, source_target_pairs={{0,16},{4,20},{8,24},{12,28},{16,0},{20,4},{24,8},{28,12},{1,17},{... | collective-permute-start | bytes 393224 | tf_op jit(solution)/shard_map/ppermute | solution.py:870
  272.9 14.0 %collective-permute-start.17 = (bf16[256,512]{1,0:T(8,128)(2,1)S(1)}, bf16[256,512]{1,0:T(8,128)(2,1)S(1)}, u32[]{:S(2)}, u32[]{:S(2)}) collective-permute-start(bf16[256,512]{1,0:T(8,128)(2,1)S(1)} %add_convert_fusion.3), channel_id=1, source_target_pairs={{0,16},{4,20},{8,24},{12,28},{16,0},{20,4},{24,8},{28,12},{1,17},{... | collective-permute-start | bytes 786440 | tf_op jit(solution)/shard_map/ppermute | solution.py:879
  273.0 14.0 %collective-permute-start.2 = (f32[96,512]{1,0:T(8,128)S(1)}, f32[96,512]{1,0:T(8,128)S(1)}, u32[]{:S(2)}, u32[]{:S(2)}) collective-permute-start(f32[96,512]{1,0:T(8,128)S(1)} %pad_dynamic-slice_fusion.4), channel_id=1, source_target_pairs={{0,4},{4,0},{8,12},{12,8},{16,20},{20,16},{24,28},{28,24},{1,5},{5... | collective-permute-start | bytes 589832 | tf_op jit(solution)/shard_map/ppermute | solution.py:870
  279.9 9.3 %collective-permute-start.11 = (bf16[128,512]{1,0:T(8,128)(2,1)S(1)}, bf16[128,512]{1,0:T(8,128)(2,1)S(1)}, u32[]{:S(2)}, u32[]{:S(2)}) collective-permute-start(bf16[128,512]{1,0:T(8,128)(2,1)S(1)} %add_convert_fusion.5), channel_id=1, source_target_pairs={{0,16},{4,20},{8,24},{12,28},{16,0},{20,4},{24,8},{28,12},{1,17},{... | collective-permute-start | bytes 393224 | tf_op jit(solution)/shard_map/ppermute | solution.py:879
  286.9 14.9 %collective-permute-start.18 = (bf16[512,512]{1,0:T(8,128)(2,1)S(1)}, bf16[512,512]{1,0:T(8,128)(2,1)S(1)}, u32[]{:S(2)}, u32[]{:S(2)}) collective-permute-start(bf16[512,512]{1,0:T(8,128)(2,1)S(1)} %pad_maximum_fusion.3), channel_id=1, source_target_pairs={{0,8},{4,12},{8,0},{12,4},{16,24},{20,28},{24,16},{28,20},{1,9},{5... | collective-permute-start | bytes 1572872 | tf_op jit(solution)/shard_map/ppermute | solution.py:879
  287.1 22.6 %collective-permute-start.3 = (f32[48,512]{1,0:T(8,128)S(1)}, f32[48,512]{1,0:T(8,128)S(1)}, u32[]{:S(2)}, u32[]{:S(2)}) collective-permute-start(f32[48,512]{1,0:T(8,128)S(1)} %constant_dynamic-slice_fusion.8), channel_id=1, source_target_pairs={{0,8},{4,12},{8,0},{12,4},{16,24},{20,28},{24,16},{28,20},{1,9},{5... | collective-permute-start | bytes 294920 | tf_op jit(solution)/shard_map/ppermute | solution.py:870
  289.2 18.2 %collective-permute-start.12 = (bf16[256,512]{1,0:T(8,128)(2,1)S(1)}, bf16[256,512]{1,0:T(8,128)(2,1)S(1)}, u32[]{:S(2)}, u32[]{:S(2)}) collective-permute-start(bf16[256,512]{1,0:T(8,128)(2,1)S(1)} %pad_maximum_fusion.4), channel_id=1, source_target_pairs={{0,8},{4,12},{8,0},{12,4},{16,24},{20,28},{24,16},{28,20},{1,9},{5... | collective-permute-start | bytes 786440 | tf_op jit(solution)/shard_map/ppermute | solution.py:879
  302.1 33.1 %collective-permute-start.19 = (bf16[1024,512]{1,0:T(8,128)(2,1)S(1)}, bf16[1024,512]{1,0:T(8,128)(2,1)}, u32[]{:S(2)}, u32[]{:S(2)}) collective-permute-start(bf16[1024,512]{1,0:T(8,128)(2,1)S(1)} %pad_maximum_fusion.1), channel_id=1, source_target_pairs={{0,4},{4,0},{8,12},{12,8},{16,20},{20,16},{24,28},{28,24},{1,5},{5... | collective-permute-start | bytes 3145736 | tf_op jit(solution)/shard_map/ppermute | solution.py:879
  307.6 27.0 %copy-start.5 = (bf16[256,512]{1,0:T(8,128)(2,1)}, bf16[256,512]{1,0:T(8,128)(2,1)S(1)}, u32[]{:S(2)}) copy-start(bf16[256,512]{1,0:T(8,128)(2,1)S(1)} %get-tuple-element.141) | copy-start | bytes 786436
  308.4 26.0 %collective-permute-start.13 = (bf16[512,512]{1,0:T(8,128)(2,1)}, bf16[512,512]{1,0:T(8,128)(2,1)S(1)}, u32[]{:S(2)}, u32[]{:S(2)}) collective-permute-start(bf16[512,512]{1,0:T(8,128)(2,1)} %pad_maximum_fusion.2), channel_id=1, source_target_pairs={{0,4},{4,0},{8,12},{12,8},{16,20},{20,16},{24,28},{28,24},{1,5},{5... | collective-permute-start | bytes 1572872 | tf_op jit(solution)/shard_map/ppermute | solution.py:879
  309.8 5.4 %collective-permute-start.4 = (f32[24,512]{1,0:T(8,128)S(1)}, f32[24,512]{1,0:T(8,128)S(1)}, u32[]{:S(2)}, u32[]{:S(2)}) collective-permute-start(f32[24,512]{1,0:T(8,128)S(1)} %constant_dynamic-slice_fusion.7), channel_id=1, source_target_pairs={{0,16},{4,20},{8,24},{12,28},{16,0},{20,4},{24,8},{28,12},{1,17},{... | collective-permute-start | bytes 147464 | tf_op jit(solution)/shard_map/ppermute | solution.py:870
  315.2 23.5 %collective-permute-start.5 = (f32[24,512]{1,0:T(8,128)S(1)}, f32[24,512]{1,0:T(8,128)S(1)}, u32[]{:S(2)}, u32[]{:S(2)}) collective-permute-start(f32[24,512]{1,0:T(8,128)S(1)} %dynamic-slice_add_fusion.1), channel_id=1, source_target_pairs={{0,16},{4,20},{8,24},{12,28},{16,0},{20,4},{24,8},{28,12},{1,17},{... | collective-permute-start | bytes 147464 | tf_op jit(solution)/shard_map/ppermute | solution.py:879
  338.5 31.7 %copy-start.6 = (bf16[256,512]{1,0:T(8,128)(2,1)S(1)}, bf16[256,512]{1,0:T(8,128)(2,1)}, u32[]{:S(2)}) copy-start(bf16[256,512]{1,0:T(8,128)(2,1)} %copy-done.5) | copy-start | bytes 786436
  338.5 31.7 %collective-permute-start.20 = (bf16[3,512,512]{2,1,0:T(8,128)(2,1)}, bf16[3,512,512]{2,1,0:T(8,128)(2,1)}, u32[]{:S(2)}, u32[]{:S(2)}) collective-permute-start(bf16[3,512,512]{2,1,0:T(8,128)(2,1)} %pad_maximum_fusion), channel_id=1, source_target_pairs={{0,1},{1,0},{2,3},{3,2},{4,5},{5,4},{6,7},{7,6},{8,9},{9,8},{10,11... | collective-permute-start | bytes 4718600 | tf_op jit(solution)/shard_map/ppermute | solution.py:1087
  338.8 4.7 %collective-permute-start.6 = (f32[48,512]{1,0:T(8,128)S(1)}, f32[48,512]{1,0:T(8,128)S(1)}, u32[]{:S(2)}, u32[]{:S(2)}) collective-permute-start(f32[48,512]{1,0:T(8,128)S(1)} %pad_maximum_fusion.7), channel_id=1, source_target_pairs={{0,8},{4,12},{8,0},{12,4},{16,24},{20,28},{24,16},{28,20},{1,9},{5... | collective-permute-start | bytes 294920 | tf_op jit(solution)/shard_map/ppermute | solution.py:879
  343.5 5.7 %collective-permute-start.7 = (f32[96,512]{1,0:T(8,128)S(1)}, f32[96,512]{1,0:T(8,128)S(1)}, u32[]{:S(2)}, u32[]{:S(2)}) collective-permute-start(f32[96,512]{1,0:T(8,128)S(1)} %pad_maximum_fusion.6), channel_id=1, source_target_pairs={{0,4},{4,0},{8,12},{12,8},{16,20},{20,16},{24,28},{28,24},{1,5},{5... | collective-permute-start | bytes 589832 | tf_op jit(solution)/shard_map/ppermute | solution.py:879
  (9 other events, 40.1 us)
where the time goes:
time: 382 us; the launch traced here: 381 us
  Pallas kernels  204 us (53%)
  waiting for transfers between devices  97 us (25%)
  local copies, waits for them, and re-layouts  40.7 us (11%)
  other arithmetic  18.1 us (5%)
  starting transfers between devices  17.9 us (5%)
    pallas_call x15, Pallas kernels, run_kernel(): pl.pallas_call(kernel, out_shape=outs, in_specs=[smem_spec() if a.dtype =...  204 us
    ppermute x9, waiting for transfers between devices, gather_back(): got = lax.ppermute(value, 'seq', [(i, i ^ mask) for i in range(count)])  51.2 us
    ppermute x9, waiting for transfers between devices, sum_scatter(): got = lax.ppermute(give, 'seq', [(i, i ^ mask) for i in range(count)])  28.1 us
    ppermute x1, waiting for transfers between devices, on_device(): from_pair = lax.ppermute(jnp.stack([og[1], igg[1], igi[1]]), 'col', swap)  17.7 us
    ppermute x9, starting transfers between devices, sum_scatter(): got = lax.ppermute(give, 'seq', [(i, i ^ mask) for i in range(count)])  10.7 us
    unnamed x44, local copies, waits for them, and re-layouts  8.25 us
  transfers between devices with their start and end apart: 21, of which 11 were waited for; matrix products, arithmetic and copies ran while one was open for 8% of the time, Pallas kernels for 35%

commit v1 on v0

--- a/solution.py
+++ b/solution.py
@@ -860,27 +860,183 @@
     return bits
 
 
-def sum_scatter(value, count):
+def mask_order(count, swapped):
+    bits = seq_bits(count)
+    if swapped and len(bits) > 1:
+        bits = [bits[1], bits[0]] + bits[2:]
+    return bits
+
+
+def widen(values):
+    return values.astype(F32)
+
+
+class Chunk:
+    def __init__(self, source, total, stages, send, recv, masks, crossed, emit):
+        self.source, self.total, self.stages = source, total, stages
+        self.send, self.recv, self.masks, self.crossed, self.emit = send, recv, masks, crossed, emit
+        self.count = source.shape[0]
+        self.me = lax.axis_index("seq")
+        self.copies = []
+        self.levels = len(masks)
+
+    def bit(self, level):
+        return (self.me // self.masks[level]) % 2
+
+    def peer(self, level):
+        mask = self.masks[level]
+        return {"seq": self.me + mask - 2 * mask * self.bit(level)}
+
+    def start(self, src, dst, peer):
+        at = len(self.copies)
+        copy = remote(src, dst, self.send.at[at], self.recv.at[at], peer)
+        copy.start()
+        self.copies.append(copy)
+
+    def place(self, level):
+        start = 0
+        for j in range(level + 1):
+            start = start + self.bit(j) * (self.count >> (j + 1))
+        return start
+
+    def held(self, level):
+        return self.source if level == 0 else self.stages[level - 1]
+
+    def halve(self, level):
+        size = self.count >> (level + 1)
+        away = self.held(level).at[pl.ds((1 - self.bit(level)) * size, size)]
+        self.start(away, self.stages[level], self.peer(level))
+
+    def add(self, level):
+        size = self.count >> (level + 1)
+        kept = self.held(level)[pl.ds(self.bit(level) * size, size)]
+        got = self.stages[level]
+        got[...] = (widen(kept) + widen(got[...])).astype(got.dtype)
+
+    def double(self, level):
+        size = self.count >> (level + 1)
+        region = self.total.at[pl.ds(self.place(level), size)]
+        self.start(region, region, self.peer(level))
+
+    def step(self, index):
+        last = self.levels
+        if index > 0:
+            if index > 2 * last + int(self.crossed):
+                return False
+            self.copies[index - 1].wait_recv()
+        if index < last:
+            if index > 0:
+                self.add(index - 1)
+            self.halve(index)
+            return True
+        at = index - last
+        if at == 0:
+            self.add(last - 1)
+            piece = self.stages[last - 1]
+            home = self.total.at[pl.ds(self.place(last - 1), 1)]
+            if self.crossed:
+                self.start(piece, home, col_peer())
+                return True
+            home[...] = piece[...]
+        level = last - 1 - (at - int(self.crossed))
+        if level >= 0:
+            self.double(level)
+        else:
+            self.emit(self.total)
+        return True
+
+    def finish(self):
+        for copy in self.copies:
+            copy.wait_send()
+
+
+def run_chunks(chunks):
+    for chunk in chunks:
+        chunk.step(0)
+    begun = [1] * len(chunks)
+    longest = max(2 * c.levels + int(c.crossed) for c in chunks)
+    for tick in range(longest + len(chunks)):
+        for i, chunk in enumerate(chunks):
+            if tick >= i and begun[i] <= 2 * chunk.levels + int(chunk.crossed):
+                chunk.step(begun[i])
+                begun[i] += 1
+    for chunk in chunks:
+        chunk.finish()
+
+
+def grad_kernel(og_ref, igg_ref, igi_ref, small_ref, og_out, ig_out, small_out, totals, *rest):
+    count = og_ref.shape[1]
+    levels = len(seq_bits(count))
+    halves, smalls, send, recv = rest[:levels], rest[levels : 2 * levels], rest[-2], rest[-1]
+    col = lax.axis_index("col")
     me = lax.axis_index("seq")
-    for mask in seq_bits(count):
-        half = value.shape[0] // 2
-        mine = (me // mask) % 2
-        keep = lax.dynamic_slice_in_dim(value, mine * half, half, 0)
-        give = lax.dynamic_slice_in_dim(value, (1 - mine) * half, half, 0)
-        got = lax.ppermute(give, "seq", [(i, i ^ mask) for i in range(count)])
-        value = (keep.astype(F32) + got.astype(F32)).astype(value.dtype)
-    return value
-
-
-def gather_back(value, count):
-    me = lax.axis_index("seq")
-    for mask in reversed(seq_bits(count)):
-        mine = (me // mask) % 2
-        got = lax.ppermute(value, "seq", [(i, i ^ mask) for i in range(count)])
-        low = jnp.where(mine == 0, value, got)
-        high = jnp.where(mine == 0, got, value)
-        value = jnp.concatenate([low, high], axis=0)
-    return value
+    rows, width = og_ref.shape[2], og_ref.shape[3]
+
+    def rows_out(side):
+        def emit(total):
+            for i in range(count):
+                at = pl.multiple_of(side * count * rows, count * rows) + i * rows
+                og_out[pl.ds(pl.multiple_of(at, 8), rows), :] = widen(total[i])
+        return emit
+
+    def lanes_out(which, side):
+        def emit(total):
+            at = pl.multiple_of(side * width, width)
+            for i in range(count):
+                ig_out[which, i * rows : (i + 1) * rows, pl.ds(at, width)] = widen(total[i])
+        return emit
+
+    def small_emit(total):
+        pass
+
+    peers = [
+        {"seq": me + mask - 2 * mask * ((me // mask) % 2)} for mask in seq_bits(count)
+    ]
+    barrier_with([col_peer()] + peers)
+    chunks = []
+    plan = [
+        (og_ref, 0, rows_out(col), False),
+        (og_ref, 1, rows_out(1 - col), False),
+        (igg_ref, 0, lanes_out(1, col), True),
+        (igg_ref, 1, lanes_out(1, 1 - col), True),
+        (igi_ref, 0, lanes_out(0, col), False),
+        (igi_ref, 1, lanes_out(0, 1 - col), False),
+    ]
+    for i, (source, h, emit, swapped) in enumerate(plan):
+        chunks.append(
+            Chunk(
+                source.at[h], totals.at[i], [s.at[i] for s in halves], send.at[i], recv.at[i],
+                mask_order(count, swapped), h == 1, emit,
+            )
+        )
+    chunks.append(
+        Chunk(
+            small_ref, small_out, smalls, send.at[len(plan)], recv.at[len(plan)],
+            mask_order(count, False), False, small_emit,
+        )
+    )
+    run_chunks(chunks)
+
+
+def grad_sum(og, igg, igi, small):
+    _, count, rows, width = og.shape
+    levels = len(seq_bits(count))
+    scratch = [pltpu.VMEM((6, count, rows, width), BF16)]
+    scratch += [pltpu.VMEM((6, count >> (k + 1), rows, width), BF16) for k in range(levels)]
+    scratch += [pltpu.VMEM((count >> (k + 1),) + small.shape[1:], F32) for k in range(levels)]
+    scratch += [pltpu.SemaphoreType.DMA((7, 2 * levels + 1))] * 2
+    return run_kernel(
+        grad_kernel,
+        (
+            struct((2 * count * rows, width), F32),
+            struct((2, count * rows, 2 * width), F32),
+            struct(small.shape, F32),
+        ),
+        (og, igg, igi, small),
+        "grad_sum",
+        scratch=scratch,
+        collective=9,
+    )
 
 
 def on_device(
@@ -1065,9 +1221,6 @@
         hid_tile, tail_table, tok_tile, toko_tile, gain, cot_tile, parents, lengths, width
     )
 
-    def flat(pair):
-        return pair.reshape(-1, pair.shape[-1])
-
     small = jnp.concatenate(
         [
             step_part, decay_part, select_part, conv_part[:5], skip_part[:1], step_bias_part[:1],
@@ -1077,23 +1230,15 @@
     )
     pad = -small.shape[0] % (8 * count)
     small = jnp.pad(small, ((0, pad), (0, 0)))
-    first = jnp.concatenate([flat(out_part), flat(ig_gate)], axis=0)
-    first = gather_back(sum_scatter(first, count), count)
-    second = gather_back(sum_scatter(flat(ig_inner), count), count)
-    small = gather_back(sum_scatter(small, count), count)
-    og = first[: 2 * inner].reshape(2, inner, half)
-    igg = first[2 * inner :].reshape(2, half, inner)
-    igi = second.reshape(2, half, inner)
-    from_pair = lax.ppermute(jnp.stack([og[1], igg[1], igi[1]]), "col", swap)
-    left = col == 0
-
-    def beside(own, other, axis):
-        return jnp.concatenate(
-            [jnp.where(left, own, other), jnp.where(left, other, own)], axis=axis
-        ).astype(F32)
-
-    out_grad = beside(og[0], from_pair[0], 0)
-    in_grad = jnp.stack([beside(igi[0], from_pair[2], 1), beside(igg[0], from_pair[1], 1)], axis=1)
+
+    def split(value):
+        return value.reshape(2, count, value.shape[1] // count, value.shape[2])
+
+    out_grad, in_both, small = grad_sum(
+        split(out_part), split(ig_gate), split(ig_inner), small.reshape(count, -1, inner)
+    )
+    small = small.reshape(-1, inner)
+    in_grad = in_both.transpose(1, 0, 2)
     at = 0
     pieces = []
     for size in (rank, states, selects, 4, 1, 1, 1, 1):

time: 382 us -> 330 us (0.86)
  waiting for transfers between devices: 97 us -> 0.01 us
  Pallas kernels: 204 us -> 279 us
  other arithmetic: 18.1 us -> 1.96 us
  starting transfers between devices: 17.9 us -> 2.09 us
    ppermute x19 -> x0, waiting for transfers between devices: 97 us -> none  [the longest x9 51.2 us: gather_back(): got = lax.ppermute(value, 'seq', [(i, i ^ mask) for i in range(count)])]
    pallas_call x15 -> x16, Pallas kernels: 204 us -> 279 us  [run_kernel(): pl.pallas_call(kernel, out_shape=outs, in_specs=[smem_spec() if a.dtype =...]
    ppermute x19 -> x0, starting transfers between devices: 15.8 us -> none  [the longest x9 10.7 us: sum_scatter(): got = lax.ppermute(give, 'seq', [(i, i ^ mask) for i in range(count)])]
    convert_element_type x7 -> x0, other arithmetic: 6.12 us -> none  [the longest x6 4.52 us: sum_scatter(): value = (keep.astype(F32) + got.astype(F32)).astype(value.dtype)]
    select_n x9 -> x0, other arithmetic: 3.98 us -> none  [the longest x8 2.04 us: gather_back(): low = jnp.where(mine == 0, value, got)]
    unnamed x44 -> x39, local copies, waits for them, and re-layouts: 8.25 us -> 11.2 us
  transfers between devices with their start and end apart: 21 -> 2, of which waited for: 11 -> 0; matrix products, arithmetic and copies ran while one was open for 8% -> 3% of each run, Pallas kernels for 35% -> 11%
where the time goes in v1:
time: 330 us; the launch traced here: 329 us
  Pallas kernels  279 us (85%)
  local copies, waits for them, and re-layouts  43 us (13%)
    pallas_call x16, Pallas kernels, run_kernel(): pl.pallas_call(kernel, out_shape=outs, in_specs=[smem_spec() if a.dtype =...  279 us
    unnamed x39, local copies, waits for them, and re-layouts  11.2 us
  transfers between devices with their start and end apart: 2, of which 0 were waited for; matrix products, arithmetic and copies ran while one was open for 3% of the time, Pallas kernels for 11%

profile of v1, /device:TPU:0, one launch (start us, length us, event | category | flops | bytes accessed | tf_op | source)
XLA Modules:
  0.0 329.0 jit_solution(7381454239163888014)
XLA Ops:
  0.7 1.3 dynamic_slice.47.ints_ref.length_ref
  3.3 1.4 constant_dynamic-slice_fusion.9.tail_ref
  4.6 2.8 constant_dynamic-slice_fusion.3
  7.5 5.1 %constant_dynamic-slice_fusion.5 = (bf16[512,1,512]{2,1,0:T(2,128)(2,1)S(1)}, bf16[512,1,512]{2,1,0:T(2,128)(2,1)S(1)}, bf16[512,1,512]{2,1,0:T(2,128)(2,1)S(1)}, bf16[512,1,512]{2,1,0:T(2,128)(2,1)S(1)}) fusion(bf16[512,2,1024]{2,1,0:T(2,128)(2,1)S(1)} %copy-done.1, s32[]{:T(128)S(6)} %add.44, s32[]{:T(128)S(6)} %select_n.31, s32[]{:T(128)S(6)} %select_n.32), kind=kLoop, calls=%fused_computation.11 | loop fusion | bytes 4194316 | tf_op jit(solution)/shard_map/slice | solution.py:1077
  12.7 1.2 copy_bitcast_fusion.1
  14.5 21.4 %entry_exchange.1 = (bf16[8,8,1024]{2,1,0:T(8,128)(2,1)}, bf16[512,512]{1,0:T(8,128)(2,1)}, bf16[8,512]{1,0:T(8,128)(2,1)}) custom-call(bf16[8,1024]{1,0:T(8,128)(2,1)} %constant_dynamic-slice_fusion.9.tail_ref, bf16[512,512]{1,0:T(8,128)(2,1)} %get-tuple-element.141.wi_ref, bf16[8,512]{1,0:T(8,128)(2,1)} %broadcast_in_dim.10.gain_ref), custom_call_target="tpu_custom_call" | custom-call | bytes 548864 | tf_op jit(solution)/shard_map/entry_exchange/pallas_call | solution.py:99
  36.5 1.5 collective-permute-start.1
  39.4 1.5 constant_dynamic-slice_fusion.6
  40.9 1.3 copy_bitcast_fusion
  42.7 5.6 %forward_in.1 = (bf16[2,512,512]{2,1,0:T(8,128)(2,1)}, bf16[2,8,512]{2,1,0:T(8,128)(2,1)}, f32[536,512]{1,0:T(8,128)}, bf16[512,512]{1,0:T(8,128)(2,1)}, f32[512,96]{1,0:T(8,128)}) custom-call(bf16[512,512]{1,0:T(8,128)(2,1)} %get-tuple-element.136.tok_ref, bf16[512,512]{1,0:T(8,128)(2,1)} %get-tuple-element.137.toko_ref, ...), custom_call_target="tpu_custom_call" | custom-call | flops 2000000000 | bytes 2355204 | tf_op jit(solution)/shard_map/forward_in/pallas_call | solution.py:99
  50.2 13.6 %select_sum.1.sel_ref = f32[512,96]{1,0:T(8,128)} custom-call(f32[512,96]{1,0:T(8,128)} %get-tuple-element.64.x_ref), custom_call_target="tpu_custom_call" | custom-call | bytes 196608 | tf_op jit(solution)/shard_map/select_sum/pallas_call | solution.py:99
  64.4 9.9 %forward_ends.1 = (f32[512,512]{1,0:T(8,128)}, f32[512,512]{1,0:T(8,128)}, f32[16,8,512]{2,1,0:T(8,128)}, f32[8,512]{1,0:T(8,128)}, bf16[24,512]{1,0:T(8,128)(2,1)}) custom-call(f32[512,96]{1,0:T(8,128)} %select_sum.1.sel_ref, bf16[64,512]{1,0:T(8,128)(2,1)} %tw_ref.3, bf16[8,512]{1,0:T(8,128)(2,1)} %broadcast_in_dim.12.tb_ref, f32[16,512]{1,0:T(8,128)} %dl_ref.7, ...), custom_call_target="tpu_custom_call" | custom-call | flops 2000000000 | bytes 827396 | tf_op jit(solution)/shard_map/forward_ends/pallas_call | solution.py:99
  74.3 8.2 %state_gather.1.table_ref = bf16[8,24,512]{2,1,0:T(8,128)(2,1)} custom-call(bf16[24,512]{1,0:T(8,128)(2,1)} %get-tuple-element.66.x_ref), custom_call_target="tpu_custom_call" | custom-call | bytes 24576 | tf_op jit(solution)/shard_map/state_gather/pallas_call | solution.py:99
  85.1 13.4 %forward_out.1 = (f32[16,8,512]{2,1,0:T(8,128)}, f32[512,512]{1,0:T(8,128)}, f32[512,512]{1,0:T(8,128)}, bf16[512,512]{1,0:T(8,128)(2,1)}, bf16[2,512,512]{2,1,0:T(8,128)(2,1)}) custom-call(bf16[8,24,512]{2,1,0:T(8,128)(2,1)} %state_gather.1.table_ref, s32[8]{0:T(128)} %parents_ref.5, s32[1]{0:T(128)} %bitcast.5.me_ref, f32[16,512]{1,0:T(8,128)} %dl_ref.7, ...), custom_call_target="tpu_custom_call" | custom-call | flops 4000000000 | bytes 5431332 | tf_op jit(solution)/shard_map/forward_out/pallas_call | solution.py:99
  99.1 21.6 %middle_exchange.1 = (bf16[256,512]{1,0:T(8,128)(2,1)}, f32[256,512]{1,0:T(8,128)}, bf16[2,512,512]{2,1,0:T(8,128)(2,1)}) custom-call(bf16[2,512,512]{2,1,0:T(8,128)(2,1)} %get-tuple-element.73.part_ref, bf16[256,512]{1,0:T(8,128)(2,1)} %get-tuple-element.125.tok_ref, bf16[256,512]{1,0:T(8,128)(2,1)} %constant_dynamic-slice_fusion.2.teach_ref, ...), custom_call_target="tpu_custom_call" | custom-call | bytes 1576964 | tf_op jit(solution)/shard_map/middle_exchange/pallas_call | solution.py:99
  120.7 13.0 %backward_in.1 = (bf16[2,512,512]{2,1,0:T(8,128)(2,1)}, bf16[512,512]{1,0:T(8,128)(2,1)}, bf16[2,512,512]{2,1,0:T(8,128)(2,1)}, f32[512,512]{1,0:T(8,128)}, f32[...) custom-call(bf16[2,512,512]{2,1,0:T(8,128)(2,1)} %get-tuple-element.75.cot_ref, ...), custom_call_target="tpu_custom_call" | custom-call | flops 4000000000 | bytes 7593984 | tf_op jit(solution)/shard_map/backward_in/pallas_call | solution.py:99
  134.4 8.2 %flow_gather.1.flows_ref = bf16[8,16,512]{2,1,0:T(8,128)(2,1)} custom-call(bf16[16,512]{1,0:T(8,128)(2,1)} %get-tuple-element.79.x_ref), custom_call_target="tpu_custom_call" | custom-call | bytes 16384 | tf_op jit(solution)/shard_map/flow_gather/pallas_call | solution.py:99
  142.6 24.5 %backward_scan.1 = (f32[512,96]{1,0:T(8,128)}, f32[512,512]{1,0:T(8,128)}, f32[8,512]{1,0:T(8,128)}, f32[64,512]{1,0:T(8,128)}, f32[16,512]{1,0:T(8,128)}) custom-call(bf16[8,24,512]{2,1,0:T(8,128)(2,1)} %state_gather.1.table_ref, bf16[8,16,512]{2,1,0:T(8,128)(2,1)} %flow_gather.1.flows_ref, s32[8]{0:T(128)} %parents_ref.5, s32[1]{0:T(128)} %bitcast.5.me_ref, ...), custom_call_target="tpu_custom_call" | custom-call | flops 8000000000 | bytes 4833320 | tf_op jit(solution)/shard_map/backward_scan/pallas_call | solution.py:99
  167.1 9.0 %select_grad_sum.1.selg_ref = f32[512,96]{1,0:T(8,128)} custom-call(f32[512,96]{1,0:T(8,128)} %get-tuple-element.84.x_ref), custom_call_target="tpu_custom_call" | custom-call | bytes 196608 | tf_op jit(solution)/shard_map/select_grad_sum/pallas_call | solution.py:99
  176.8 8.4 %backward_out.1 = (bf16[2,512,512]{2,1,0:T(8,128)(2,1)}, bf16[2,512,512]{2,1,0:T(8,128)(2,1)}, f32[2,8,512]{2,1,0:T(8,128)}, f32[96,512]{1,0:T(8,128)}, f32[8,512]{1,0:T(8,128)}) custom-call(f32[512,96]{1,0:T(8,128)} %select_grad_sum.1.selg_ref, bf16[512,512]{1,0:T(8,128)(2,1)} %get-tuple-element.65.act_ref, bf16[512,96]{1,0:T(8,128)(2,1)} %copy.29.sw_ref, ...), custom_call_target="tpu_custom_call" | custom-call | flops 6000000000 | bytes 7720960 | tf_op jit(solution)/shard_map/backward_out/pallas_call | solution.py:99
  185.3 12.5 %hidden_exchange.1 = (f32[256,512]{1,0:T(8,128)}, f32[8,512]{1,0:T(8,128)}) custom-call(bf16[2,512,512]{2,1,0:T(8,128)(2,1)} %get-tuple-element.89.part_ref, f32[2,8,512]{2,1,0:T(8,128)} %get-tuple-element.90.tail_ref), custom_call_target="tpu_custom_call" | custom-call | bytes 1081344 | tf_op jit(solution)/shard_map/hidden_exchange/pallas_call | solution.py:99
  198.5 1.3 pad_maximum_fusion.x_ref
  199.8 8.5 %tail_gather.1.tails_ref = f32[8,8,512]{2,1,0:T(8,128)} custom-call(f32[8,512]{1,0:T(8,128)} %pad_maximum_fusion.x_ref), custom_call_target="tpu_custom_call" | custom-call | bytes 16384 | tf_op jit(solution)/shard_map/tail_gather/pallas_call | solution.py:99
  208.4 7.5 %finish_exchange.1 = (f32[256,512]{1,0:T(8,128)}, f32[8,512]{1,0:T(8,128)}) custom-call(f32[256,512]{1,0:T(8,128)} %get-tuple-element.91.hid_ref, f32[8,8,512]{2,1,0:T(8,128)} %tail_gather.1.tails_ref, bf16[256,512]{1,0:T(8,128)(2,1)} %get-tuple-element.125.tok_ref, bf16[256,512]{1,0:T(8,128)(2,1)} %get-tuple-element.124.toko_ref, ...), custom_call_target="tpu_custom_call" | custom-call | bytes 1712192 | tf_op jit(solution)/shard_map/finish_exchange/pallas_call | solution.py:99
  217.5 93.8 %grad_sum.1 = (f32[1024,512]{1,0:T(8,128)}, f32[2,512,1024]{2,1,0:T(8,128)}, f32[8,24,512]{2,1,0:T(8,128)}) custom-call(bf16[2,8,64,512]{3,2,1,0:T(8,128)(2,1)} %bitcast.27, bf16[2,8,64,512]{3,2,1,0:T(8,128)(2,1)} %bitcast.28, bf16[2,8,64,512]{3,2,1,0:T(8,128)(2,1)} %bitcast.29, f32[8,24,512]{2,1,0:T(8,128)} %bitcast.26), custom_call_target="tpu_custom_call" | custom-call | bytes 3538944 | tf_op jit(solution)/shard_map/grad_sum/pallas_call | solution.py:99
  311.3 1.3 slice.73
  312.6 1.5 fusion.1
  314.0 1.4 slice.78
  315.4 1.6 slice.76
  317.0 1.6 slice_bitcast_fusion
  318.6 7.6 %copy.31 = f32[512,2,1024]{2,1,0:T(2,128)} copy(f32[512,2,1024]{2,0,1:T(8,128)} %bitcast.25) | data formatting | bytes 8388608
  327.7 1.3 copy.47
  (56 shorter events, 13.3 us)
Async XLA Ops:
  0.6 81.9 %copy-start = (bf16[512,512]{1,0:T(8,128)(2,1)S(1)}, bf16[512,512]{1,0:T(8,128)(2,1)}, u32[]{:S(2)}) copy-start(bf16[512,512]{1,0:T(8,128)(2,1)} %param.16) | copy-start | bytes 1572868
  4.6 2.8 copy-start.1
  12.6 1.3 copy-start.11
  12.6 25.4 %copy-start.15 = (s32[8]{0:T(128)S(1)}, s32[8]{0:T(128)}, u32[]{:S(2)}) copy-start(s32[8]{0:T(128)} %parents_ref.5) | copy-start | bytes 100
  12.6 26.0 %copy-start.8 = (bf16[512,96]{0,1:T(8,128)(2,1)S(1)}, bf16[512,96]{0,1:T(8,128)(2,1)}, u32[]{:S(2)}) copy-start(bf16[512,96]{0,1:T(8,128)(2,1)} %param.21) | copy-start | bytes 294916
  14.5 27.6 %copy-start.12 = (bf16[512]{0:T(512)(128)(2,1)S(1)}, bf16[512]{0:T(512)(128)(2,1)}, u32[]{:S(2)}) copy-start(bf16[512]{0:T(512)(128)(2,1)} %param.20) | copy-start | bytes 3076
  35.9 48.5 %collective-permute-start = (bf16[512,512]{1,0:T(8,128)(2,1)}, bf16[512,512]{1,0:T(8,128)(2,1)}, u32[]{:S(2)}, u32[]{:S(2)}) collective-permute-start(bf16[512,512]{1,0:T(8,128)(2,1)} %get-tuple-element.71), channel_id=1, source_target_pairs={{0,1},{1,0},{2,3},{3,2},{4,5},{5,4},{6,7},{7,6},{8,9},{9,8},{10,11... | collective-permute-start | bytes 1572872 | tf_op jit(solution)/shard_map/ppermute | solution.py:1087
  36.5 47.9 %collective-permute-start.1 = (bf16[512,512]{1,0:T(8,128)(2,1)S(1)}, bf16[512,512]{1,0:T(8,128)(2,1)}, u32[]{:S(2)}, u32[]{:S(2)}) collective-permute-start(bf16[512,512]{1,0:T(8,128)(2,1)S(1)} %get-tuple-element.72), channel_id=1, source_target_pairs={{0,1},{1,0},{2,3},{3,2},{4,5},{5,4},{6,7},{7,6},{8,9},{9,8},{10,11... | collective-permute-start | bytes 1572872 | tf_op jit(solution)/shard_map/ppermute | solution.py:1088
  42.7 5.6 %copy-start.16 = (s32[8]{0:T(128)S(1)}, s32[8]{0:T(128)}, u32[]{:S(2)}) copy-start(s32[8]{0:T(128)} %param.29) | copy-start | bytes 100
  42.7 21.1 %copy-start.13 = (bf16[512]{0:T(512)(128)(2,1)S(1)}, bf16[512]{0:T(512)(128)(2,1)}, u32[]{:S(2)}) copy-start(bf16[512]{0:T(512)(128)(2,1)} %param.23) | copy-start | bytes 3076
  64.4 18.9 %copy-start.2 = (bf16[512,1024]{1,0:T(8,128)(2,1)S(1)}, bf16[512,1024]{1,0:T(8,128)(2,1)}, u32[]{:S(2)}) copy-start(bf16[512,1024]{1,0:T(8,128)(2,1)} %param.15) | copy-start | bytes 3145732
  64.4 20.0 %copy-start.14 = (bf16[512]{0:T(512)(128)(2,1)S(1)}, bf16[512]{0:T(512)(128)(2,1)}, u32[]{:S(2)}) copy-start(bf16[512]{0:T(512)(128)(2,1)} %param.25) | copy-start | bytes 3076
  185.2 31.4 %copy-start.6 = (f32[96,512]{1,0:T(8,128)S(1)}, f32[96,512]{1,0:T(8,128)}, u32[]{:S(2)}) copy-start(f32[96,512]{1,0:T(8,128)} %get-tuple-element.100) | copy-start | bytes 589828
  185.2 31.4 %copy-start.7 = (f32[64,512]{1,0:T(8,128)S(1)}, f32[64,512]{1,0:T(8,128)}, u32[]{:S(2)}) copy-start(f32[64,512]{1,0:T(8,128)} %get-tuple-element.98) | copy-start | bytes 393220
  185.3 31.4 %copy-start.9 = (f32[16,512]{1,0:T(8,128)S(1)}, f32[16,512]{1,0:T(8,128)}, u32[]{:S(2)}) copy-start(f32[16,512]{1,0:T(8,128)} %get-tuple-element.99) | copy-start | bytes 98308
  185.3 31.4 %copy-start.10 = (f32[8,512]{1,0:T(8,128)S(1)}, f32[8,512]{1,0:T(8,128)}, u32[]{:S(2)}) copy-start(f32[8,512]{1,0:T(8,128)} %get-tuple-element.101) | copy-start | bytes 49156
  318.6 7.6 %copy-start.5 = (bf16[256,512]{1,0:T(8,128)(2,1)S(1)}, bf16[256,512]{1,0:T(8,128)(2,1)}, u32[]{:S(2)}) copy-start(bf16[256,512]{1,0:T(8,128)(2,1)} %get-tuple-element.154) | copy-start | bytes 786436
  318.6 8.3 %copy-start.4 = (f32[256,512]{1,0:T(8,128)S(1)}, f32[256,512]{1,0:T(8,128)}, u32[]{:S(2)}) copy-start(f32[256,512]{1,0:T(8,128)} %get-tuple-element.155) | copy-start | bytes 1572868
  318.6 9.1 %copy-start.3 = (f32[1024,512]{1,0:T(8,128)S(1)}, f32[1024,512]{1,0:T(8,128)}, u32[]{:S(2)}) copy-start(f32[1024,512]{1,0:T(8,128)} %get-tuple-element.165) | copy-start | bytes 6291460

commit v2 on v0

--- a/solution.py
+++ b/solution.py
@@ -15,6 +15,7 @@
 lanes = 128
 log2e = 1.4426950408889634
 vmem_bytes = 60 * 1024 * 1024
+vmem_most = 67043328
 
 
 def vmem_spec():
@@ -92,8 +93,8 @@
     return lax.broadcasted_iota(jnp.int32, shape, len(shape) - 2)
 
 
-def run_kernel(kernel, outs, args, name, scratch=(), specs=None, flops=0, collective=None):
-    params = dict(vmem_limit_bytes=vmem_bytes)
+def run_kernel(kernel, outs, args, name, scratch=(), flops=0, collective=None, grant=vmem_bytes):
+    params = dict(vmem_limit_bytes=grant)
     if collective is not None:
         params.update(collective_id=collective, has_side_effects=True)
     return pl.pallas_call(
@@ -294,128 +295,6 @@
     )
 
 
-def hidden_kernel(part_ref, tail_ref, out_ref, tout_ref, from_row, trow, to_col, from_col, tcol, tfrom, send, recv):
-    half = out_ref.shape[0]
-    row = lax.axis_index("row")
-    mine = pl.multiple_of(row * half, half)
-    other = pl.multiple_of((1 - row) * half, half)
-    barrier_with([row_peer(), col_peer()])
-    first = [
-        remote(part_ref.at[h, pl.ds(other, half), :], from_row.at[h], send.at[h], recv.at[h], row_peer())
-        for h in (1, 0)
-    ]
-    first.append(remote(tail_ref, trow, send.at[2], recv.at[2], row_peer()))
-    for copy in (first[2], first[0], first[1]):
-        copy.start()
-    first[2].wait()
-    tails = tail_ref[...] + trow[...]
-    tcol[...] = tails[1]
-    last = remote(tcol, tfrom, send.at[3], recv.at[3], col_peer())
-    last.start()
-    first[0].wait()
-    to_col[...] = (
-        part_ref[1, pl.ds(mine, half), :].astype(F32) + from_row[1].astype(F32)
-    ).astype(BF16)
-    second = remote(to_col, from_col, send.at[4], recv.at[4], col_peer())
-    second.start()
-    first[1].wait()
-    out_ref[...] = part_ref[0, pl.ds(mine, half), :].astype(F32) + from_row[0].astype(F32)
-    last.wait()
-    tout_ref[...] = tails[0] + tfrom[...]
-    second.wait()
-    out_ref[...] += from_col[...].astype(F32)
-
-
-def hidden_exchange(part, tail):
-    _, rows, width = part.shape
-    half = rows // 2
-    return run_kernel(
-        hidden_kernel,
-        (struct((half, width), F32), struct(tail.shape[1:], F32)),
-        (part, tail),
-        "hidden_exchange",
-        scratch=[
-            pltpu.VMEM((2, half, width), BF16),
-            pltpu.VMEM(tail.shape, F32),
-            pltpu.VMEM((half, width), BF16),
-            pltpu.VMEM((half, width), BF16),
-            pltpu.VMEM(tail.shape[1:], F32),
-            pltpu.VMEM(tail.shape[1:], F32),
-            pltpu.SemaphoreType.DMA((5,)),
-            pltpu.SemaphoreType.DMA((5,)),
-        ],
-        collective=5,
-    )
-
-
-def finish_kernel(
-    hid_ref, tails_ref, tok_ref, toko_ref, gain_ref, cot_ref, parents_ref, lengths_ref,
-    tg_ref, gg_ref, mean_out, mean_in, gain_out, gain_in, send, recv, *, width
-):
-    half = tok_ref.shape[0]
-    count, margin8 = tails_ref.shape[0], tails_ref.shape[1]
-    row = lax.axis_index("row")
-    me = lax.axis_index("seq")
-    barrier_with([row_peer(), col_peer()])
-    positions = row * half + lax.broadcasted_iota(jnp.int32, (half, margin8), 0)
-    slot = lax.broadcasted_iota(jnp.int32, (half, margin8), 1)
-    hidden = hid_ref[...]
-    length = lengths_ref[me]
-    own_tail = jnp.zeros(tails_ref.shape[1:], F32)
-    for child in range(count):
-        is_child = (parents_ref[child] == me).astype(F32)
-        own_tail = own_tail + is_child * tails_ref[child].astype(F32)
-    place = ((positions == length - 3 + slot) & (slot < 3)).astype(F32)
-    hidden = hidden + jnp.dot(place, own_tail, preferred_element_type=F32, precision=lax.Precision.HIGHEST)
-    tok = tok_ref[...].astype(F32)
-    toko = toko_ref[...].astype(F32)
-    total = jnp.sum(tok * tok, axis=1, keepdims=True) + jnp.sum(toko * toko, axis=1, keepdims=True)
-    inv = lax.rsqrt(total / width + norm_epsilon)
-    normed = tok * inv
-    gain_out[...] = jnp.broadcast_to(jnp.sum(hidden * normed, axis=0, keepdims=True), gain_out.shape)
-    scaled = hidden * gain_ref[0:1, :].astype(F32)
-    mean = jnp.sum(scaled * normed, axis=1, keepdims=True)
-    ones = jnp.ones((8, lanes), F32)
-    mean_out[...] = lax.dot_general(
-        ones, jnp.broadcast_to(mean / lanes, (half, lanes)), (((1,), (1,)), ((), ())),
-        preferred_element_type=F32, precision=lax.Precision.HIGHEST,
-    )
-    copies = [
-        remote(mean_out, mean_in, send.at[0], recv.at[0], col_peer()),
-        remote(gain_out, gain_in, send.at[1], recv.at[1], row_peer()),
-    ]
-    for copy in copies:
-        copy.start()
-    for copy in copies:
-        copy.wait()
-    other = lax.dot_general(
-        mean_in[...], jnp.full((8, lanes), 0.125, F32), (((0,), (0,)), ((), ())),
-        preferred_element_type=F32, precision=lax.Precision.HIGHEST,
-    )
-    mean = (mean + other[:, 0:1]) / width
-    tg_ref[...] = cot_ref[...] + inv * (scaled - normed * mean)
-    gg_ref[...] = gain_out[...] + gain_in[...]
-
-
-def finish_exchange(hid, tails, tok, toko, gain, cot, parents, lengths, width):
-    half, cols = hid.shape
-    return run_kernel(
-        functools.partial(finish_kernel, width=width),
-        (struct((half, cols), F32), struct((8, cols), F32)),
-        (hid, tails, tok, toko, gain, cot, parents, lengths),
-        "finish_exchange",
-        scratch=[
-            pltpu.VMEM((8, half), F32),
-            pltpu.VMEM((8, half), F32),
-            pltpu.VMEM((8, cols), F32),
-            pltpu.VMEM((8, cols), F32),
-            pltpu.SemaphoreType.DMA((2,)),
-            pltpu.SemaphoreType.DMA((2,)),
-        ],
-        collective=6,
-    )
-
-
 def forward_in_kernel(
     tok_ref, toko_ref, tails_ref, tailso_ref, gain_ref, gaino_ref, wi_ref, wio_ref,
     cw_ref, cb_ref, sw_ref, ints_ref,
@@ -684,49 +563,282 @@
     flow_ref[...] = jnp.concatenate(
         [back_ref[n, 0:1, :] for n in range(states)], axis=0
     ).astype(BF16)
-    og_ref[0] = dot_tn(mixed_ref[...], cot).astype(BF16)
-    og_ref[1] = dot_tn(mixed_ref[...], coto).astype(BF16)
-    ig_ref[0] = dot_tn(hid_ref[0], gate_grad).astype(BF16)
-    ig_ref[1] = dot_tn(hid_ref[1], gate_grad).astype(BF16)
-
-
-def backward_scan_kernel(
-    table_ref, flows_ref, parents_ref, me_ref, length_ref, dl_ref, starts_ref, back_ref, cum_ref,
+    store_split(og_ref.at[0], dot_tn(mixed_ref[...], cot))
+    store_split(og_ref.at[1], dot_tn(mixed_ref[...], coto))
+    store_split(ig_ref.at[0], dot_tn(hid_ref[0], gate_grad))
+    store_split(ig_ref.at[1], dot_tn(hid_ref[1], gate_grad))
+
+
+def seq_bits(count):
+    bits = []
+    mask = 1
+    while mask < count:
+        bits.append(mask)
+        mask *= 2
+    return bits
+
+
+def mask_order(count, swapped):
+    bits = seq_bits(count)
+    if swapped and len(bits) > 1:
+        bits = [bits[1], bits[0]] + bits[2:]
+    return bits
+
+
+def widen(values):
+    return values.astype(F32)
+
+
+class Chunk:
+    def __init__(self, source, total, stages, send, recv, masks, crossed, emit):
+        self.source, self.total, self.stages = source, total, stages
+        self.send, self.recv, self.masks, self.crossed, self.emit = send, recv, masks, crossed, emit
+        self.count = source.shape[0]
+        self.me = lax.axis_index("seq")
+        self.copies = []
+        self.at = 0
+        self.levels = len(masks)
+
+    def bit(self, level):
+        return (self.me // self.masks[level]) % 2
+
+    def peer(self, level):
+        mask = self.masks[level]
+        return {"seq": self.me + mask - 2 * mask * self.bit(level)}
+
+    def start(self, src, dst, peer):
+        at = len(self.copies)
+        copy = remote(src, dst, self.send.at[at], self.recv.at[at], peer)
+        copy.start()
+        self.copies.append(copy)
+
+    def place(self, level):
+        start = 0
+        for j in range(level + 1):
+            start = start + self.bit(j) * (self.count >> (j + 1))
+        return start
+
+    def held(self, level):
+        return self.source if level == 0 else self.stages[level - 1]
+
+    def halve(self, level):
+        size = self.count >> (level + 1)
+        away = self.held(level).at[pl.ds((1 - self.bit(level)) * size, size)]
+        self.start(away, self.stages[level], self.peer(level))
+
+    def add(self, level):
+        size = self.count >> (level + 1)
+        kept = self.held(level)[pl.ds(self.bit(level) * size, size)]
+        got = self.stages[level]
+        got[...] = (widen(kept) + widen(got[...])).astype(got.dtype)
+
+    def double(self, level):
+        size = self.count >> (level + 1)
+        region = self.total.at[pl.ds(self.place(level), size)]
+        self.start(region, region, self.peer(level))
+
+    def step(self, index):
+        last = self.levels
+        if index > 0:
+            self.copies[index - 1].wait_recv()
+        if index < last:
+            if index > 0:
+                self.add(index - 1)
+            self.halve(index)
+            return
+        at = index - last
+        if at == 0:
+            self.add(last - 1)
+            piece = self.stages[last - 1]
+            home = self.total.at[pl.ds(self.place(last - 1), 1)]
+            if self.crossed:
+                self.start(piece, home, col_peer())
+                return
+            home[...] = piece[...]
+        level = last - 1 - (at - int(self.crossed))
+        if level >= 0:
+            self.double(level)
+        else:
+            self.emit(self.total)
+
+    def done(self):
+        return self.at > 2 * self.levels + int(self.crossed)
+
+    def next(self):
+        if not self.done():
+            self.step(self.at)
+            self.at += 1
+
+    def finish(self):
+        for copy in self.copies:
+            copy.wait_send()
+
+
+def store_split(ref, value):
+    rows = ref.shape[1]
+    for i in range(ref.shape[0]):
+        ref[i] = value[i * rows : (i + 1) * rows].astype(ref.dtype)
+
+
+def advance_all(chunks):
+    for chunk in chunks:
+        chunk.next()
+
+
+def run_out(chunks):
+    while any(not chunk.done() for chunk in chunks):
+        advance_all(chunks)
+    for chunk in chunks:
+        chunk.finish()
+
+
+def small_rows(count, rank, states, selects):
+    total = rank + states + selects + 8
+    total += -total % (8 * count)
+    return total // count
+
+
+def backward_kernel(
+    table_ref, flow_ref, parents_ref, lengths_ref, dl_ref, starts_ref, back_ref, cum_ref,
     delta_ref, act_ref, sel_ref, pgrad_ref, pre_ref, tw_ref,
-    selg_ref, agrad_ref, small_ref, stepg_ref, dgrad_ref,
-    grads, drive, b_ref, c_ref, rate_ref, decay_buf, state_buf, b_sum, c_sum, dg_ref,
+    sw_ref, skip_ref, ext_ref, cw_ref, cb_ref, hid_ref, hidt_ref, wi_ref, wio_ref, wg_ref, wgo_ref,
+    ggrad_ref, tok_ref, toko_ref, gain_ref, cot_ref, og_ref, igg_ref, sgrad_ref,
+    og_out, ig_out, tg_ref, gg_ref, stepg_out, decayg_out, selectg_out, smallg_out,
+    flows_ref, grads, c_ref, rate_ref, decay_buf, state_buf, b_sum, c_sum, agrad_ref, dgrad_ref,
+    sel_part, sel_row, sel_low, sel_col, cig_ref, part_ref, tpart_ref,
+    hid_row, tail_row, hid_low, hid_col, tail_low_ref, tail_col, tail_own, tails_ref,
+    mean_out, mean_in, gain_out, gain_in, gain_pair, gains_ref,
+    igi_ref, small_ref, totals, small_total, *rest,
+    width,
 ):
-    rows, width = act_ref.shape
+    count = table_ref.shape[0]
+    levels = len(seq_bits(count))
+    halves, smalls = rest[:levels], rest[levels : 2 * levels]
+    send, recv, pair_send, pair_recv, flow_send, flow_recv, tail_send, tail_recv, gain_send, gain_recv = rest[2 * levels :]
+    rows, inner = act_ref.shape
+    half = rows // 2
     steps = rows // spans
     states = dl_ref.shape[0]
     rank = tw_ref.shape[0]
-    count = table_ref.shape[0]
-    me = me_ref[0]
+    selects = sel_ref.shape[1]
+    me = lax.axis_index("seq")
+    row = lax.axis_index("row")
+    col = lax.axis_index("col")
+    mine = pl.multiple_of(row * half, half)
+    other = pl.multiple_of((1 - row) * half, half)
+    length = lengths_ref[me]
+    peers = [{"seq": lax.rem(me + j, count)} for j in range(1, count)]
+    barrier_with([row_peer(), col_peer()] + peers)
+
+    def pair_copy(at, src, dst, peer):
+        copy = remote(src, dst, pair_send.at[at], pair_recv.at[at], peer)
+        copy.start()
+        return copy
+
+    def to_all(src, dst, sends, recvs):
+        copies = [
+            remote(src, dst.at[me], sends.at[j], recvs.at[j], peer) for j, peer in enumerate(peers)
+        ]
+        for copy in copies:
+            copy.start()
+        dst[me] = src[...]
+        return copies
+
+    block_rows, block = og_ref.shape[2], og_ref.shape[3]
+
+    def rows_out(side):
+        def emit(total):
+            base = pl.multiple_of(side * (count * block_rows), count * block_rows)
+            for i in range(count):
+                og_out[pl.ds(pl.multiple_of(base + i * block_rows, 8), block_rows), :] = widen(total[i])
+        return emit
+
+    def lanes_out(which, side):
+        def emit(total):
+            tiles = block // lanes
+            for i in range(count):
+                value = widen(total[i])
+                for j in range(tiles):
+                    first = i * block_rows * 4 * tiles + (side * tiles + j) * 2 + which
+                    ig_out[pl.ds(first, block_rows, stride=4 * tiles), :] = value[:, j * lanes : (j + 1) * lanes]
+        return emit
+
+    def small_slabs():
+        slab = small_ref.shape[1] // 8
+        return lambda at: (at // slab, slice((at % slab) * 8, (at % slab) * 8 + 8))
+
+    place_of = small_slabs()
+
+    def small_store(first, value):
+        for j in range(value.shape[0] // 8):
+            a, b = place_of(first // 8 + j)
+            small_ref[a, b, :] = value[j * 8 : (j + 1) * 8]
+
+    def small_emit(total):
+        def read(first, size):
+            parts = []
+            for j in range(size // 8):
+                a, b = place_of(first // 8 + j)
+                parts.append(total[a, b, :])
+            return jnp.concatenate(parts, axis=0) if len(parts) > 1 else parts[0]
+        stepg_out[...] = read(0, rank)
+        decayg_out[...] = read(rank, states)
+        selectg_out[...] = read(rank + states, selects)
+        smallg_out[...] = read(rank + states + selects, 8)
+
+    plan = [
+        (og_ref, 0, rows_out(col), False),
+        (og_ref, 1, rows_out(1 - col), True),
+        (igg_ref, 0, lanes_out(1, col), False),
+        (igg_ref, 1, lanes_out(1, 1 - col), False),
+        (igi_ref, 0, lanes_out(0, col), False),
+        (igi_ref, 1, lanes_out(0, 1 - col), True),
+    ]
+    chunks = [
+        Chunk(
+            source.at[h], totals.at[i], [s.at[i] for s in halves], send.at[i], recv.at[i],
+            mask_order(count, swapped), h == 1, emit,
+        )
+        for i, (source, h, emit, swapped) in enumerate(plan)
+    ]
+    small_chunk = Chunk(
+        small_ref, small_total, smalls, send.at[len(plan)], recv.at[len(plan)],
+        mask_order(count, False), False, small_emit,
+    )
+
+    drive = og_out.at[0:rows]
+    dg_ref = og_out.at[rows : 2 * rows]
+
+    def b_at(n, step):
+        return ig_out[pl.ds(pl.multiple_of(n * rows + step * spans, spans), spans), :]
+
+    flow_copies = to_all(flow_ref, flows_ref, flow_send, flow_recv)
+    advance_all(chunks[:4])
+    decay_rows(dl_ref, rate_ref, log2e)
     rate = -jnp.exp(dl_ref[...]) * log2e
-    decay_rows(dl_ref, rate_ref, log2e)
-    grads[...] = jnp.zeros(grads.shape, F32)
+    sel = sel_ref[...]
+    drive[...] = delta_ref[...] * act_ref[...].astype(F32)
+    for n in range(states):
+        ig_out[n * rows : (n + 1) * rows, :] = jnp.broadcast_to(
+            sel[:, rank + n : rank + n + 1], (rows, lanes)
+        )
+    c_ref[...] = spread(sel[:, rank + states :], states)
+    index2 = span_index((spans, inner))
+    cum = cum_ref[...]
+    after = cum[spans - 1 : spans, :] - cum
+    inside = index2 < spans - 1
+    slot = lax.broadcasted_iota(jnp.int32, (count, 1, 1), 0)
 
     def visit(visited, carry):
         target = count - 1 - visited
         _, total = segment_sum(table_ref, target, states)
         flow = flows_ref[target].astype(F32) + jnp.exp2(rate * total) * grads[target]
-        above = parents_ref[target]
-        slot = jnp.maximum(above, 0)
-        grads[slot] = grads[slot] + flow * (above >= 0).astype(F32)
+        grads[...] = grads[...] + jnp.where(slot == parents_ref[target], flow[None], 0.0)
         return carry
 
-    lax.fori_loop(0, count - 1, visit, 0)
-    end_grad = grads[me]
-    sel = sel_ref[...]
-    drive[...] = delta_ref[...] * act_ref[...].astype(F32)
-    b_ref[...] = spread(sel[:, rank : rank + states], states)
-    c_ref[...] = spread(sel[:, rank + states :], states)
-    index2 = span_index((spans, width))
-    cum = cum_ref[...]
-    after = cum[spans - 1 : spans, :] - cum
-    inside = index2 < spans - 1
-
-    for group in range(width // lanes):
+    groups = inner // lanes
+    pumps = {(0, 1): (), (1, 0): chunks[:2], (1, 1): chunks[2:4], (2, 0): chunks[:2], (2, 1): (), (3, 0): chunks[2:4], (3, 1): chunks[:2]}
+    for group in range(groups):
         here = slice(group * lanes, (group + 1) * lanes)
 
         def advance(step, carry):
@@ -737,12 +849,20 @@
                 state_buf[n, step_ds(step), :] = carry[n]
                 a = jnp.exp2(d * rate_ref[n, :, here])
                 decay_buf[n, step_ds(step), :] = a
-                out.append(a * carry[n] + w * b_ref[step_ds(step), n * lanes : (n + 1) * lanes])
+                out.append(a * carry[n] + w * b_at(n, step))
             return tuple(out)
 
+        advance_all(pumps.get((group, 0), ()))
         finals = lax.fori_loop(0, steps, advance, tuple(starts_ref[n, :, here] for n in range(states)))
         for n in range(states):
             state_buf[n, rows : rows + spans, :] = finals[n]
+        if group == 0:
+            for copy in flow_copies:
+                copy.wait()
+            grads[...] = jnp.zeros(grads.shape, F32)
+            lax.fori_loop(0, count - 1, visit, 0)
+        advance_all(pumps.get((group, 1), ()))
+        end_grad = grads[me]
 
         later = []
         for n in range(states):
@@ -767,7 +887,7 @@
                 growth = moved * state_buf[n, at, :]
                 new_flows.append(moved)
                 new_sums.append(sums[n] + growth * d)
-                term = adjoint * b_ref[at, cols]
+                term = adjoint * b_at(n, step)
                 weighted[n % 2] = term if weighted[n % 2] is None else weighted[n % 2] + term
                 term = growth * rate_ref[n, :, here]
                 decayed[n % 2] = term if decayed[n % 2] is None else decayed[n % 2] + term
@@ -791,96 +911,190 @@
                 jnp.sum(sums[n], axis=0, keepdims=True) * rate[n : n + 1, here] * (1.0 / log2e)
             )
 
-    live = (step_tokens(rows, steps) < length_ref[0]).astype(F32)
+    live = (step_tokens(rows, steps) < length).astype(F32)
     step_pre_grad = dg_ref[...] * live * sigmoid(pre_ref[...])
-    small_ref[...] = jnp.broadcast_to(jnp.sum(step_pre_grad, axis=0, keepdims=True), small_ref.shape)
     low = step_pre_grad.astype(BF16)
-    stepg_ref[...] = dot_tn(sel[:, :rank].astype(BF16), low)
     gather = gather_matrix(states)
-    selg_ref[...] = jnp.concatenate(
+    sel_part[...] = jnp.concatenate(
         [dot_nt(low, tw_ref[...]), dot(b_sum[...].astype(BF16), gather), dot(c_sum[...].astype(BF16), gather)],
         axis=1,
     )
-
-
-def backward_out_kernel(
-    selg_ref, act_ref, sw_ref, agrad_ref, skip_ref, pgrad_ref, ext_ref, cw_ref, cb_ref,
-    hid_ref, hidt_ref, wi_ref, wio_ref, wg_ref, wgo_ref, ggrad_ref,
-    ig_ref, part_ref, tpart_ref, selw_ref, cgrad_ref,
-    cig_ref,
-):
-    rows, width = act_ref.shape
-    steps = rows // spans
-    selg = selg_ref[...].astype(BF16)
-    selw_ref[...] = dot_tn(selg, act_ref[...])
-    active_grad = (
-        agrad_ref[...] + skip_ref[0:1, :].astype(F32) * pgrad_ref[...] + dot_nt(selg, sw_ref[...])
-    )
-    pre = conv_pre(ext_ref, cw_ref, cb_ref, rows, width)
-    conv_in = active_grad * slope_of(pre, sigmoid(pre))
+    first = pair_copy(0, sel_part, sel_row, row_peer())
+    advance_all(chunks[2:4])
+    bias_sum = jnp.sum(step_pre_grad, axis=0, keepdims=True)
+    small_store(0, dot_tn(sel[:, :rank].astype(BF16), low))
+    small_store(rank, dgrad_ref[...])
+    first.wait()
+    pair = sel_part[...] + sel_row[...]
+    sel_low[...] = pair.astype(BF16)
+    second = pair_copy(1, sel_low, sel_col, col_peer())
+    sel_part[...] = pair
+    order = to_tokens(rows, steps)
+    naturalg = dot(order, ggrad_ref[...]).astype(BF16)
+    gate_parts = [dot_nt(naturalg, wg[...]) for wg in (wg_ref, wgo_ref)]
+    pre = conv_pre(ext_ref, cw_ref, cb_ref, rows, inner)
+    slope = slope_of(pre, sigmoid(pre))
+    base_grad = agrad_ref[...] + skip_ref[0:1, :].astype(F32) * pgrad_ref[...]
+    advance_all(chunks[:2])
+    second.wait()
+    selg = (sel_part[...] + sel_col[...].astype(F32)).astype(BF16)
+    conv_in = (base_grad + dot_nt(selg, sw_ref[...])) * slope
     cig_ref[0:rows, :] = conv_in
-    last_span = lax.broadcasted_iota(jnp.int32, (spans, width), 0) == spans - 1
+    taps = cw_ref[...].astype(F32)
+    tails = [jnp.zeros((5, inner), F32)]
+    for i in range(3):
+        line = jnp.zeros((1, inner), F32)
+        for k in range(i + 1):
+            line = line + taps[k : k + 1, :] * conv_in[(i - k) * spans : (i - k) * spans + 1, :]
+        tails.append(line * (parents_ref[me] >= 0).astype(F32))
+    tail_low = jnp.concatenate(tails, axis=0).astype(BF16)
+    for h, wi in enumerate((wi_ref, wio_ref)):
+        tpart_ref[h] = dot_nt(tail_low, wi[...])
+    tail_first = pair_copy(2, tpart_ref, tail_row, row_peer())
+    last_span = lax.broadcasted_iota(jnp.int32, (spans, inner), 0) == spans - 1
     for j in range(3):
-        block = jnp.roll(conv_in[j * spans : (j + 1) * spans], -1, axis=0)
-        cig_ref[rows + j * spans : rows + (j + 1) * spans, :] = jnp.where(last_span, 0.0, block)
-    taps = cw_ref[...].astype(F32)
+        slab = jnp.roll(conv_in[j * spans : (j + 1) * spans], -1, axis=0)
+        cig_ref[rows + j * spans : rows + (j + 1) * spans, :] = jnp.where(last_span, 0.0, slab)
+    inner_grad = jnp.zeros((rows, inner), F32)
+    for k in range(4):
+        inner_grad = inner_grad + taps[k : k + 1, :] * cig_ref[(3 - k) * spans : (3 - k) * spans + rows, :]
+    inner_low = inner_grad.astype(BF16)
+    natural = dot(order, inner_low).astype(BF16)
+    hid_copies = []
+    for h, wi in ((1, wio_ref), (0, wi_ref)):
+        part_ref[h] = (dot_nt(natural, wi[...]) + gate_parts[h]).astype(BF16)
+        hid_copies.append(
+            pair_copy(3 + h, part_ref.at[h, pl.ds(other, half), :], hid_row.at[h], row_peer())
+        )
+    tail_first.wait()
+    tail_sum = tpart_ref[...] + tail_row[...]
+    tail_low_ref[...] = tail_sum[1]
+    tail_second = pair_copy(5, tail_low_ref, tail_col, col_peer())
+    hid_copies[0].wait()
+    hid_low[...] = (
+        part_ref[1, pl.ds(mine, half), :].astype(F32) + hid_row[1].astype(F32)
+    ).astype(BF16)
+    hid_second = pair_copy(6, hid_low, hid_col, col_peer())
+    for h in range(2):
+        store_split(igi_ref.at[h], dot_tn(hid_ref[h], inner_low) + dot_tn(hidt_ref[h], tail_low))
+    advance_all(chunks[4:])
+    tail_second.wait()
+    tail_own[...] = tail_sum[0] + tail_col[...]
+    tail_copies = to_all(tail_own, tails_ref, tail_send, tail_recv)
+    small_store(rank + states, dot_tn(selg, act_ref[...]))
     sums = [
         jnp.sum(conv_in * ext_ref[k * spans : k * spans + rows, :], axis=0, keepdims=True)
         for k in range(4)
     ]
     sums.append(jnp.sum(conv_in, axis=0, keepdims=True))
-    sums.append(jnp.zeros((3, width), F32))
-    cgrad_ref[...] = jnp.concatenate(sums, axis=0)
-    inner_grad = jnp.zeros((rows, width), F32)
-    for k in range(4):
-        inner_grad = inner_grad + taps[k : k + 1, :] * cig_ref[(3 - k) * spans : (3 - k) * spans + rows, :]
-    inner_low = inner_grad.astype(BF16)
-    tails = [jnp.zeros((5, width), F32)]
-    for i in range(3):
-        row = jnp.zeros((1, width), F32)
-        for k in range(i + 1):
-            row = row + taps[k : k + 1, :] * conv_in[(i - k) * spans : (i - k) * spans + 1, :]
-        tails.append(row)
-    tail_low = jnp.concatenate(tails, axis=0).astype(BF16)
-    order = to_tokens(rows, steps)
-    natural = dot(order, inner_low).astype(BF16)
-    naturalg = dot(order, ggrad_ref[...]).astype(BF16)
-    for h, (wi, wg) in enumerate(((wi_ref, wg_ref), (wio_ref, wgo_ref))):
-        part_ref[h] = (dot_nt(natural, wi[...]) + dot_nt(naturalg, wg[...])).astype(BF16)
-        tpart_ref[h] = dot_nt(tail_low, wi[...])
-        ig_ref[h] = (dot_tn(hid_ref[h], inner_low) + dot_tn(hidt_ref[h], tail_low)).astype(BF16)
-
-
-def seq_bits(count):
-    bits = []
-    mask = 1
-    while mask < count:
-        bits.append(mask)
-        mask *= 2
-    return bits
-
-
-def sum_scatter(value, count):
-    me = lax.axis_index("seq")
-    for mask in seq_bits(count):
-        half = value.shape[0] // 2
-        mine = (me // mask) % 2
-        keep = lax.dynamic_slice_in_dim(value, mine * half, half, 0)
-        give = lax.dynamic_slice_in_dim(value, (1 - mine) * half, half, 0)
-        got = lax.ppermute(give, "seq", [(i, i ^ mask) for i in range(count)])
-        value = (keep.astype(F32) + got.astype(F32)).astype(value.dtype)
-    return value
-
-
-def gather_back(value, count):
-    me = lax.axis_index("seq")
-    for mask in reversed(seq_bits(count)):
-        mine = (me // mask) % 2
-        got = lax.ppermute(value, "seq", [(i, i ^ mask) for i in range(count)])
-        low = jnp.where(mine == 0, value, got)
-        high = jnp.where(mine == 0, got, value)
-        value = jnp.concatenate([low, high], axis=0)
-    return value
+    sums.append(sgrad_ref[0:1, :])
+    sums.append(bias_sum)
+    sums.append(jnp.zeros((1, inner), F32))
+    small_store(rank + states + selects, jnp.concatenate(sums, axis=0))
+    for at in range((rank + states + selects + 8) // 8, small_ref.shape[0] * small_ref.shape[1] // 8):
+        a, b = place_of(at)
+        small_ref[a, b, :] = jnp.zeros((8, inner), F32)
+    small_chunk.next()
+    hid_copies[1].wait()
+    hidden = part_ref[0, pl.ds(mine, half), :].astype(F32) + hid_row[0].astype(F32)
+    advance_all(chunks[2:4])
+    advance_all(chunks[:2])
+
+    tok = tok_ref[...].astype(F32)
+    toko = toko_ref[...].astype(F32)
+    power = jnp.sum(tok * tok, axis=1, keepdims=True) + jnp.sum(toko * toko, axis=1, keepdims=True)
+    inv = lax.rsqrt(power / width + norm_epsilon)
+    normed = tok * inv
+    margin8 = tails_ref.shape[1]
+    positions = row * half + lax.broadcasted_iota(jnp.int32, (half, margin8), 0)
+    line_of = lax.broadcasted_iota(jnp.int32, (half, margin8), 1)
+    place = ((positions == length - margin8 + line_of) & (line_of >= margin8 - 3)).astype(F32)
+    for copy in tail_copies:
+        copy.wait()
+    own_tail = jnp.zeros(tails_ref.shape[1:], F32)
+    for child in range(count):
+        is_child = (parents_ref[child] == me).astype(F32)
+        own_tail = own_tail + is_child * tails_ref[child]
+    hidden = hidden + jnp.dot(place, own_tail, preferred_element_type=F32, precision=lax.Precision.HIGHEST)
+    hid_second.wait()
+    hidden = hidden + hid_col[...].astype(F32)
+    scaled = hidden * gain_ref[0:1, :].astype(F32)
+    mean = jnp.sum(scaled * normed, axis=1, keepdims=True)
+    mean_out[...] = lax.dot_general(
+        jnp.ones((8, lanes), F32), jnp.broadcast_to(mean / lanes, (half, lanes)), (((1,), (1,)), ((), ())),
+        preferred_element_type=F32, precision=lax.Precision.HIGHEST,
+    )
+    mean_copy = pair_copy(7, mean_out, mean_in, col_peer())
+    gain_out[...] = jnp.broadcast_to(jnp.sum(hidden * normed, axis=0, keepdims=True), gain_out.shape)
+    gain_copy = pair_copy(8, gain_out, gain_in, row_peer())
+    advance_all(chunks[4:] + [small_chunk])
+    gain_copy.wait()
+    gain_pair[...] = gain_out[...] + gain_in[...]
+    gain_copies = to_all(gain_pair, gains_ref, gain_send, gain_recv)
+    mean_copy.wait()
+    apart = lax.dot_general(
+        mean_in[...], jnp.full((8, lanes), 0.125, F32), (((0,), (0,)), ((), ())),
+        preferred_element_type=F32, precision=lax.Precision.HIGHEST,
+    )
+    mean = (mean + apart[:, 0:1]) / width
+    tg_ref[...] = cot_ref[...] + inv * (scaled - normed * mean)
+    advance_all(chunks[:4])
+    advance_all(chunks[4:] + [small_chunk])
+    for copy in gain_copies:
+        copy.wait()
+    gain_total = gains_ref[0]
+    for i in range(1, count):
+        gain_total = gain_total + gains_ref[i]
+    gg_ref[...] = gain_total
+    run_out(chunks + [small_chunk])
+
+
+def backward_call(args, count, rows, width, inner, states, rank, selects):
+    half = width // 2
+    tile = rows // 2
+    block_rows = half // count
+    levels = len(seq_bits(count))
+    small = small_rows(count, rank, states, selects)
+    f32, bf16 = F32, BF16
+    vm = pltpu.VMEM
+    scratch = [
+        vm((count, states, inner), bf16), vm((count, states, inner), f32),
+        vm((rows, states * lanes), f32), vm((states, spans, inner), f32),
+        vm((states, rows, lanes), f32), vm((states, rows + spans, lanes), f32),
+        vm((rows, states * lanes), f32), vm((rows, states * lanes), f32),
+        vm((rows, inner), f32), vm((states, inner), f32),
+        vm((rows, selects), f32), vm((rows, selects), f32), vm((rows, selects), bf16), vm((rows, selects), bf16),
+        vm((rows + 3 * spans, inner), f32), vm((2, rows, half), bf16), vm((2, 8, half), f32),
+        vm((2, tile, half), bf16), vm((2, 8, half), f32), vm((tile, half), bf16), vm((tile, half), bf16),
+        vm((8, half), f32), vm((8, half), f32), vm((8, half), f32), vm((count, 8, half), f32),
+        vm((8, tile), f32), vm((8, tile), f32), vm((8, half), f32), vm((8, half), f32), vm((8, half), f32),
+        vm((count, 8, half), f32),
+        vm((2, count, block_rows, inner), bf16), vm((count, small, inner), f32),
+        vm((6, count, block_rows, inner), bf16), vm((count, small, inner), f32),
+    ]
+    scratch += [vm((6, count >> (k + 1), block_rows, inner), bf16) for k in range(levels)]
+    scratch += [vm((count >> (k + 1), small, inner), f32) for k in range(levels)]
+    dma = pltpu.SemaphoreType.DMA
+    scratch += [dma((7, 2 * levels + 1))] * 2 + [dma((9,))] * 2 + [dma((count,))] * 6
+    return run_kernel(
+        functools.partial(backward_kernel, width=width),
+        (
+            struct((2 * inner, half), f32),
+            struct((half * 4 * inner // lanes, lanes), f32),
+            struct((tile, half), f32),
+            struct((8, half), f32),
+            struct((rank, inner), f32),
+            struct((states, inner), f32),
+            struct((selects, inner), f32),
+            struct((8, inner), f32),
+        ),
+        args,
+        "backward",
+        scratch=scratch,
+        flops=16e9,
+        collective=4,
+        grant=vmem_most,
+    )
 
 
 def on_device(
@@ -994,9 +1208,9 @@
     out_part, gate_grad, ig_gate, pre_grad, skip_part, back, flow = run_kernel(
         backward_in_kernel,
         (
-            struct((2, inner, half), BF16),
+            struct((2, count, inner // count, half), BF16),
             struct((rows, inner), BF16),
-            struct((2, half, inner), BF16),
+            struct((2, count, half // count, inner), BF16),
             struct((rows, inner), F32),
             struct((8, inner), F32),
             struct((states, spans, inner), F32),
@@ -1010,96 +1224,16 @@
         ],
         flops=4e9,
     )
-    flows = seq_gather(flow, count, 4, "flow_gather")
-    selg_part, active_grad, step_bias_part, step_part, decay_part = run_kernel(
-        backward_scan_kernel,
+    out_grad, in_both, tokens_grad, gain_grad, step_grad, decay_grad, select_grad, small = backward_call(
         (
-            struct((rows, selects), F32),
-            struct((rows, inner), F32),
-            struct((8, inner), F32),
-            struct((rank, inner), F32),
-            struct((states, inner), F32),
+            table, flow, parents, lengths, decay_log, starts, back, cum, delta, act, sel, pre_grad,
+            step_pre, step_weight, select_weight, skip, ext, conv_weight, conv_b, hid, hid_tail,
+            wi, wio, wg, wgo, gate_grad, tok_tile, toko_tile, gain, cot_tile, out_part, ig_gate, skip_part,
         ),
-        (
-            table, flows, parents, me1, my_len, decay_log, starts, back, cum, delta, act, sel,
-            pre_grad, step_pre, step_weight,
-        ),
-        "backward_scan",
-        scratch=[
-            pltpu.VMEM((count, states, inner), F32),
-            pltpu.VMEM((rows, inner), F32),
-            pltpu.VMEM((rows, states * lanes), F32),
-            pltpu.VMEM((rows, states * lanes), F32),
-            pltpu.VMEM((states, spans, inner), F32),
-            pltpu.VMEM((states, rows, lanes), F32),
-            pltpu.VMEM((states, rows + spans, lanes), F32),
-            pltpu.VMEM((rows, states * lanes), F32),
-            pltpu.VMEM((rows, states * lanes), F32),
-            pltpu.VMEM((rows, inner), F32),
-        ],
-        flops=8e9,
-    )
-    selg = quad_sum(selg_part, 7, "select_grad_sum")
-    ig_inner, hid_part, tail_part, select_part, conv_part = run_kernel(
-        backward_out_kernel,
-        (
-            struct((2, half, inner), BF16),
-            struct((2, rows, half), BF16),
-            struct((2, 8, half), F32),
-            struct((selects, inner), F32),
-            struct((8, inner), F32),
-        ),
-        (
-            selg, act, select_weight, active_grad, skip, pre_grad, ext, conv_weight, conv_b,
-            hid, hid_tail, wi, wio, wg, wgo, gate_grad,
-        ),
-        "backward_out",
-        scratch=[pltpu.VMEM((rows + 3 * spans, inner), F32)],
-        flops=6e9,
-    )
-    hid_tile, tail_tile = hidden_exchange(hid_part, tail_part)
-    tail_table = seq_gather(
-        jnp.concatenate([tail_tile[5:8], tail_tile[:5]], axis=0), count, 8, "tail_gather"
-    )
-    tokens_grad, gain_part = finish_exchange(
-        hid_tile, tail_table, tok_tile, toko_tile, gain, cot_tile, parents, lengths, width
-    )
-
-    def flat(pair):
-        return pair.reshape(-1, pair.shape[-1])
-
-    small = jnp.concatenate(
-        [
-            step_part, decay_part, select_part, conv_part[:5], skip_part[:1], step_bias_part[:1],
-            gain_part[:1],
-        ],
-        axis=0,
-    )
-    pad = -small.shape[0] % (8 * count)
-    small = jnp.pad(small, ((0, pad), (0, 0)))
-    first = jnp.concatenate([flat(out_part), flat(ig_gate)], axis=0)
-    first = gather_back(sum_scatter(first, count), count)
-    second = gather_back(sum_scatter(flat(ig_inner), count), count)
-    small = gather_back(sum_scatter(small, count), count)
-    og = first[: 2 * inner].reshape(2, inner, half)
-    igg = first[2 * inner :].reshape(2, half, inner)
-    igi = second.reshape(2, half, inner)
-    from_pair = lax.ppermute(jnp.stack([og[1], igg[1], igi[1]]), "col", swap)
-    left = col == 0
-
-    def beside(own, other, axis):
-        return jnp.concatenate(
-            [jnp.where(left, own, other), jnp.where(left, other, own)], axis=axis
-        ).astype(F32)
-
-    out_grad = beside(og[0], from_pair[0], 0)
-    in_grad = jnp.stack([beside(igi[0], from_pair[2], 1), beside(igg[0], from_pair[1], 1)], axis=1)
-    at = 0
-    pieces = []
-    for size in (rank, states, selects, 4, 1, 1, 1, 1):
-        pieces.append(small[at : at + size])
-        at += size
-    step_grad, decay_grad, select_grad, conv_grad, conv_bias_grad, skip_grad, step_bias_grad, gain_grad = pieces
+        count, rows, width, inner, states, rank, selects,
+    )
+    in_grad = in_both.reshape(half, -1, 2, lanes).transpose(0, 2, 1, 3).reshape(half, 2, -1)
+    conv_grad, conv_bias_grad, skip_grad, step_bias_grad = small[:4], small[4:5], small[5:6], small[6:7]
     return (
         output,
         tokens_grad,

time: 382 us -> 276 us (0.72)
  waiting for transfers between devices: 97 us -> 0.01 us
  Pallas kernels: 204 us -> 233 us
  other arithmetic: 18.1 us -> 0.63 us
  starting transfers between devices: 17.9 us -> 2.09 us
  local copies, waits for them, and re-layouts: 40.7 us -> 36.4 us
    ppermute x19 -> x0, waiting for transfers between devices: 97 us -> none  [the longest x9 51.2 us: gather_back(): got = lax.ppermute(value, 'seq', [(i, i ^ mask) for i in range(count)])]
    pallas_call x15 -> x9, Pallas kernels: 204 us -> 233 us  [run_kernel(): pl.pallas_call(kernel, out_shape=outs, in_specs=[smem_spec() if a.dtype =...]
    ppermute x19 -> x0, starting transfers between devices: 15.8 us -> none  [the longest x9 10.7 us: sum_scatter(): got = lax.ppermute(give, 'seq', [(i, i ^ mask) for i in range(count)])]
    convert_element_type x7 -> x0, other arithmetic: 6.12 us -> none  [the longest x6 4.52 us: sum_scatter(): value = (keep.astype(F32) + got.astype(F32)).astype(value.dtype)]
    unnamed x44 -> x38, local copies, waits for them, and re-layouts: 8.25 us -> 13.4 us
    concatenate x8 -> x0, other arithmetic: 4.33 us -> none  [the longest x1 1.98 us: on_device(): first = jnp.concatenate([flat(out_part), flat(ig_gate)], axis=0)]
    select_n x9 -> x0, other arithmetic: 3.98 us -> none  [the longest x8 2.04 us: gather_back(): low = jnp.where(mine == 0, value, got)]
  transfers between devices with their start and end apart: 21 -> 2, of which waited for: 11 -> 0; matrix products, arithmetic and copies ran while one was open for 8% -> 3% of each run, Pallas kernels for 35% -> 14%
where the time goes in v2:
time: 276 us; the launch traced here: 275 us
  Pallas kernels  233 us (84%)
  local copies, waits for them, and re-layouts  36.4 us (13%)
  between operations  2.78 us (1%)
    pallas_call x9, Pallas kernels, run_kernel(): pl.pallas_call(kernel, out_shape=outs, in_specs=[smem_spec() if a.dtype =...  233 us
    unnamed x38, local copies, waits for them, and re-layouts  13.4 us
  transfers between devices with their start and end apart: 2, of which 0 were waited for; matrix products, arithmetic and copies ran while one was open for 3% of the time, Pallas kernels for 14%

profile of v2, /device:TPU:0, one launch (start us, length us, event | category | flops | bytes accessed | tf_op | source)
XLA Modules:
  0.0 274.8 jit_solution(15131378439682126645)
XLA Ops:
  0.7 1.2 dynamic_slice.47.ints_ref
  3.2 1.4 constant_dynamic-slice_fusion.9.tail_ref
  4.6 2.9 %constant_dynamic-slice_fusion.3 = (bf16[512,512]{1,0:T(8,128)(2,1)}, bf16[512,512]{1,0:T(8,128)(2,1)S(1)}, bf16[512,512]{1,0:T(8,128)(2,1)}, bf16[512,512]{1,0:T(8,128)(2,1)}) fusion(bf16[1024,512]{1,0:T(8,128)(2,1)} %param.26, s32[]{:T(128)S(6)} %select_n.31, s32[]{:T(128)S(6)} %select_n.32, bf16[512,1024]{1,0:T(8,128)(2,1)} %param.15), kind=kLoop, calls=%fused_computation.7 | loop fusion | bytes 4194312 | tf_op jit(solution)/shard_map/dynamic_slice | solution.py:1124
  7.4 5.1 %constant_dynamic-slice_fusion.5 = (bf16[512,1,512]{2,1,0:T(2,128)(2,1)S(1)}, bf16[512,1,512]{2,1,0:T(2,128)(2,1)S(1)}, bf16[512,1,512]{2,1,0:T(2,128)(2,1)S(1)}, bf16[512,1,512]{2,1,0:T(2,128)(2,1)S(1)}) fusion(bf16[512,2,1024]{2,1,0:T(2,128)(2,1)S(1)} %copy-done, s32[]{:T(128)S(6)} %add.42, s32[]{:T(128)S(6)} %select_n.31, s32[]{:T(128)S(6)} %select_n.32), kind=kLoop, calls=%fused_computation.9 | loop fusion | bytes 4194316 | tf_op jit(solution)/shard_map/slice | solution.py:1135
  12.6 1.1 copy_bitcast_fusion.1
  13.7 0.6 broadcast_in_dim.10.gain_ref
  14.3 21.4 %entry_exchange.1 = (bf16[8,8,1024]{2,1,0:T(8,128)(2,1)}, bf16[512,512]{1,0:T(8,128)(2,1)}, bf16[8,512]{1,0:T(8,128)(2,1)}) custom-call(bf16[8,1024]{1,0:T(8,128)(2,1)} %constant_dynamic-slice_fusion.9.tail_ref, bf16[512,512]{1,0:T(8,128)(2,1)} %get-tuple-element.110.wi_ref, bf16[8,512]{1,0:T(8,128)(2,1)} %broadcast_in_dim.10.gain_ref), custom_call_target="tpu_custom_call" | custom-call | bytes 548864 | tf_op jit(solution)/shard_map/entry_exchange/pallas_call | solution.py:100
  35.7 0.6 collective-permute-start
  36.3 1.5 collective-permute-start.1
  37.8 1.3 copy_bitcast_fusion
  39.1 0.7 constant_dynamic-slice_fusion.6
  39.8 0.6 reduce_sum.9
  42.2 0.8 copy.29.sw_ref
  43.6 5.6 %forward_in.1 = (bf16[2,512,512]{2,1,0:T(8,128)(2,1)}, bf16[2,8,512]{2,1,0:T(8,128)(2,1)}, f32[536,512]{1,0:T(8,128)}, bf16[512,512]{1,0:T(8,128)(2,1)}, f32[512,96]{1,0:T(8,128)}) custom-call(bf16[512,512]{1,0:T(8,128)(2,1)} %get-tuple-element.105.tok_ref, bf16[512,512]{1,0:T(8,128)(2,1)} %get-tuple-element.106.toko_ref, ...), custom_call_target="tpu_custom_call" | custom-call | flops 2000000000 | bytes 2355204 | tf_op jit(solution)/shard_map/forward_in/pallas_call | solution.py:100
  49.2 14.2 %select_sum.1.sel_ref = f32[512,96]{1,0:T(8,128)} custom-call(f32[512,96]{1,0:T(8,128)} %get-tuple-element.55.x_ref), custom_call_target="tpu_custom_call" | custom-call | bytes 196608 | tf_op jit(solution)/shard_map/select_sum/pallas_call | solution.py:100
  64.0 9.9 %forward_ends.1 = (f32[512,512]{1,0:T(8,128)}, f32[512,512]{1,0:T(8,128)}, f32[16,8,512]{2,1,0:T(8,128)}, f32[8,512]{1,0:T(8,128)}, bf16[24,512]{1,0:T(8,128)(2,1)}) custom-call(f32[512,96]{1,0:T(8,128)} %select_sum.1.sel_ref, bf16[64,512]{1,0:T(8,128)(2,1)} %tw_ref.3, bf16[8,512]{1,0:T(8,128)(2,1)} %broadcast_in_dim.12.tb_ref, f32[16,512]{1,0:T(8,128)} %dl_ref.7, ...), custom_call_target="tpu_custom_call" | custom-call | flops 2000000000 | bytes 827396 | tf_op jit(solution)/shard_map/forward_ends/pallas_call | solution.py:100
  73.9 8.2 %state_gather.1.table_ref = bf16[8,24,512]{2,1,0:T(8,128)(2,1)} custom-call(bf16[24,512]{1,0:T(8,128)(2,1)} %get-tuple-element.57.x_ref), custom_call_target="tpu_custom_call" | custom-call | bytes 24576 | tf_op jit(solution)/shard_map/state_gather/pallas_call | solution.py:100
  82.2 1.2 fusion
  84.0 13.4 %forward_out.1 = (f32[16,8,512]{2,1,0:T(8,128)}, f32[512,512]{1,0:T(8,128)}, f32[512,512]{1,0:T(8,128)}, bf16[512,512]{1,0:T(8,128)(2,1)}, bf16[2,512,512]{2,1,0:T(8,128)(2,1)}) custom-call(bf16[8,24,512]{2,1,0:T(8,128)(2,1)} %state_gather.1.table_ref, s32[8]{0:T(128)} %parents_ref.3, s32[1]{0:T(128)} %bitcast.5.me_ref, f32[16,512]{1,0:T(8,128)} %dl_ref.7, ...), custom_call_target="tpu_custom_call" | custom-call | flops 4000000000 | bytes 5431332 | tf_op jit(solution)/shard_map/forward_out/pallas_call | solution.py:100
  98.0 21.5 %middle_exchange.1 = (bf16[256,512]{1,0:T(8,128)(2,1)}, f32[256,512]{1,0:T(8,128)}, bf16[2,512,512]{2,1,0:T(8,128)(2,1)}) custom-call(bf16[2,512,512]{2,1,0:T(8,128)(2,1)} %get-tuple-element.64.part_ref, bf16[256,512]{1,0:T(8,128)(2,1)} %get-tuple-element.95.tok_ref, bf16[256,512]{1,0:T(8,128)(2,1)} %get-tuple-element.111.teach_ref, ...), custom_call_target="tpu_custom_call" | custom-call | bytes 1576964 | tf_op jit(solution)/shard_map/middle_exchange/pallas_call | solution.py:100
  119.6 13.0 %backward_in.1 = (bf16[2,8,64,512]{3,2,1,0:T(8,128)(2,1)}, bf16[512,512]{1,0:T(8,128)(2,1)}, bf16[2,8,64,512]{3,2,1,0:T(8,128)(2,1)}, f32[512,512]{1,0:T(8,128)}...) custom-call(bf16[2,512,512]{2,1,0:T(8,128)(2,1)} %get-tuple-element.66.cot_ref, ...), custom_call_target="tpu_custom_call" | custom-call | flops 4000000000 | bytes 7593984 | tf_op jit(solution)/shard_map/backward_in/pallas_call | solution.py:100
  132.5 125.6 %backward.1 = (f32[1024,512]{1,0:T(8,128)}, f32[8192,128]{1,0:T(8,128)}, f32[256,512]{1,0:T(8,128)}, f32[8,512]{1,0:T(8,128)}, f32[64,512]{1,0:T(8,128)}, /*inde...) custom-call(bf16[8,24,512]{2,1,0:T(8,128)(2,1)} %state_gather.1.table_ref, ...), custom_call_target="tpu_custom_call" | custom-call | flops 16000000000 | bytes 12791872 | tf_op jit(solution)/shard_map/backward/pallas_call | solution.py:100
  258.2 1.4 fusion.1
  259.6 1.3 slice.32
  260.9 1.3 slice.31
  262.2 1.7 copy.49
  263.9 1.9 copy.50
  265.8 5.8 %copy.51 = f32[512,2,1024]{2,1,0:T(2,128)} copy(f32[512,2,1024]{2,1,0:T(2,128)} %bitcast.21) | data formatting | bytes 8388608
  271.6 0.7 copy.52
  272.2 0.7 copy.53
  272.9 0.6 copy.54
  273.5 1.3 copy.55
  (38 shorter events, 3.6 us)
Async XLA Ops:
  4.6 2.9 %copy-start = (bf16[512,2,1024]{2,1,0:T(2,128)(2,1)S(1)}, bf16[512,2,1024]{2,1,0:T(2,128)(2,1)}, u32[]{:S(2)}) copy-start(bf16[512,2,1024]{2,1,0:T(2,128)(2,1)} %param.18) | copy-start | bytes 6291460
  12.6 1.1 copy-start.9
  13.7 26.1 %copy-start.13 = (s32[8]{0:T(128)S(1)}, s32[8]{0:T(128)}, u32[]{:S(2)}) copy-start(s32[8]{0:T(128)} %param.29) | copy-start | bytes 100
  13.7 27.3 %copy-start.14 = (s32[8]{0:T(128)S(1)}, s32[8]{0:T(128)}, u32[]{:S(2)}) copy-start(s32[8]{0:T(128)} %parents_ref.3) | copy-start | bytes 100
  13.7 28.6 %copy-start.7 = (bf16[512,96]{0,1:T(8,128)(2,1)S(1)}, bf16[512,96]{0,1:T(8,128)(2,1)}, u32[]{:S(2)}) copy-start(bf16[512,96]{0,1:T(8,128)(2,1)} %param.21) | copy-start | bytes 294916
  14.3 28.7 %copy-start.10 = (bf16[512]{0:T(512)(128)(2,1)S(1)}, bf16[512]{0:T(512)(128)(2,1)}, u32[]{:S(2)}) copy-start(bf16[512]{0:T(512)(128)(2,1)} %param.20) | copy-start | bytes 3076
  35.7 3.4 %copy-start.5 = (bf16[8,8,1024]{2,1,0:T(8,128)(2,1)S(1)}, bf16[8,8,1024]{2,1,0:T(8,128)(2,1)}, u32[]{:S(2)}) copy-start(bf16[8,8,1024]{2,1,0:T(8,128)(2,1)} %get-tuple-element.51) | copy-start | bytes 393220
  35.7 47.7 %collective-permute-start = (bf16[512,512]{1,0:T(8,128)(2,1)S(1)}, bf16[512,512]{1,0:T(8,128)(2,1)}, u32[]{:S(2)}, u32[]{:S(2)}) collective-permute-start(bf16[512,512]{1,0:T(8,128)(2,1)S(1)} %get-tuple-element.62), channel_id=1, source_target_pairs={{0,1},{1,0},{2,3},{3,2},{4,5},{5,4},{6,7},{7,6},{8,9},{9,8},{10,11... | collective-permute-start | bytes 1572872 | tf_op jit(solution)/shard_map/ppermute | solution.py:1145
  36.3 47.1 %collective-permute-start.1 = (bf16[512,512]{1,0:T(8,128)(2,1)S(1)}, bf16[512,512]{1,0:T(8,128)(2,1)}, u32[]{:S(2)}, u32[]{:S(2)}) collective-permute-start(bf16[512,512]{1,0:T(8,128)(2,1)S(1)} %get-tuple-element.63), channel_id=1, source_target_pairs={{0,1},{1,0},{2,3},{3,2},{4,5},{5,4},{6,7},{7,6},{8,9},{9,8},{10,11... | collective-permute-start | bytes 1572872 | tf_op jit(solution)/shard_map/ppermute | solution.py:1146
  43.6 19.8 %copy-start.11 = (bf16[512]{0:T(512)(128)(2,1)S(1)}, bf16[512]{0:T(512)(128)(2,1)}, u32[]{:S(2)}) copy-start(bf16[512]{0:T(512)(128)(2,1)} %param.23) | copy-start | bytes 3076
  64.0 18.2 %copy-start.1 = (bf16[512,1024]{1,0:T(8,128)(2,1)S(1)}, bf16[512,1024]{1,0:T(8,128)(2,1)}, u32[]{:S(2)}) copy-start(bf16[512,1024]{1,0:T(8,128)(2,1)} %param.15) | copy-start | bytes 3145732
  64.0 18.2 %copy-start.6 = (bf16[512,512]{1,0:T(8,128)(2,1)S(1)}, bf16[512,512]{1,0:T(8,128)(2,1)}, u32[]{:S(2)}) copy-start(bf16[512,512]{1,0:T(8,128)(2,1)} %param.16) | copy-start | bytes 1572868
  64.0 19.4 %copy-start.12 = (bf16[512]{0:T(512)(128)(2,1)S(1)}, bf16[512]{0:T(512)(128)(2,1)}, u32[]{:S(2)}) copy-start(bf16[512]{0:T(512)(128)(2,1)} %param.25) | copy-start | bytes 3076
  265.8 5.8 %copy-start.3 = (f32[96,512]{1,0:T(8,128)S(1)}, f32[96,512]{1,0:T(8,128)}, u32[]{:S(2)}) copy-start(f32[96,512]{1,0:T(8,128)} %get-tuple-element.86) | copy-start | bytes 589828
  265.8 6.5 %copy-start.4 = (f32[64,512]{1,0:T(8,128)S(1)}, f32[64,512]{1,0:T(8,128)}, u32[]{:S(2)}) copy-start(f32[64,512]{1,0:T(8,128)} %get-tuple-element.131) | copy-start | bytes 393220
  265.8 7.1 %copy-start.8 = (f32[16,512]{1,0:T(8,128)S(1)}, f32[16,512]{1,0:T(8,128)}, u32[]{:S(2)}) copy-start(f32[16,512]{1,0:T(8,128)} %get-tuple-element.133) | copy-start | bytes 98308
  265.8 7.8 %copy-start.2 = (f32[1024,512]{1,0:T(8,128)S(1)}, f32[1024,512]{1,0:T(8,128)}, u32[]{:S(2)}) copy-start(f32[1024,512]{1,0:T(8,128)} %get-tuple-element.135) | copy-start | bytes 6291460

commit v3 on v2

--- a/solution.py
+++ b/solution.py
@@ -16,6 +16,7 @@
 log2e = 1.4426950408889634
 vmem_bytes = 60 * 1024 * 1024
 vmem_most = 67043328
+chunk_plan = (False, True, False, True, False, False)
 
 
 def vmem_spec():
@@ -578,11 +579,40 @@
     return bits
 
 
-def mask_order(count, swapped):
+def stages_of(count, first_pair):
     bits = seq_bits(count)
-    if swapped and len(bits) > 1:
-        bits = [bits[1], bits[0]] + bits[2:]
-    return bits
+    if len(bits) < 3:
+        return [(mask,) for mask in bits]
+    if first_pair:
+        return [(bits[1],), (bits[0],)] + [(mask,) for mask in bits[2:]]
+    return [(bits[0],), (bits[1], bits[2])] + [(mask,) for mask in bits[3:]]
+
+
+def stage_sizes(stages, count, crossed):
+    sizes, copies = [], 0
+    for i, masks in enumerate(stages):
+        radix = 2 ** len(masks)
+        count //= radix
+        got = radix if crossed and i == len(stages) - 1 else radix - 1
+        sizes.append((got, count))
+        copies += got + radix - 1
+    return sizes, copies
+
+
+def bit_of(me, mask):
+    return (me // mask) % 2
+
+
+def toward(me, masks, pick):
+    device, part = me, 0
+    for k, mask in enumerate(masks):
+        bit = bit_of(me, mask)
+        weight = 2 ** (len(masks) - 1 - k)
+        if (pick // weight) % 2:
+            device = device + mask - 2 * mask * bit
+            bit = 1 - bit
+        part = part + weight * bit
+    return device, part
 
 
 def widen(values):
@@ -590,84 +620,90 @@
 
 
 class Chunk:
-    def __init__(self, source, total, stages, send, recv, masks, crossed, emit):
-        self.source, self.total, self.stages = source, total, stages
-        self.send, self.recv, self.masks, self.crossed, self.emit = send, recv, masks, crossed, emit
+    def __init__(self, source, total, landings, send, recv, stages, crossed, emit):
+        self.source, self.total, self.landings = source, total, landings
+        self.send, self.recv, self.stages, self.crossed, self.emit = send, recv, stages, crossed, emit
         self.count = source.shape[0]
         self.me = lax.axis_index("seq")
         self.copies = []
+        self.flying = []
         self.at = 0
-        self.levels = len(masks)
-
-    def bit(self, level):
-        return (self.me // self.masks[level]) % 2
-
-    def peer(self, level):
-        mask = self.masks[level]
-        return {"seq": self.me + mask - 2 * mask * self.bit(level)}
+        self.levels = len(stages)
+        self.sizes = stage_sizes(stages, self.count, crossed)[0]
 
     def start(self, src, dst, peer):
         at = len(self.copies)
         copy = remote(src, dst, self.send.at[at], self.recv.at[at], peer)
         copy.start()
         self.copies.append(copy)
+        self.flying.append(copy)
+
+    def land(self):
+        for copy in self.flying:
+            copy.wait_recv()
+        self.flying = []
 
     def place(self, level):
         start = 0
         for j in range(level + 1):
-            start = start + self.bit(j) * (self.count >> (j + 1))
+            start = start + toward(self.me, self.stages[j], 0)[1] * self.sizes[j][1]
         return start
 
-    def held(self, level):
-        return self.source if level == 0 else self.stages[level - 1]
-
-    def halve(self, level):
-        size = self.count >> (level + 1)
-        away = self.held(level).at[pl.ds((1 - self.bit(level)) * size, size)]
-        self.start(away, self.stages[level], self.peer(level))
+    def crossing(self, level):
+        return self.crossed and level == self.levels - 1
+
+    def scatter(self, level):
+        held = self.source if level == 0 else self.landings[level - 1].at[0]
+        masks, (_, size) = self.stages[level], self.sizes[level]
+        for pick in range(0 if self.crossing(level) else 1, 2 ** len(masks)):
+            device, part = toward(self.me, masks, pick)
+            peer = {"seq": device}
+            if self.crossing(level):
+                peer["col"] = 1 - lax.axis_index("col")
+            slot = pick if self.crossing(level) else pick - 1
+            self.start(held.at[pl.ds(part * size, size)], self.landings[level].at[slot], peer)
 
     def add(self, level):
-        size = self.count >> (level + 1)
-        kept = self.held(level)[pl.ds(self.bit(level) * size, size)]
-        got = self.stages[level]
-        got[...] = (widen(kept) + widen(got[...])).astype(got.dtype)
-
-    def double(self, level):
-        size = self.count >> (level + 1)
+        held = self.source if level == 0 else self.landings[level - 1].at[0]
+        masks, (got, size) = self.stages[level], self.sizes[level]
+        landing = self.landings[level]
+        if self.crossing(level):
+            total = widen(landing[0])
+        else:
+            own = toward(self.me, masks, 0)[1]
+            total = widen(held[pl.ds(own * size, size)]) + widen(landing[0])
+        for slot in range(1, got):
+            total = total + widen(landing[slot])
+        return total.astype(landing.dtype)
+
+    def gather(self, level):
+        size = self.sizes[level][1]
         region = self.total.at[pl.ds(self.place(level), size)]
-        self.start(region, region, self.peer(level))
-
-    def step(self, index):
-        last = self.levels
-        if index > 0:
-            self.copies[index - 1].wait_recv()
-        if index < last:
-            if index > 0:
-                self.add(index - 1)
-            self.halve(index)
+        masks = self.stages[level]
+        for pick in range(1, 2 ** len(masks)):
+            self.start(region, region, {"seq": toward(self.me, masks, pick)[0]})
+
+    def done(self):
+        return self.at > 2 * self.levels
+
+    def next(self):
+        if self.done():
             return
-        at = index - last
-        if at == 0:
-            self.add(last - 1)
-            piece = self.stages[last - 1]
-            home = self.total.at[pl.ds(self.place(last - 1), 1)]
-            if self.crossed:
-                self.start(piece, home, col_peer())
-                return
-            home[...] = piece[...]
-        level = last - 1 - (at - int(self.crossed))
+        self.land()
+        at, last = self.at, self.levels
+        self.at += 1
+        if at < last:
+            if at > 0:
+                self.landings[at - 1][0] = self.add(at - 1)
+            self.scatter(at)
+            return
+        if at == last:
+            self.total[pl.ds(self.place(last - 1), 1)] = self.add(last - 1)
+        level = 2 * last - 1 - at
         if level >= 0:
-            self.double(level)
+            self.gather(level)
         else:
             self.emit(self.total)
-
-    def done(self):
-        return self.at > 2 * self.levels + int(self.crossed)
-
-    def next(self):
-        if not self.done():
-            self.step(self.at)
-            self.at += 1
 
     def finish(self):
         for copy in self.copies:
@@ -712,9 +748,12 @@
     width,
 ):
     count = table_ref.shape[0]
-    levels = len(seq_bits(count))
-    halves, smalls = rest[:levels], rest[levels : 2 * levels]
-    send, recv, pair_send, pair_recv, flow_send, flow_recv, tail_send, tail_recv, gain_send, gain_recv = rest[2 * levels :]
+    landings = []
+    for paired in chunk_plan + (False,):
+        size = len(stages_of(count, paired))
+        landings.append(rest[:size])
+        rest = rest[size:]
+    send, recv, pair_send, pair_recv, flow_send, flow_recv, tail_send, tail_recv, gain_send, gain_recv = rest
     rows, inner = act_ref.shape
     half = rows // 2
     steps = rows // spans
@@ -728,7 +767,15 @@
     other = pl.multiple_of((1 - row) * half, half)
     length = lengths_ref[me]
     peers = [{"seq": lax.rem(me + j, count)} for j in range(1, count)]
-    barrier_with([row_peer(), col_peer()] + peers)
+    across = sorted(
+        {(masks, pick) for masks in (stages_of(count, p)[-1] for p in chunk_plan) for pick in range(1, 2 ** len(masks))}
+    )
+    flips = sorted({sum(m for k, m in enumerate(masks) if (pick >> (len(masks) - 1 - k)) % 2) for masks, pick in across})
+    crossers = []
+    for flip in flips:
+        masks = tuple(m for m in seq_bits(count) if (flip // m) % 2)
+        crossers.append({"seq": toward(me, masks, 2 ** len(masks) - 1)[0], "col": 1 - col})
+    barrier_with([row_peer(), col_peer()] + peers + crossers)
 
     def pair_copy(at, src, dst, peer):
         copy = remote(src, dst, pair_send.at[at], pair_recv.at[at], peer)
@@ -787,23 +834,23 @@
         smallg_out[...] = read(rank + states + selects, 8)
 
     plan = [
-        (og_ref, 0, rows_out(col), False),
-        (og_ref, 1, rows_out(1 - col), True),
-        (igg_ref, 0, lanes_out(1, col), False),
-        (igg_ref, 1, lanes_out(1, 1 - col), False),
-        (igi_ref, 0, lanes_out(0, col), False),
-        (igi_ref, 1, lanes_out(0, 1 - col), True),
+        (og_ref, 0, rows_out(col)),
+        (og_ref, 1, rows_out(1 - col)),
+        (igg_ref, 0, lanes_out(1, col)),
+        (igg_ref, 1, lanes_out(1, 1 - col)),
+        (igi_ref, 0, lanes_out(0, col)),
+        (igi_ref, 1, lanes_out(0, 1 - col)),
     ]
     chunks = [
         Chunk(
-            source.at[h], totals.at[i], [s.at[i] for s in halves], send.at[i], recv.at[i],
-            mask_order(count, swapped), h == 1, emit,
+            source.at[h], totals.at[i], landings[i], send.at[i], recv.at[i],
+            stages_of(count, chunk_plan[i]), h == 1, emit,
         )
-        for i, (source, h, emit, swapped) in enumerate(plan)
+        for i, (source, h, emit) in enumerate(plan)
     ]
     small_chunk = Chunk(
-        small_ref, small_total, smalls, send.at[len(plan)], recv.at[len(plan)],
-        mask_order(count, False), False, small_emit,
+        small_ref, small_total, landings[-1], send.at[len(plan)], recv.at[len(plan)],
+        stages_of(count, False), False, small_emit,
     )
 
     drive = og_out.at[0:rows]
@@ -812,8 +859,9 @@
     def b_at(n, step):
         return ig_out[pl.ds(pl.multiple_of(n * rows + step * spans, spans), spans), :]
 
+    c0, c1, c2, c3, c4, c5 = chunks
     flow_copies = to_all(flow_ref, flows_ref, flow_send, flow_recv)
-    advance_all(chunks[:4])
+    advance_all((c0, c1, c2, c3))
     decay_rows(dl_ref, rate_ref, log2e)
     rate = -jnp.exp(dl_ref[...]) * log2e
     sel = sel_ref[...]
@@ -837,7 +885,9 @@
         return carry
 
     groups = inner // lanes
-    pumps = {(0, 1): (), (1, 0): chunks[:2], (1, 1): chunks[2:4], (2, 0): chunks[:2], (2, 1): (), (3, 0): chunks[2:4], (3, 1): chunks[:2]}
+    pumps = {
+        (1, 0): (c0, c1), (2, 0): (c2, c3), (2, 1): (c1,), (3, 0): (c0, c3), (3, 1): (c1,),
+    }
     for group in range(groups):
         here = slice(group * lanes, (group + 1) * lanes)
 
@@ -920,7 +970,7 @@
         axis=1,
     )
     first = pair_copy(0, sel_part, sel_row, row_peer())
-    advance_all(chunks[2:4])
+    advance_all((c2, c3, c0, c1))
     bias_sum = jnp.sum(step_pre_grad, axis=0, keepdims=True)
     small_store(0, dot_tn(sel[:, :rank].astype(BF16), low))
     small_store(rank, dgrad_ref[...])
@@ -935,7 +985,7 @@
     pre = conv_pre(ext_ref, cw_ref, cb_ref, rows, inner)
     slope = slope_of(pre, sigmoid(pre))
     base_grad = agrad_ref[...] + skip_ref[0:1, :].astype(F32) * pgrad_ref[...]
-    advance_all(chunks[:2])
+    advance_all((c3,))
     second.wait()
     selg = (sel_part[...] + sel_col[...].astype(F32)).astype(BF16)
     conv_in = (base_grad + dot_nt(selg, sw_ref[...])) * slope
@@ -977,7 +1027,7 @@
     hid_second = pair_copy(6, hid_low, hid_col, col_peer())
     for h in range(2):
         store_split(igi_ref.at[h], dot_tn(hid_ref[h], inner_low) + dot_tn(hidt_ref[h], tail_low))
-    advance_all(chunks[4:])
+    advance_all((c4, c5, c2, c1, c3))
     tail_second.wait()
     tail_own[...] = tail_sum[0] + tail_col[...]
     tail_copies = to_all(tail_own, tails_ref, tail_send, tail_recv)
@@ -997,8 +1047,7 @@
     small_chunk.next()
     hid_copies[1].wait()
     hidden = part_ref[0, pl.ds(mine, half), :].astype(F32) + hid_row[0].astype(F32)
-    advance_all(chunks[2:4])
-    advance_all(chunks[:2])
+    advance_all((c0, c4))
 
     tok = tok_ref[...].astype(F32)
     toko = toko_ref[...].astype(F32)
@@ -1027,7 +1076,7 @@
     mean_copy = pair_copy(7, mean_out, mean_in, col_peer())
     gain_out[...] = jnp.broadcast_to(jnp.sum(hidden * normed, axis=0, keepdims=True), gain_out.shape)
     gain_copy = pair_copy(8, gain_out, gain_in, row_peer())
-    advance_all(chunks[4:] + [small_chunk])
+    advance_all((c5, small_chunk))
     gain_copy.wait()
     gain_pair[...] = gain_out[...] + gain_in[...]
     gain_copies = to_all(gain_pair, gains_ref, gain_send, gain_recv)
@@ -1038,8 +1087,7 @@
     )
     mean = (mean + apart[:, 0:1]) / width
     tg_ref[...] = cot_ref[...] + inv * (scaled - normed * mean)
-    advance_all(chunks[:4])
-    advance_all(chunks[4:] + [small_chunk])
+    advance_all((c4, small_chunk, c5))
     for copy in gain_copies:
         copy.wait()
     gain_total = gains_ref[0]
@@ -1053,7 +1101,6 @@
     half = width // 2
     tile = rows // 2
     block_rows = half // count
-    levels = len(seq_bits(count))
     small = small_rows(count, rank, states, selects)
     f32, bf16 = F32, BF16
     vm = pltpu.VMEM
@@ -1072,10 +1119,16 @@
         vm((2, count, block_rows, inner), bf16), vm((count, small, inner), f32),
         vm((6, count, block_rows, inner), bf16), vm((count, small, inner), f32),
     ]
-    scratch += [vm((6, count >> (k + 1), block_rows, inner), bf16) for k in range(levels)]
-    scratch += [vm((count >> (k + 1), small, inner), f32) for k in range(levels)]
+    most = 0
+    for i, paired in enumerate(chunk_plan + (False,)):
+        last = i == len(chunk_plan)
+        sizes, copies = stage_sizes(stages_of(count, paired), count, i % 2 == 1)
+        most = max(most, copies)
+        scratch += [
+            vm(size + ((small, inner) if last else (block_rows, inner)), f32 if last else bf16) for size in sizes
+        ]
     dma = pltpu.SemaphoreType.DMA
-    scratch += [dma((7, 2 * levels + 1))] * 2 + [dma((9,))] * 2 + [dma((count,))] * 6
+    scratch += [dma((7, most))] * 2 + [dma((9,))] * 2 + [dma((count,))] * 6
     return run_kernel(
         functools.partial(backward_kernel, width=width),
         (

time: 276 us -> 272 us (0.986)
  Pallas kernels: 233 us -> 229 us
    pallas_call x9, Pallas kernels: 233 us -> 229 us  [run_kernel(): pl.pallas_call(kernel, out_shape=outs, in_specs=[smem_spec() if a.dtype =...]
where the time goes in v3:
time: 272 us; the launch traced here: 271 us
  Pallas kernels  229 us (84%)
  local copies, waits for them, and re-layouts  36.4 us (13%)
  between operations  2.78 us (1%)
    pallas_call x9, Pallas kernels, run_kernel(): pl.pallas_call(kernel, out_shape=outs, in_specs=[smem_spec() if a.dtype =...  229 us
    unnamed x38, local copies, waits for them, and re-layouts  13.4 us
  transfers between devices with their start and end apart: 2, of which 0 were waited for; matrix products, arithmetic and copies ran while one was open for 3% of the time, Pallas kernels for 14%

profile of v3, /device:TPU:0, one launch (start us, length us, event | category | flops | bytes accessed | tf_op | source)
XLA Modules:
  0.0 271.3 jit_solution(4093944429812643048)
XLA Ops:
  0.7 1.2 dynamic_slice.47.ints_ref
  3.2 1.4 constant_dynamic-slice_fusion.9.tail_ref
  4.6 2.9 %constant_dynamic-slice_fusion.3 = (bf16[512,512]{1,0:T(8,128)(2,1)}, bf16[512,512]{1,0:T(8,128)(2,1)S(1)}, bf16[512,512]{1,0:T(8,128)(2,1)}, bf16[512,512]{1,0:T(8,128)(2,1)}) fusion(bf16[1024,512]{1,0:T(8,128)(2,1)} %param.26, s32[]{:T(128)S(6)} %select_n.31, s32[]{:T(128)S(6)} %select_n.32, bf16[512,1024]{1,0:T(8,128)(2,1)} %param.15), kind=kLoop, calls=%fused_computation.7 | loop fusion | bytes 4194312 | tf_op jit(solution)/shard_map/dynamic_slice | solution.py:1177
  7.4 5.1 %constant_dynamic-slice_fusion.5 = (bf16[512,1,512]{2,1,0:T(2,128)(2,1)S(1)}, bf16[512,1,512]{2,1,0:T(2,128)(2,1)S(1)}, bf16[512,1,512]{2,1,0:T(2,128)(2,1)S(1)}, bf16[512,1,512]{2,1,0:T(2,128)(2,1)S(1)}) fusion(bf16[512,2,1024]{2,1,0:T(2,128)(2,1)S(1)} %copy-done, s32[]{:T(128)S(6)} %add.42, s32[]{:T(128)S(6)} %select_n.31, s32[]{:T(128)S(6)} %select_n.32), kind=kLoop, calls=%fused_computation.9 | loop fusion | bytes 4194316 | tf_op jit(solution)/shard_map/slice | solution.py:1188
  12.6 1.1 copy_bitcast_fusion.1
  13.7 0.6 broadcast_in_dim.10.gain_ref
  14.3 21.4 %entry_exchange.1 = (bf16[8,8,1024]{2,1,0:T(8,128)(2,1)}, bf16[512,512]{1,0:T(8,128)(2,1)}, bf16[8,512]{1,0:T(8,128)(2,1)}) custom-call(bf16[8,1024]{1,0:T(8,128)(2,1)} %constant_dynamic-slice_fusion.9.tail_ref, bf16[512,512]{1,0:T(8,128)(2,1)} %get-tuple-element.110.wi_ref, bf16[8,512]{1,0:T(8,128)(2,1)} %broadcast_in_dim.10.gain_ref), custom_call_target="tpu_custom_call" | custom-call | bytes 548864 | tf_op jit(solution)/shard_map/entry_exchange/pallas_call | solution.py:101
  35.7 0.6 collective-permute-start
  36.3 1.5 collective-permute-start.1
  37.8 1.3 copy_bitcast_fusion
  39.1 0.7 constant_dynamic-slice_fusion.6
  39.7 0.6 reduce_sum.9
  42.2 0.8 copy.29.sw_ref
  43.6 5.6 %forward_in.1 = (bf16[2,512,512]{2,1,0:T(8,128)(2,1)}, bf16[2,8,512]{2,1,0:T(8,128)(2,1)}, f32[536,512]{1,0:T(8,128)}, bf16[512,512]{1,0:T(8,128)(2,1)}, f32[512,96]{1,0:T(8,128)}) custom-call(bf16[512,512]{1,0:T(8,128)(2,1)} %get-tuple-element.105.tok_ref, bf16[512,512]{1,0:T(8,128)(2,1)} %get-tuple-element.106.toko_ref, ...), custom_call_target="tpu_custom_call" | custom-call | flops 2000000000 | bytes 2355204 | tf_op jit(solution)/shard_map/forward_in/pallas_call | solution.py:101
  49.1 14.2 %select_sum.1.sel_ref = f32[512,96]{1,0:T(8,128)} custom-call(f32[512,96]{1,0:T(8,128)} %get-tuple-element.55.x_ref), custom_call_target="tpu_custom_call" | custom-call | bytes 196608 | tf_op jit(solution)/shard_map/select_sum/pallas_call | solution.py:101
  64.0 9.9 %forward_ends.1 = (f32[512,512]{1,0:T(8,128)}, f32[512,512]{1,0:T(8,128)}, f32[16,8,512]{2,1,0:T(8,128)}, f32[8,512]{1,0:T(8,128)}, bf16[24,512]{1,0:T(8,128)(2,1)}) custom-call(f32[512,96]{1,0:T(8,128)} %select_sum.1.sel_ref, bf16[64,512]{1,0:T(8,128)(2,1)} %tw_ref.3, bf16[8,512]{1,0:T(8,128)(2,1)} %broadcast_in_dim.12.tb_ref, f32[16,512]{1,0:T(8,128)} %dl_ref.7, ...), custom_call_target="tpu_custom_call" | custom-call | flops 2000000000 | bytes 827396 | tf_op jit(solution)/shard_map/forward_ends/pallas_call | solution.py:101
  73.9 8.2 %state_gather.1.table_ref = bf16[8,24,512]{2,1,0:T(8,128)(2,1)} custom-call(bf16[24,512]{1,0:T(8,128)(2,1)} %get-tuple-element.57.x_ref), custom_call_target="tpu_custom_call" | custom-call | bytes 24576 | tf_op jit(solution)/shard_map/state_gather/pallas_call | solution.py:101
  82.2 1.2 fusion
  84.0 13.4 %forward_out.1 = (f32[16,8,512]{2,1,0:T(8,128)}, f32[512,512]{1,0:T(8,128)}, f32[512,512]{1,0:T(8,128)}, bf16[512,512]{1,0:T(8,128)(2,1)}, bf16[2,512,512]{2,1,0:T(8,128)(2,1)}) custom-call(bf16[8,24,512]{2,1,0:T(8,128)(2,1)} %state_gather.1.table_ref, s32[8]{0:T(128)} %parents_ref.3, s32[1]{0:T(128)} %bitcast.5.me_ref, f32[16,512]{1,0:T(8,128)} %dl_ref.7, ...), custom_call_target="tpu_custom_call" | custom-call | flops 4000000000 | bytes 5431332 | tf_op jit(solution)/shard_map/forward_out/pallas_call | solution.py:101
  98.0 21.5 %middle_exchange.1 = (bf16[256,512]{1,0:T(8,128)(2,1)}, f32[256,512]{1,0:T(8,128)}, bf16[2,512,512]{2,1,0:T(8,128)(2,1)}) custom-call(bf16[2,512,512]{2,1,0:T(8,128)(2,1)} %get-tuple-element.64.part_ref, bf16[256,512]{1,0:T(8,128)(2,1)} %get-tuple-element.95.tok_ref, bf16[256,512]{1,0:T(8,128)(2,1)} %get-tuple-element.111.teach_ref, ...), custom_call_target="tpu_custom_call" | custom-call | bytes 1576964 | tf_op jit(solution)/shard_map/middle_exchange/pallas_call | solution.py:101
  119.5 13.0 %backward_in.1 = (bf16[2,8,64,512]{3,2,1,0:T(8,128)(2,1)}, bf16[512,512]{1,0:T(8,128)(2,1)}, bf16[2,8,64,512]{3,2,1,0:T(8,128)(2,1)}, f32[512,512]{1,0:T(8,128)}...) custom-call(bf16[2,512,512]{2,1,0:T(8,128)(2,1)} %get-tuple-element.66.cot_ref, ...), custom_call_target="tpu_custom_call" | custom-call | flops 4000000000 | bytes 7593984 | tf_op jit(solution)/shard_map/backward_in/pallas_call | solution.py:101
  132.5 122.2 %backward.1 = (f32[1024,512]{1,0:T(8,128)}, f32[8192,128]{1,0:T(8,128)}, f32[256,512]{1,0:T(8,128)}, f32[8,512]{1,0:T(8,128)}, f32[64,512]{1,0:T(8,128)}, /*inde...) custom-call(bf16[8,24,512]{2,1,0:T(8,128)(2,1)} %state_gather.1.table_ref, ...), custom_call_target="tpu_custom_call" | custom-call | flops 16000000000 | bytes 12791872 | tf_op jit(solution)/shard_map/backward/pallas_call | solution.py:101
  254.7 1.4 fusion.1
  256.1 1.3 slice.32
  257.4 1.3 slice.31
  258.7 1.7 copy.49
  260.4 1.9 copy.50
  262.3 5.8 %copy.51 = f32[512,2,1024]{2,1,0:T(2,128)} copy(f32[512,2,1024]{2,1,0:T(2,128)} %bitcast.21) | data formatting | bytes 8388608
  268.1 0.7 copy.52
  268.8 0.7 copy.53
  269.4 0.6 copy.54
  270.0 1.3 copy.55
  (38 shorter events, 3.6 us)
Async XLA Ops:
  4.6 2.9 %copy-start = (bf16[512,2,1024]{2,1,0:T(2,128)(2,1)S(1)}, bf16[512,2,1024]{2,1,0:T(2,128)(2,1)}, u32[]{:S(2)}) copy-start(bf16[512,2,1024]{2,1,0:T(2,128)(2,1)} %param.18) | copy-start | bytes 6291460
  12.6 1.1 copy-start.9
  13.7 26.1 %copy-start.13 = (s32[8]{0:T(128)S(1)}, s32[8]{0:T(128)}, u32[]{:S(2)}) copy-start(s32[8]{0:T(128)} %param.29) | copy-start | bytes 100
  13.7 27.3 %copy-start.14 = (s32[8]{0:T(128)S(1)}, s32[8]{0:T(128)}, u32[]{:S(2)}) copy-start(s32[8]{0:T(128)} %parents_ref.3) | copy-start | bytes 100
  13.7 28.5 %copy-start.7 = (bf16[512,96]{0,1:T(8,128)(2,1)S(1)}, bf16[512,96]{0,1:T(8,128)(2,1)}, u32[]{:S(2)}) copy-start(bf16[512,96]{0,1:T(8,128)(2,1)} %param.21) | copy-start | bytes 294916
  14.3 28.7 %copy-start.10 = (bf16[512]{0:T(512)(128)(2,1)S(1)}, bf16[512]{0:T(512)(128)(2,1)}, u32[]{:S(2)}) copy-start(bf16[512]{0:T(512)(128)(2,1)} %param.20) | copy-start | bytes 3076
  35.7 3.4 %copy-start.5 = (bf16[8,8,1024]{2,1,0:T(8,128)(2,1)S(1)}, bf16[8,8,1024]{2,1,0:T(8,128)(2,1)}, u32[]{:S(2)}) copy-start(bf16[8,8,1024]{2,1,0:T(8,128)(2,1)} %get-tuple-element.51) | copy-start | bytes 393220
  35.7 47.7 %collective-permute-start = (bf16[512,512]{1,0:T(8,128)(2,1)S(1)}, bf16[512,512]{1,0:T(8,128)(2,1)}, u32[]{:S(2)}, u32[]{:S(2)}) collective-permute-start(bf16[512,512]{1,0:T(8,128)(2,1)S(1)} %get-tuple-element.62), channel_id=1, source_target_pairs={{0,1},{1,0},{2,3},{3,2},{4,5},{5,4},{6,7},{7,6},{8,9},{9,8},{10,11... | collective-permute-start | bytes 1572872 | tf_op jit(solution)/shard_map/ppermute | solution.py:1198
  36.3 47.1 %collective-permute-start.1 = (bf16[512,512]{1,0:T(8,128)(2,1)S(1)}, bf16[512,512]{1,0:T(8,128)(2,1)}, u32[]{:S(2)}, u32[]{:S(2)}) collective-permute-start(bf16[512,512]{1,0:T(8,128)(2,1)S(1)} %get-tuple-element.63), channel_id=1, source_target_pairs={{0,1},{1,0},{2,3},{3,2},{4,5},{5,4},{6,7},{7,6},{8,9},{9,8},{10,11... | collective-permute-start | bytes 1572872 | tf_op jit(solution)/shard_map/ppermute | solution.py:1199
  43.6 19.8 %copy-start.11 = (bf16[512]{0:T(512)(128)(2,1)S(1)}, bf16[512]{0:T(512)(128)(2,1)}, u32[]{:S(2)}) copy-start(bf16[512]{0:T(512)(128)(2,1)} %param.23) | copy-start | bytes 3076
  64.0 18.2 %copy-start.1 = (bf16[512,1024]{1,0:T(8,128)(2,1)S(1)}, bf16[512,1024]{1,0:T(8,128)(2,1)}, u32[]{:S(2)}) copy-start(bf16[512,1024]{1,0:T(8,128)(2,1)} %param.15) | copy-start | bytes 3145732
  64.0 18.2 %copy-start.6 = (bf16[512,512]{1,0:T(8,128)(2,1)S(1)}, bf16[512,512]{1,0:T(8,128)(2,1)}, u32[]{:S(2)}) copy-start(bf16[512,512]{1,0:T(8,128)(2,1)} %param.16) | copy-start | bytes 1572868
  64.0 19.4 %copy-start.12 = (bf16[512]{0:T(512)(128)(2,1)S(1)}, bf16[512]{0:T(512)(128)(2,1)}, u32[]{:S(2)}) copy-start(bf16[512]{0:T(512)(128)(2,1)} %param.25) | copy-start | bytes 3076
  262.3 5.8 %copy-start.3 = (f32[96,512]{1,0:T(8,128)S(1)}, f32[96,512]{1,0:T(8,128)}, u32[]{:S(2)}) copy-start(f32[96,512]{1,0:T(8,128)} %get-tuple-element.86) | copy-start | bytes 589828
  262.3 6.5 %copy-start.4 = (f32[64,512]{1,0:T(8,128)S(1)}, f32[64,512]{1,0:T(8,128)}, u32[]{:S(2)}) copy-start(f32[64,512]{1,0:T(8,128)} %get-tuple-element.131) | copy-start | bytes 393220
  262.3 7.1 %copy-start.8 = (f32[16,512]{1,0:T(8,128)S(1)}, f32[16,512]{1,0:T(8,128)}, u32[]{:S(2)}) copy-start(f32[16,512]{1,0:T(8,128)} %get-tuple-element.133) | copy-start | bytes 98308
  262.3 7.8 %copy-start.2 = (f32[1024,512]{1,0:T(8,128)S(1)}, f32[1024,512]{1,0:T(8,128)}, u32[]{:S(2)}) copy-start(f32[1024,512]{1,0:T(8,128)} %get-tuple-element.135) | copy-start | bytes 6291460

commit v4 on v3

--- a/solution.py
+++ b/solution.py
@@ -232,11 +232,12 @@
 
 
 def middle_kernel(
-    part_ref, tok_ref, teach_ref, ints_ref, scale_ref,
+    part_ref, tok_ref, teach_ref, ints_ref,
     out_ref, cot_ref, low_ref,
     from_row, to_col, from_col, send, recv,
 ):
     half = tok_ref.shape[0]
+    segments = ints_ref.shape[0]
     row = lax.axis_index("row")
     mine = pl.multiple_of(row * half, half)
     other = pl.multiple_of((1 - row) * half, half)
@@ -260,7 +261,11 @@
     result = tile + from_col[...].astype(F32)
     out_ref[...] = result.astype(BF16)
     positions = mine + lax.broadcasted_iota(jnp.int32, (half, 1), 0)
-    counted = (positions < ints_ref[0]).astype(F32) * scale_ref[0:1, 0:1]
+    total = ints_ref[0]
+    for i in range(1, segments):
+        total = total + ints_ref[i]
+    share = jnp.full((half, 1), total, jnp.int32).astype(F32)
+    counted = (positions < ints_ref[lax.axis_index("seq")]).astype(F32) * ((2 * half * segments) / share)
     cot = (result - teach_ref[...].astype(F32)) * counted
     cot_ref[...] = cot
     low_ref[0, pl.ds(mine, half), :] = cot.astype(BF16)
@@ -277,13 +282,13 @@
     fourth.wait()
 
 
-def middle_exchange(part, tok_tile, teach_tile, my_valid, scale):
+def middle_exchange(part, tok_tile, teach_tile, valid_rows):
     _, rows, width = part.shape
     half = rows // 2
     return run_kernel(
         middle_kernel,
         (struct((half, width), BF16), struct((half, width), F32), struct((2, rows, width), BF16)),
-        (part, tok_tile, teach_tile, my_valid, scale),
+        (part, tok_tile, teach_tile, valid_rows),
         "middle_exchange",
         scratch=[
             pltpu.VMEM((2, half, width), BF16),
@@ -304,8 +309,9 @@
     rows, half = tok_ref.shape
     steps = rows // spans
     width = 2 * half
-    parent = jnp.maximum(ints_ref[0], 0)
-    present = (ints_ref[0] >= 0).astype(F32)
+    above = ints_ref[lax.axis_index("seq")]
+    parent = jnp.maximum(above, 0)
+    present = (above >= 0).astype(F32)
     gain = gain_ref[0:1, :].astype(F32)
     gaino = gaino_ref[0:1, :].astype(F32)
 
@@ -341,7 +347,10 @@
         pre = pre + taps[k : k + 1, :] * ext_ref[k * spans : k * spans + rows, :]
     act = (pre * sigmoid(pre)).astype(BF16)
     act_ref[...] = act
-    sel_ref[...] = dot(act, sw_ref[...])
+    chosen = dot(act, sw_ref[...])
+    sel_ref[...] = jnp.concatenate(
+        [chosen, jnp.zeros((rows, sel_ref.shape[1] - chosen.shape[1]), F32)], axis=1
+    )
 
 
 def conv_pre(ext_ref, cw_ref, cb_ref, rows, half):
@@ -383,7 +392,7 @@
     steps = rows // spans
     states = dl_ref.shape[0]
     rank = tw_ref.shape[0]
-    length = ints_ref[0]
+    length = ints_ref[lax.axis_index("seq")]
     sel = sel_ref[...]
     step_pre = dot(sel[:, :rank].astype(BF16), tw_ref[...]) + tb_ref[0:1, :].astype(F32)
     pre_ref[...] = step_pre
@@ -440,17 +449,16 @@
 
 
 def forward_out_kernel(
-    table_ref, parents_ref, me_ref, dl_ref, reach_ref, cum_ref, delta_ref, act_ref, sel_ref,
+    table_ref, parents_ref, dl_ref, reach_ref, cum_ref, delta_ref, act_ref, sel_ref,
     hid_ref, wg_ref, wgo_ref, skip_ref, ow_ref, owo_ref,
     starts_ref, mpre_ref, gate_ref, mixed_ref, part_ref,
-    finals, drive, b_ref, c_ref, rate_ref,
+    finals, drive, b_ref, c_ref, rate_ref, *, rank
 ):
     rows, width = act_ref.shape
     steps = rows // spans
     states = dl_ref.shape[0]
-    rank = sel_ref.shape[1] - 2 * states
     count = table_ref.shape[0]
-    me = me_ref[0]
+    me = lax.axis_index("seq")
     decay_rows(dl_ref, rate_ref, log2e)
     rate = -jnp.exp(dl_ref[...]) * log2e
 
@@ -469,7 +477,7 @@
     sel = sel_ref[...]
     drive[...] = delta_ref[...] * act_ref[...].astype(F32)
     b_ref[...] = spread(sel[:, rank : rank + states], states)
-    c_ref[...] = spread(sel[:, rank + states :], states)
+    c_ref[...] = spread(sel[:, rank + states : rank + 2 * states], states)
     index2 = span_index((spans, width))
     cum = jnp.where(index2 >= 1, shift_spans(cum_ref[...], 1), 0.0)
     for n in range(states):
@@ -506,70 +514,6 @@
     part_ref[1] = dot(natural, owo_ref[...]).astype(BF16)
 
 
-def backward_in_kernel(
-    cot_ref, mixed_ref, ow_ref, owo_ref, gate_ref, mpre_ref, act_ref, skip_ref, sel_ref,
-    delta_ref, dl_ref, cum_ref, hid_ref,
-    og_ref, ggrad_ref, ig_ref, pgrad_ref, sgrad_ref, back_ref, flow_ref,
-    c_ref, rate_ref,
-):
-    rows, width = act_ref.shape
-    steps = rows // spans
-    states = dl_ref.shape[0]
-    rank = sel_ref.shape[1] - 2 * states
-    order = to_steps(rows, steps)
-    cot = dot(order, cot_ref[0]).astype(BF16)
-    coto = dot(order, cot_ref[1]).astype(BF16)
-    mixed_grad = dot_nt(cot, ow_ref[...]) + dot_nt(coto, owo_ref[...])
-    gate = gate_ref[...]
-    sigma = sigmoid(gate)
-    pre_grad = mixed_grad * (gate * sigma)
-    pgrad_ref[...] = pre_grad
-    gate_grad = (mixed_grad * mpre_ref[...] * slope_of(gate, sigma)).astype(BF16)
-    ggrad_ref[...] = gate_grad
-    sgrad_ref[...] = jnp.broadcast_to(
-        jnp.sum(pre_grad * act_ref[...].astype(F32), axis=0, keepdims=True), sgrad_ref.shape
-    )
-    c_ref[...] = spread(sel_ref[:, rank + states :], states)
-    decay_rows(dl_ref, rate_ref, log2e)
-
-    for group in range(width // lanes):
-        here = slice(group * lanes, (group + 1) * lanes)
-
-        def retreat(back, carry):
-            step = steps - 1 - back
-            d = delta_ref[step_ds(step), here]
-            p = pgrad_ref[step_ds(step), here]
-            out = []
-            for n in range(states):
-                a = jnp.exp2(d * rate_ref[n, :, here])
-                out.append(a * (c_ref[step_ds(step), n * lanes : (n + 1) * lanes] * p + carry[n]))
-            return tuple(out)
-
-        flows = lax.fori_loop(0, steps, retreat, (jnp.zeros((spans, lanes), F32),) * states)
-        for n in range(states):
-            back_ref[n, :, here] = flows[n]
-
-    index2 = span_index((spans, width))
-    cum = cum_ref[...]
-    part = cum - jnp.where(index2 >= 1, shift_spans(cum, 1), 0.0)
-    shift = 1
-    while shift < spans:
-        inside = index2 < spans - shift
-        for n in range(states):
-            own = back_ref[n]
-            later = jnp.where(inside, shift_spans(own, -shift), 0.0)
-            back_ref[n] = own + jnp.exp2(part * rate_ref[n]) * later
-        part = part + jnp.where(inside, shift_spans(part, -shift), 0.0)
-        shift *= 2
-    flow_ref[...] = jnp.concatenate(
-        [back_ref[n, 0:1, :] for n in range(states)], axis=0
-    ).astype(BF16)
-    store_split(og_ref.at[0], dot_tn(mixed_ref[...], cot))
-    store_split(og_ref.at[1], dot_tn(mixed_ref[...], coto))
-    store_split(ig_ref.at[0], dot_tn(hid_ref[0], gate_grad))
-    store_split(ig_ref.at[1], dot_tn(hid_ref[1], gate_grad))
-
-
 def seq_bits(count):
     bits = []
     mask = 1
@@ -620,9 +564,9 @@
 
 
 class Chunk:
-    def __init__(self, source, total, landings, send, recv, stages, crossed, emit):
+    def __init__(self, source, total, landings, send, recv, stages, crossed):
         self.source, self.total, self.landings = source, total, landings
-        self.send, self.recv, self.stages, self.crossed, self.emit = send, recv, stages, crossed, emit
+        self.send, self.recv, self.stages, self.crossed = send, recv, stages, crossed
         self.count = source.shape[0]
         self.me = lax.axis_index("seq")
         self.copies = []
@@ -702,8 +646,6 @@
         level = 2 * last - 1 - at
         if level >= 0:
             self.gather(level)
-        else:
-            self.emit(self.total)
 
     def finish(self):
         for copy in self.copies:
@@ -735,16 +677,18 @@
 
 
 def backward_kernel(
-    table_ref, flow_ref, parents_ref, lengths_ref, dl_ref, starts_ref, back_ref, cum_ref,
-    delta_ref, act_ref, sel_ref, pgrad_ref, pre_ref, tw_ref,
+    cotangent_ref, mixed_ref, ow_ref, owo_ref, gate_ref, mpre_ref,
+    table_ref, parents_ref, lengths_ref, dl_ref, starts_ref, cum_ref,
+    delta_ref, act_ref, sel_ref, pre_ref, tw_ref,
     sw_ref, skip_ref, ext_ref, cw_ref, cb_ref, hid_ref, hidt_ref, wi_ref, wio_ref, wg_ref, wgo_ref,
-    ggrad_ref, tok_ref, toko_ref, gain_ref, cot_ref, og_ref, igg_ref, sgrad_ref,
-    og_out, ig_out, tg_ref, gg_ref, stepg_out, decayg_out, selectg_out, smallg_out,
-    flows_ref, grads, c_ref, rate_ref, decay_buf, state_buf, b_sum, c_sum, agrad_ref, dgrad_ref,
+    tok_ref, toko_ref, gain_ref, cot_ref,
+    totals, small_total, tg_ref, gg_ref,
+    og_ref, igg_ref, ggrad_ref, pgrad_ref, back_ref, flow_ref,
+    flows_ref, grads, c_ref, rate_ref, state_buf, b_sum, c_sum, agrad_ref, dgrad_ref,
     sel_part, sel_row, sel_low, sel_col, cig_ref, part_ref, tpart_ref,
     hid_row, tail_row, hid_low, hid_col, tail_low_ref, tail_col, tail_own, tails_ref,
-    mean_out, mean_in, gain_out, gain_in, gain_pair, gains_ref,
-    igi_ref, small_ref, totals, small_total, *rest,
+    mean_out, mean_in, gain_out, gain_in, gains_ref,
+    igi_ref, small_ref, og_out, ig_out, *rest,
     width,
 ):
     count = table_ref.shape[0]
@@ -759,7 +703,7 @@
     steps = rows // spans
     states = dl_ref.shape[0]
     rank = tw_ref.shape[0]
-    selects = sel_ref.shape[1]
+    selects = sw_ref.shape[1]
     me = lax.axis_index("seq")
     row = lax.axis_index("row")
     col = lax.axis_index("col")
@@ -791,25 +735,6 @@
         dst[me] = src[...]
         return copies
 
-    block_rows, block = og_ref.shape[2], og_ref.shape[3]
-
-    def rows_out(side):
-        def emit(total):
-            base = pl.multiple_of(side * (count * block_rows), count * block_rows)
-            for i in range(count):
-                og_out[pl.ds(pl.multiple_of(base + i * block_rows, 8), block_rows), :] = widen(total[i])
-        return emit
-
-    def lanes_out(which, side):
-        def emit(total):
-            tiles = block // lanes
-            for i in range(count):
-                value = widen(total[i])
-                for j in range(tiles):
-                    first = i * block_rows * 4 * tiles + (side * tiles + j) * 2 + which
-                    ig_out[pl.ds(first, block_rows, stride=4 * tiles), :] = value[:, j * lanes : (j + 1) * lanes]
-        return emit
-
     def small_slabs():
         slab = small_ref.shape[1] // 8
         return lambda at: (at // slab, slice((at % slab) * 8, (at % slab) * 8 + 8))
@@ -821,36 +746,17 @@
             a, b = place_of(first // 8 + j)
             small_ref[a, b, :] = value[j * 8 : (j + 1) * 8]
 
-    def small_emit(total):
-        def read(first, size):
-            parts = []
-            for j in range(size // 8):
-                a, b = place_of(first // 8 + j)
-                parts.append(total[a, b, :])
-            return jnp.concatenate(parts, axis=0) if len(parts) > 1 else parts[0]
-        stepg_out[...] = read(0, rank)
-        decayg_out[...] = read(rank, states)
-        selectg_out[...] = read(rank + states, selects)
-        smallg_out[...] = read(rank + states + selects, 8)
-
-    plan = [
-        (og_ref, 0, rows_out(col)),
-        (og_ref, 1, rows_out(1 - col)),
-        (igg_ref, 0, lanes_out(1, col)),
-        (igg_ref, 1, lanes_out(1, 1 - col)),
-        (igi_ref, 0, lanes_out(0, col)),
-        (igi_ref, 1, lanes_out(0, 1 - col)),
-    ]
+    sources = [og_ref.at[0], og_ref.at[1], igg_ref.at[0], igg_ref.at[1], igi_ref.at[0], igi_ref.at[1]]
     chunks = [
         Chunk(
-            source.at[h], totals.at[i], landings[i], send.at[i], recv.at[i],
-            stages_of(count, chunk_plan[i]), h == 1, emit,
+            source, totals.at[i], landings[i], send.at[i], recv.at[i],
+            stages_of(count, chunk_plan[i]), i % 2 == 1,
         )
-        for i, (source, h, emit) in enumerate(plan)
+        for i, source in enumerate(sources)
     ]
     small_chunk = Chunk(
-        small_ref, small_total, landings[-1], send.at[len(plan)], recv.at[len(plan)],
-        stages_of(count, False), False, small_emit,
+        small_ref, small_total, landings[-1], send.at[len(sources)], recv.at[len(sources)],
+        stages_of(count, False), False,
     )
 
     drive = og_out.at[0:rows]
@@ -860,9 +766,66 @@
         return ig_out[pl.ds(pl.multiple_of(n * rows + step * spans, spans), spans), :]
 
     c0, c1, c2, c3, c4, c5 = chunks
+    early = {2: (c0, c1), -1: (c2, c3)}
+    pumps = {
+        (1, 0): (c0, c1), (2, 0): (c2, c3), (2, 1): (c1,), (3, 0): (c0, c3), (3, 1): (c1,),
+    }
+    from_tokens = to_steps(rows, steps)
+    cot = dot(from_tokens, cotangent_ref[0]).astype(BF16)
+    coto = dot(from_tokens, cotangent_ref[1]).astype(BF16)
+    store_split(og_ref.at[0], dot_tn(mixed_ref[...], cot))
+    store_split(og_ref.at[1], dot_tn(mixed_ref[...], coto))
+    advance_all((c0, c1))
+    mixed_grad = dot_nt(cot, ow_ref[...]) + dot_nt(coto, owo_ref[...])
+    gate = gate_ref[...]
+    sigma = sigmoid(gate)
+    pre_grad = mixed_grad * (gate * sigma)
+    pgrad_ref[...] = pre_grad
+    gate_grad = (mixed_grad * mpre_ref[...] * slope_of(gate, sigma)).astype(BF16)
+    ggrad_ref[...] = gate_grad
+    store_split(igg_ref.at[0], dot_tn(hid_ref[0], gate_grad))
+    store_split(igg_ref.at[1], dot_tn(hid_ref[1], gate_grad))
+    advance_all((c2, c3))
+    skip_sum = jnp.sum(pre_grad * act_ref[...].astype(F32), axis=0, keepdims=True)
+    decay_rows(dl_ref, rate_ref, log2e)
+    c_ref[...] = spread(sel_ref[:, rank + states : rank + 2 * states], states)
+
+    for group in range(inner // lanes):
+        here = slice(group * lanes, (group + 1) * lanes)
+
+        def fall(back, carry):
+            step = steps - 1 - back
+            d = delta_ref[step_ds(step), here]
+            p = pgrad_ref[step_ds(step), here]
+            out = []
+            for n in range(states):
+                a = jnp.exp2(d * rate_ref[n, :, here])
+                out.append(a * (c_ref[step_ds(step), n * lanes : (n + 1) * lanes] * p + carry[n]))
+            return tuple(out)
+
+        advance_all(early.get(group, ()))
+        ends = lax.fori_loop(0, steps, fall, (jnp.zeros((spans, lanes), F32),) * states)
+        for n in range(states):
+            back_ref[n, :, here] = ends[n]
+
+    index2 = span_index((spans, inner))
+    cum = cum_ref[...]
+    part = cum - jnp.where(index2 >= 1, shift_spans(cum, 1), 0.0)
+    shift = 1
+    while shift < spans:
+        inside = index2 < spans - shift
+        for n in range(states):
+            own = back_ref[n]
+            later = jnp.where(inside, shift_spans(own, -shift), 0.0)
+            back_ref[n] = own + jnp.exp2(part * rate_ref[n]) * later
+        part = part + jnp.where(inside, shift_spans(part, -shift), 0.0)
+        shift *= 2
+    flow_ref[...] = jnp.concatenate(
+        [back_ref[n, 0:1, :] for n in range(states)], axis=0
+    ).astype(BF16)
+
     flow_copies = to_all(flow_ref, flows_ref, flow_send, flow_recv)
-    advance_all((c0, c1, c2, c3))
-    decay_rows(dl_ref, rate_ref, log2e)
+    advance_all(early.get(-1, ()))
     rate = -jnp.exp(dl_ref[...]) * log2e
     sel = sel_ref[...]
     drive[...] = delta_ref[...] * act_ref[...].astype(F32)
@@ -870,9 +833,6 @@
         ig_out[n * rows : (n + 1) * rows, :] = jnp.broadcast_to(
             sel[:, rank + n : rank + n + 1], (rows, lanes)
         )
-    c_ref[...] = spread(sel[:, rank + states :], states)
-    index2 = span_index((spans, inner))
-    cum = cum_ref[...]
     after = cum[spans - 1 : spans, :] - cum
     inside = index2 < spans - 1
     slot = lax.broadcasted_iota(jnp.int32, (count, 1, 1), 0)
@@ -885,9 +845,6 @@
         return carry
 
     groups = inner // lanes
-    pumps = {
-        (1, 0): (c0, c1), (2, 0): (c2, c3), (2, 1): (c1,), (3, 0): (c0, c3), (3, 1): (c1,),
-    }
     for group in range(groups):
         here = slice(group * lanes, (group + 1) * lanes)
 
@@ -898,7 +855,6 @@
             for n in range(states):
                 state_buf[n, step_ds(step), :] = carry[n]
                 a = jnp.exp2(d * rate_ref[n, :, here])
-                decay_buf[n, step_ds(step), :] = a
                 out.append(a * carry[n] + w * b_at(n, step))
             return tuple(out)
 
@@ -931,7 +887,7 @@
             decayed = [None, None]
             for n in range(states):
                 cols = slice(n * lanes, (n + 1) * lanes)
-                a = decay_buf[n, at, :]
+                a = jnp.exp2(d * rate_ref[n, :, here])
                 adjoint = c_ref[at, cols] * p + flows[n]
                 moved = a * adjoint
                 growth = moved * state_buf[n, at, :]
@@ -966,7 +922,10 @@
     low = step_pre_grad.astype(BF16)
     gather = gather_matrix(states)
     sel_part[...] = jnp.concatenate(
-        [dot_nt(low, tw_ref[...]), dot(b_sum[...].astype(BF16), gather), dot(c_sum[...].astype(BF16), gather)],
+        [
+            dot_nt(low, tw_ref[...]), dot(b_sum[...].astype(BF16), gather),
+            dot(c_sum[...].astype(BF16), gather), jnp.zeros((rows, sel_part.shape[1] - selects), F32),
+        ],
         axis=1,
     )
     first = pair_copy(0, sel_part, sel_row, row_peer())
@@ -987,7 +946,7 @@
     base_grad = agrad_ref[...] + skip_ref[0:1, :].astype(F32) * pgrad_ref[...]
     advance_all((c3,))
     second.wait()
-    selg = (sel_part[...] + sel_col[...].astype(F32)).astype(BF16)
+    selg = (sel_part[...] + sel_col[...].astype(F32)).astype(BF16)[:, :selects]
     conv_in = (base_grad + dot_nt(selg, sw_ref[...])) * slope
     cig_ref[0:rows, :] = conv_in
     taps = cw_ref[...].astype(F32)
@@ -1037,7 +996,7 @@
         for k in range(4)
     ]
     sums.append(jnp.sum(conv_in, axis=0, keepdims=True))
-    sums.append(sgrad_ref[0:1, :])
+    sums.append(skip_sum)
     sums.append(bias_sum)
     sums.append(jnp.zeros((1, inner), F32))
     small_store(rank + states + selects, jnp.concatenate(sums, axis=0))
@@ -1078,8 +1037,8 @@
     gain_copy = pair_copy(8, gain_out, gain_in, row_peer())
     advance_all((c5, small_chunk))
     gain_copy.wait()
-    gain_pair[...] = gain_out[...] + gain_in[...]
-    gain_copies = to_all(gain_pair, gains_ref, gain_send, gain_recv)
+    gain_out[...] = gain_out[...] + gain_in[...]
+    gain_copies = to_all(gain_out, gains_ref, gain_send, gain_recv)
     mean_copy.wait()
     apart = lax.dot_general(
         mean_in[...], jnp.full((8, lanes), 0.125, F32), (((0,), (0,)), ((), ())),
@@ -1097,7 +1056,7 @@
     run_out(chunks + [small_chunk])
 
 
-def backward_call(args, count, rows, width, inner, states, rank, selects):
+def backward_call(args, count, rows, width, inner, states, rank, selects, padded):
     half = width // 2
     tile = rows // 2
     block_rows = half // count
@@ -1105,19 +1064,21 @@
     f32, bf16 = F32, BF16
     vm = pltpu.VMEM
     scratch = [
+        vm((2, count, inner // count, half), bf16), vm((2, count, block_rows, inner), bf16),
+        vm((rows, inner), bf16), vm((rows, inner), f32), vm((states, spans, inner), f32), vm((states, inner), bf16),
         vm((count, states, inner), bf16), vm((count, states, inner), f32),
         vm((rows, states * lanes), f32), vm((states, spans, inner), f32),
-        vm((states, rows, lanes), f32), vm((states, rows + spans, lanes), f32),
+        vm((states, rows + spans, lanes), f32),
         vm((rows, states * lanes), f32), vm((rows, states * lanes), f32),
         vm((rows, inner), f32), vm((states, inner), f32),
-        vm((rows, selects), f32), vm((rows, selects), f32), vm((rows, selects), bf16), vm((rows, selects), bf16),
+        vm((rows, padded), f32), vm((rows, padded), f32), vm((rows, padded), bf16), vm((rows, padded), bf16),
         vm((rows + 3 * spans, inner), f32), vm((2, rows, half), bf16), vm((2, 8, half), f32),
         vm((2, tile, half), bf16), vm((2, 8, half), f32), vm((tile, half), bf16), vm((tile, half), bf16),
         vm((8, half), f32), vm((8, half), f32), vm((8, half), f32), vm((count, 8, half), f32),
-        vm((8, tile), f32), vm((8, tile), f32), vm((8, half), f32), vm((8, half), f32), vm((8, half), f32),
+        vm((8, tile), f32), vm((8, tile), f32), vm((8, half), f32), vm((8, half), f32),
         vm((count, 8, half), f32),
         vm((2, count, block_rows, inner), bf16), vm((count, small, inner), f32),
-        vm((6, count, block_rows, inner), bf16), vm((count, small, inner), f32),
+        vm((2 * inner, half), f32), vm((half * 4 * inner // lanes, lanes), f32),
     ]
     most = 0
     for i, paired in enumerate(chunk_plan + (False,)):
@@ -1132,14 +1093,10 @@
     return run_kernel(
         functools.partial(backward_kernel, width=width),
         (
-            struct((2 * inner, half), f32),
-            struct((half * 4 * inner // lanes, lanes), f32),
+            struct((6, count, block_rows, inner), bf16),
+            struct((count, small, inner), f32),
             struct((tile, half), f32),
             struct((8, half), f32),
-            struct((rank, inner), f32),
-            struct((states, inner), f32),
-            struct((selects, inner), f32),
-            struct((8, inner), f32),
         ),
         args,
         "backward",
@@ -1147,6 +1104,61 @@
         flops=16e9,
         collective=4,
         grant=vmem_most,
+    )
+
+
+def final_kernel(
+    totals, small_ref, tg_ref, gg_ref, branch_ref,
+    out_out, tg_out, gain_out, ig_out, conv_out, bias_out, select_out, step_out, step_bias_out, decay_out, skip_out, og_out,
+):
+    count, rows, width = totals.shape[1:]
+    col = lax.axis_index("col")
+    tiles = width // lanes
+    for side in range(2):
+        place = col if side == 0 else 1 - col
+        base = pl.multiple_of(place * (count * rows), count * rows)
+        for i in range(count):
+            og_out[pl.ds(pl.multiple_of(base + i * rows, 8), rows), :] = widen(totals[side, i])
+            for which in range(2):
+                value = widen(totals[(4 if which == 0 else 2) + side, i])
+                for j in range(tiles):
+                    first = i * rows * 4 * tiles + (place * tiles + j) * 2 + which
+                    ig_out[pl.ds(first, rows, stride=4 * tiles), :] = value[:, j * lanes : (j + 1) * lanes]
+    slab = small_ref.shape[1] // 8
+
+    def read(first, size):
+        parts = []
+        for j in range(first // 8, (first + size) // 8):
+            parts.append(small_ref[j // slab, (j % slab) * 8 : (j % slab) * 8 + 8, :])
+        return jnp.concatenate(parts, axis=0) if len(parts) > 1 else parts[0]
+
+    rank, states, selects = step_out.shape[0], decay_out.shape[0], select_out.shape[1]
+    step_out[...] = read(0, rank)
+    decay_out[...] = read(rank, states)
+    select_out[...] = read(rank + states, selects).T
+    last = read(rank + states + selects, 8)
+    conv_out[...] = last[0:4]
+    bias_out[...] = last[4]
+    skip_out[...] = last[5]
+    step_bias_out[...] = last[6]
+    gain_out[...] = gg_ref[0, :]
+    tg_out[...] = tg_ref[...]
+    out_out[...] = branch_ref[...]
+
+
+def final_call(totals, small, tg, gg, output, rank, states, selects):
+    inner = totals.shape[3]
+    half = tg.shape[1]
+    return run_kernel(
+        final_kernel,
+        (
+            struct(output.shape, BF16), struct(tg.shape, F32), struct((half,), F32),
+            struct((half * 4 * inner // lanes, lanes), F32), struct((4, inner), F32), struct((inner,), F32),
+            struct((inner, selects), F32), struct((rank, inner), F32), struct((inner,), F32),
+            struct((states, inner), F32), struct((inner,), F32), struct((2 * inner, half), F32),
+        ),
+        (totals, small, tg, gg, output),
+        "final",
     )
 
 
@@ -1160,18 +1172,13 @@
     states = decay_log.shape[0]
     rank = step_weight.shape[0]
     selects = rank + 2 * states
+    padded = selects + -selects % lanes
     steps = rows // spans
     count = lax.axis_size("seq")
     row_len = rows // lax.axis_size("row")
     row = lax.axis_index("row")
     col = lax.axis_index("col")
     me = lax.axis_index("seq")
-    my_len = lengths[me][None]
-    my_parent = parents[me][None]
-    my_valid = valid_rows[me][None]
-    me1 = me.astype(jnp.int32)[None]
-    scale = jnp.full((8, lanes), 1.0, F32) * (rows * count / jnp.sum(valid_rows).astype(F32))
-
     def halves(value, axis):
         size = value.shape[axis] // 2
         own = lax.dynamic_slice_in_dim(value, col * size, size, axis)
@@ -1183,7 +1190,7 @@
 
     swap = [(0, 1), (1, 0)]
     tok, toko = halves(tokens_in, 1)
-    tail = lax.dynamic_slice_in_dim(tokens_in, my_len[0] - 8, 8, 0)
+    tail = lax.dynamic_slice_in_dim(tokens_in, lengths[me] - 8, 8, 0)
     w_own, w_send = halves(in_weight, 2)
     wi, wg = w_own[:, 0], w_own[:, 1]
     wi_send, wg_send = w_send[:, 0], w_send[:, 1]
@@ -1194,9 +1201,8 @@
     step_b = rows8(step_bias)
 
     tails, wio, gaino = entry_exchange(tail, wi_send, gain, count)
-    wg_send, ow_send, wio = lax.optimization_barrier((wg_send, ow_send, wio))
+    wg_send, wio = lax.optimization_barrier((wg_send, wio))
     wgo = lax.ppermute(wg_send, "col", swap)
-    owo = lax.ppermute(ow_send, "col", swap)
     tails_own, tails_oth = halves(tails, 2)
 
     hid, hid_tail, ext, act, sel_part = run_kernel(
@@ -1206,13 +1212,15 @@
             struct((2, 8, half), BF16),
             struct((rows + 3 * spans, inner), F32),
             struct((rows, inner), BF16),
-            struct((rows, selects), F32),
+            struct((rows, padded), F32),
         ),
-        (tok, toko, tails_own, tails_oth, gain, gaino, wi, wio, conv_weight, conv_b, select_weight, my_parent),
+        (tok, toko, tails_own, tails_oth, gain, gaino, wi, wio, conv_weight, conv_b, select_weight, parents),
         "forward_in",
         flops=2e9,
     )
     sel = quad_sum(sel_part, 1, "select_sum")
+    ow_send, sel = lax.optimization_barrier((ow_send, sel))
+    owo = lax.ppermute(ow_send, "col", swap)
     delta, step_pre, reach, cum, seg_map = run_kernel(
         forward_ends_kernel,
         (
@@ -1222,7 +1230,7 @@
             struct((spans, inner), F32),
             struct((states + 8, inner), BF16),
         ),
-        (sel, step_weight, step_b, decay_log, act, my_len),
+        (sel, step_weight, step_b, decay_log, act, lengths),
         "forward_ends",
         scratch=[
             pltpu.VMEM((rows, inner), F32),
@@ -1233,7 +1241,7 @@
     )
     table = seq_gather(seg_map, count, 2, "state_gather")
     starts, mixed_pre, gate, mixed, part = run_kernel(
-        forward_out_kernel,
+        functools.partial(forward_out_kernel, rank=rank),
         (
             struct((states, spans, inner), F32),
             struct((rows, inner), F32),
@@ -1242,7 +1250,7 @@
             struct((2, rows, half), BF16),
         ),
         (
-            table, parents, me1, decay_log, reach, cum, delta, act, sel, hid, wg, wgo, skip, ow, owo,
+            table, parents, decay_log, reach, cum, delta, act, sel, hid, wg, wgo, skip, ow, owo,
         ),
         "forward_out",
         scratch=[
@@ -1257,48 +1265,33 @@
     tok_tile = lax.dynamic_slice_in_dim(tok, row * row_len, row_len, 0)
     toko_tile = lax.dynamic_slice_in_dim(toko, row * row_len, row_len, 0)
     teach_tile = lax.dynamic_slice_in_dim(teacher, row * row_len, row_len, 0)
-    output, cot_tile, cot = middle_exchange(part, tok_tile, teach_tile, my_valid, scale)
-    out_part, gate_grad, ig_gate, pre_grad, skip_part, back, flow = run_kernel(
-        backward_in_kernel,
+    output, cot_tile, cot = middle_exchange(part, tok_tile, teach_tile, valid_rows)
+    totals, small, tokens_grad, gain_total = backward_call(
         (
-            struct((2, count, inner // count, half), BF16),
-            struct((rows, inner), BF16),
-            struct((2, count, half // count, inner), BF16),
-            struct((rows, inner), F32),
-            struct((8, inner), F32),
-            struct((states, spans, inner), F32),
-            struct((states, inner), BF16),
+            cot, mixed, ow, owo, gate, mixed_pre,
+            table, parents, lengths, decay_log, starts, cum, delta, act, sel,
+            step_pre, step_weight, select_weight, skip, ext, conv_weight, conv_b, hid, hid_tail,
+            wi, wio, wg, wgo, tok_tile, toko_tile, gain, cot_tile,
         ),
-        (cot, mixed, ow, owo, gate, mixed_pre, act, skip, sel, delta, decay_log, cum, hid),
-        "backward_in",
-        scratch=[
-            pltpu.VMEM((rows, states * lanes), F32),
-            pltpu.VMEM((states, spans, inner), F32),
-        ],
-        flops=4e9,
-    )
-    out_grad, in_both, tokens_grad, gain_grad, step_grad, decay_grad, select_grad, small = backward_call(
-        (
-            table, flow, parents, lengths, decay_log, starts, back, cum, delta, act, sel, pre_grad,
-            step_pre, step_weight, select_weight, skip, ext, conv_weight, conv_b, hid, hid_tail,
-            wi, wio, wg, wgo, gate_grad, tok_tile, toko_tile, gain, cot_tile, out_part, ig_gate, skip_part,
-        ),
-        count, rows, width, inner, states, rank, selects,
-    )
+        count, rows, width, inner, states, rank, selects, padded,
+    )
+    (
+        output, tokens_grad, gain_grad, in_both, conv_grad, conv_bias_grad, select_grad, step_grad,
+        step_bias_grad, decay_grad, skip_grad, out_grad,
+    ) = final_call(totals, small, tokens_grad, gain_total, output, rank, states, selects)
     in_grad = in_both.reshape(half, -1, 2, lanes).transpose(0, 2, 1, 3).reshape(half, 2, -1)
-    conv_grad, conv_bias_grad, skip_grad, step_bias_grad = small[:4], small[4:5], small[5:6], small[6:7]
     return (
         output,
         tokens_grad,
-        gain_grad[0],
+        gain_grad,
         in_grad,
         conv_grad,
-        conv_bias_grad[0],
-        select_grad.T,
+        conv_bias_grad,
+        select_grad,
         step_grad,
-        step_bias_grad[0],
+        step_bias_grad,
         decay_grad,
-        skip_grad[0],
+        skip_grad,
         out_grad,
     )
 

time: 272 us -> 251 us (0.923)
  local copies, waits for them, and re-layouts: 36.4 us -> 22.5 us
  Pallas kernels: 229 us -> 224 us
    unnamed x38 -> x22, local copies, waits for them, and re-layouts: 13.4 us -> 4.52 us
    pallas_call x9, Pallas kernels: 229 us -> 224 us  [run_kernel(): pl.pallas_call(kernel, out_shape=outs, in_specs=[smem_spec() if a.dtype =...]
    slice x3 -> x0, local copies, waits for them, and re-layouts: 4.03 us -> none  [the longest x1 1.42 us: on_device(): small[5:6]]
  transfers between devices with their start and end apart: 2 -> 2, of which waited for: 0 -> 0; matrix products, arithmetic and copies ran while one was open for 3% -> 4% of each run, Pallas kernels for 14% -> 13%
where the time goes in v4:
time: 251 us; the launch traced here: 250 us
  Pallas kernels  224 us (89%)
  local copies, waits for them, and re-layouts  22.5 us (9%)
    pallas_call x9, Pallas kernels, run_kernel(): pl.pallas_call(kernel, out_shape=outs, in_specs=[smem_spec() if a.dtype =...  224 us
    slice x1, local copies, waits for them, and re-layouts, on_device(): wi, wg = (w_own[:, 0], w_own[:, 1])  6.52 us
  transfers between devices with their start and end apart: 2, of which 0 were waited for; matrix products, arithmetic and copies ran while one was open for 4% of the time, Pallas kernels for 13%

profile of v4, /device:TPU:0, one launch (start us, length us, event | category | flops | bytes accessed | tf_op | source)
XLA Modules:
  0.0 250.2 jit_solution(12373253620594411974)
XLA Ops:
  0.7 1.2 dynamic_slice.42
  3.2 1.3 constant_dynamic-slice_fusion.8.tail_ref
  4.5 6.5 %constant_dynamic-slice_fusion.4 = (bf16[512,1,512]{2,1,0:T(2,128)(2,1)S(1)}, bf16[512,1,512]{2,1,0:T(2,128)(2,1)S(1)}, bf16[512,1,512]{2,1,0:T(2,128)(2,1)S(1)}, bf16[512,1,512]{2,1,0:T(2,128)(2,1)S(1)}) fusion(bf16[512,2,1024]{2,1,0:T(2,128)(2,1)} %param.18, s32[]{:T(128)S(6)} %add.40, s32[]{:T(128)S(6)} %select_n.30, s32[]{:T(128)S(6)} %select_n.29), kind=kLoop, calls=%fused_computation.8 | loop fusion | bytes 4194316 | tf_op jit(solution)/shard_map/slice | solution.py:1195
  11.1 0.0 copy-start.4
  11.1 0.0 copy-start
  11.1 1.2 copy_bitcast_fusion.1
  12.3 0.6 broadcast_in_dim.8.gain_ref
  12.9 21.5 %entry_exchange.1 = (bf16[8,8,1024]{2,1,0:T(8,128)(2,1)}, bf16[512,512]{1,0:T(8,128)(2,1)}, bf16[8,512]{1,0:T(8,128)(2,1)}) custom-call(bf16[8,1024]{1,0:T(8,128)(2,1)} %constant_dynamic-slice_fusion.8.tail_ref, bf16[512,512]{1,0:T(8,128)(2,1)} %get-tuple-element.119.wi_ref, bf16[8,512]{1,0:T(8,128)(2,1)} %broadcast_in_dim.8.gain_ref), custom_call_target="tpu_custom_call" | custom-call | bytes 548864 | tf_op jit(solution)/shard_map/entry_exchange/pallas_call | solution.py:101
  34.4 0.6 collective-permute-start
  35.0 1.1 constant_dynamic-slice_fusion.9
  36.1 0.8 copy.29.sw_ref
  36.9 2.2 constant_dynamic-slice_fusion.3
  39.1 0.9 copy.44
  40.0 0.7 constant_dynamic-slice_fusion.5
  40.7 0.6 broadcast_in_dim.9.cb_ref
  41.3 4.9 %forward_in.1 = (bf16[2,512,512]{2,1,0:T(8,128)(2,1)}, bf16[2,8,512]{2,1,0:T(8,128)(2,1)}, f32[536,512]{1,0:T(8,128)}, bf16[512,512]{1,0:T(8,128)(2,1)}, f32[512,128]{1,0:T(8,128)}) custom-call(bf16[512,512]{1,0:T(8,128)(2,1)} %get-tuple-element.115.tok_ref, bf16[512,512]{1,0:T(8,128)(2,1)} %get-tuple-element.114.toko_ref, ...), custom_call_target="tpu_custom_call" | custom-call | flops 2000000000 | bytes 2355232 | tf_op jit(solution)/shard_map/forward_in/pallas_call | solution.py:101
  46.2 9.0 %select_sum.1.sel_ref = f32[512,128]{1,0:T(8,128)} custom-call(f32[512,128]{1,0:T(8,128)} %get-tuple-element.57.x_ref), custom_call_target="tpu_custom_call" | custom-call | bytes 262144 | tf_op jit(solution)/shard_map/select_sum/pallas_call | solution.py:101
  55.2 1.6 collective-permute-start.1
  56.7 0.9 copy.43
  57.7 0.6 broadcast_in_dim.10.tb_ref
  58.3 9.2 %forward_ends.1 = (f32[512,512]{1,0:T(8,128)}, f32[512,512]{1,0:T(8,128)}, f32[16,8,512]{2,1,0:T(8,128)}, f32[8,512]{1,0:T(8,128)}, bf16[24,512]{1,0:T(8,128)(2,1)}) custom-call(f32[512,128]{1,0:T(8,128)} %select_sum.1.sel_ref, bf16[64,512]{1,0:T(8,128)(2,1)} %tw_ref.3, bf16[8,512]{1,0:T(8,128)(2,1)} %broadcast_in_dim.10.tb_ref, f32[16,512]{1,0:T(8,128)} %dl_ref.5, ...), custom_call_target="tpu_custom_call" | custom-call | flops 2000000000 | bytes 892960 | tf_op jit(solution)/shard_map/forward_ends/pallas_call | solution.py:101
  67.4 8.3 %state_gather.1.table_ref = bf16[8,24,512]{2,1,0:T(8,128)(2,1)} custom-call(bf16[24,512]{1,0:T(8,128)(2,1)} %get-tuple-element.60.x_ref), custom_call_target="tpu_custom_call" | custom-call | bytes 24576 | tf_op jit(solution)/shard_map/state_gather/pallas_call | solution.py:101
  75.7 1.2 fusion
  76.9 0.0 collective-permute-done.wgo_ref
  76.9 0.0 collective-permute-done.1.owo_ref
  76.9 0.6 broadcast_in_dim.11.skip_ref
  77.6 0.1 copy-done.8
  77.7 13.4 %forward_out.1 = (f32[16,8,512]{2,1,0:T(8,128)}, f32[512,512]{1,0:T(8,128)}, f32[512,512]{1,0:T(8,128)}, bf16[512,512]{1,0:T(8,128)(2,1)}, bf16[2,512,512]{2,1,0:T(8,128)(2,1)}) custom-call(bf16[8,24,512]{2,1,0:T(8,128)(2,1)} %state_gather.1.table_ref, s32[8]{0:T(128)} %parents_ref.3, f32[16,512]{1,0:T(8,128)} %dl_ref.5, ...), custom_call_target="tpu_custom_call" | custom-call | flops 4000000000 | bytes 5496864 | tf_op jit(solution)/shard_map/forward_out/pallas_call | solution.py:101
  91.2 21.0 %middle_exchange.1 = (bf16[256,512]{1,0:T(8,128)(2,1)}, f32[256,512]{1,0:T(8,128)}, bf16[2,512,512]{2,1,0:T(8,128)(2,1)}) custom-call(bf16[2,512,512]{2,1,0:T(8,128)(2,1)} %get-tuple-element.67.part_ref, bf16[256,512]{1,0:T(8,128)(2,1)} %get-tuple-element.111.tok_ref, bf16[256,512]{1,0:T(8,128)(2,1)} %get-tuple-element.120.teach_ref, s32[8]{0:T(128)} %ints_ref.5), custom_call_target="tpu_custom_call" | custom-call | bytes 1572896 | tf_op jit(solution)/shard_map/middle_exchange/pallas_call | solution.py:101
  112.2 129.8 %backward.1 = (bf16[6,8,64,512]{3,2,1,0:T(8,128)(2,1)}, f32[8,24,512]{2,1,0:T(8,128)}, f32[256,512]{1,0:T(8,128)}, f32[8,512]{1,0:T(8,128)}) custom-call(bf16[2,512,512]{2,1,0:T(8,128)(2,1)} %get-tuple-element.68.cotangent_ref, bf16[512,512]{1,0:T(8,128)(2,1)} %get-tuple-element.69.mixed_ref, bf16[512,512]{1,0:T(8,128)(2,1)} %get-tuple-element.112.ow_ref, ...), custom_call_target="tpu_custom_call" | custom-call | flops 16000000000 | bytes 13611072 | tf_op jit(solution)/shard_map/backward/pallas_call | solution.py:101
  242.0 6.4 %final.1 = (bf16[256,512]{1,0:T(8,128)(2,1)}, f32[256,512]{1,0:T(8,128)}, f32[512]{0:T(512)}, f32[8192,128]{1,0:T(8,128)}, f32[4,512]{1,0:T(4,128)}, /*index=5*/...) custom-call(bf16[6,8,64,512]{3,2,1,0:T(8,128)(2,1)} %get-tuple-eleme, ...), custom_call_target="tpu_custom_call" | custom-call | bytes 4341760 | tf_op jit(solution)/shard_map/final/pallas_call | solution.py:101
  248.5 1.8 copy.32
  (15 shorter events, 0.0 us)
Async XLA Ops:
  11.1 1.3 copy-start.4
  11.1 24.0 %copy-start = (bf16[512,1024]{1,0:T(8,128)(2,1)S(1)}, bf16[512,1024]{1,0:T(8,128)(2,1)}, u32[]{:S(2)}) copy-start(bf16[512,1024]{1,0:T(8,128)(2,1)} %param.15) | copy-start | bytes 3145732
  12.3 23.8 %copy-start.3 = (bf16[512,96]{0,1:T(8,128)(2,1)S(1)}, bf16[512,96]{0,1:T(8,128)(2,1)}, u32[]{:S(2)}) copy-start(bf16[512,96]{0,1:T(8,128)(2,1)} %param.21) | copy-start | bytes 294916
  34.4 42.5 %collective-permute-start = (bf16[512,512]{1,0:T(8,128)(2,1)}, bf16[512,512]{1,0:T(8,128)(2,1)}, u32[]{:S(2)}, u32[]{:S(2)}) collective-permute-start(bf16[512,512]{1,0:T(8,128)(2,1)} %get-tuple-element.65), channel_id=1, source_target_pairs={{0,1},{1,0},{2,3},{3,2},{4,5},{5,4},{6,7},{7,6},{8,9},{9,8},{10,11... | collective-permute-start | bytes 1572872 | tf_op jit(solution)/shard_map/ppermute | solution.py:1205
  36.1 3.9 %copy-start.1 = (bf16[8,8,1024]{2,1,0:T(8,128)(2,1)S(1)}, bf16[8,8,1024]{2,1,0:T(8,128)(2,1)}, u32[]{:S(2)}) copy-start(bf16[8,8,1024]{2,1,0:T(8,128)(2,1)} %get-tuple-element.53) | copy-start | bytes 393220
  36.1 4.6 %copy-start.5 = (bf16[512]{0:T(512)(128)(2,1)S(1)}, bf16[512]{0:T(512)(128)(2,1)}, u32[]{:S(2)}) copy-start(bf16[512]{0:T(512)(128)(2,1)} %param.20) | copy-start | bytes 3076
  46.2 11.4 %copy-start.6 = (bf16[512]{0:T(512)(128)(2,1)S(1)}, bf16[512]{0:T(512)(128)(2,1)}, u32[]{:S(2)}) copy-start(bf16[512]{0:T(512)(128)(2,1)} %param.23) | copy-start | bytes 3076
  55.2 21.7 %collective-permute-start.1 = (bf16[512,512]{1,0:T(8,128)(2,1)}, bf16[512,512]{1,0:T(8,128)(2,1)S(1)}, u32[]{:S(2)}, u32[]{:S(2)}) collective-permute-start(bf16[512,512]{1,0:T(8,128)(2,1)} %get-tuple-element.66), channel_id=1, source_target_pairs={{0,1},{1,0},{2,3},{3,2},{4,5},{5,4},{6,7},{7,6},{8,9},{9,8},{10,11... | collective-permute-start | bytes 1572872 | tf_op jit(solution)/shard_map/ppermute | solution.py:1223
  58.2 17.5 %copy-start.2 = (bf16[512,512]{1,0:T(8,128)(2,1)S(1)}, bf16[512,512]{1,0:T(8,128)(2,1)}, u32[]{:S(2)}) copy-start(bf16[512,512]{1,0:T(8,128)(2,1)} %param.16) | copy-start | bytes 1572868
  58.2 18.7 %copy-start.7 = (bf16[512]{0:T(512)(128)(2,1)S(1)}, bf16[512]{0:T(512)(128)(2,1)}, u32[]{:S(2)}) copy-start(bf16[512]{0:T(512)(128)(2,1)} %param.25) | copy-start | bytes 3076
  76.9 0.8 copy-start.8

commit v5 on v4

--- a/solution.py
+++ b/solution.py
@@ -16,7 +16,7 @@
 log2e = 1.4426950408889634
 vmem_bytes = 60 * 1024 * 1024
 vmem_most = 67043328
-chunk_plan = (False, True, False, True, False, False)
+chunk_plan = (False, True, False, True, False, True, False, True)
 
 
 def vmem_spec():
@@ -746,10 +746,16 @@
             a, b = place_of(first // 8 + j)
             small_ref[a, b, :] = value[j * 8 : (j + 1) * 8]
 
-    sources = [og_ref.at[0], og_ref.at[1], igg_ref.at[0], igg_ref.at[1], igi_ref.at[0], igi_ref.at[1]]
+    split = inner // 2
+    sources = [og_ref.at[0], og_ref.at[1], igg_ref.at[0], igg_ref.at[1]]
+    targets = [totals.at[i] for i in range(4)]
+    for part in range(2):
+        for h in range(2):
+            sources.append(igi_ref.at[h, :, :, pl.ds(part * split, split)])
+            targets.append(totals.at[4 + h, :, :, pl.ds(part * split, split)])
     chunks = [
         Chunk(
-            source, totals.at[i], landings[i], send.at[i], recv.at[i],
+            source, targets[i], landings[i], send.at[i], recv.at[i],
             stages_of(count, chunk_plan[i]), i % 2 == 1,
         )
         for i, source in enumerate(sources)
@@ -765,10 +771,14 @@
     def b_at(n, step):
         return ig_out[pl.ds(pl.multiple_of(n * rows + step * spans, spans), spans), :]
 
-    c0, c1, c2, c3, c4, c5 = chunks
-    early = {2: (c0, c1), -1: (c2, c3)}
+    c0, c1, c2, c3 = chunks[:4]
+    inners = chunks[4:]
+    late = {
+        1: (c1, c3, c0), 2: tuple(inners[:2]), 3: tuple(inners[2:]) + (c2,), 4: tuple(inners[:2]) + (c1, c3),
+        5: tuple(inners[2:]) + (small_chunk,), 6: tuple(inners) + (c1, c3, small_chunk),
+    }
     pumps = {
-        (1, 0): (c0, c1), (2, 0): (c2, c3), (2, 1): (c1,), (3, 0): (c0, c3), (3, 1): (c1,),
+        (0, 0): (c0, c1), (1, 0): (c2, c3), (2, 0): (c1,), (2, 1): (c0,), (3, 0): (c3,), (3, 1): (c2,),
     }
     from_tokens = to_steps(rows, steps)
     cot = dot(from_tokens, cotangent_ref[0]).astype(BF16)
@@ -803,7 +813,6 @@
                 out.append(a * (c_ref[step_ds(step), n * lanes : (n + 1) * lanes] * p + carry[n]))
             return tuple(out)
 
-        advance_all(early.get(group, ()))
         ends = lax.fori_loop(0, steps, fall, (jnp.zeros((spans, lanes), F32),) * states)
         for n in range(states):
             back_ref[n, :, here] = ends[n]
@@ -825,7 +834,6 @@
     ).astype(BF16)
 
     flow_copies = to_all(flow_ref, flows_ref, flow_send, flow_recv)
-    advance_all(early.get(-1, ()))
     rate = -jnp.exp(dl_ref[...]) * log2e
     sel = sel_ref[...]
     drive[...] = delta_ref[...] * act_ref[...].astype(F32)
@@ -929,7 +937,7 @@
         axis=1,
     )
     first = pair_copy(0, sel_part, sel_row, row_peer())
-    advance_all((c2, c3, c0, c1))
+    advance_all((c1,))
     bias_sum = jnp.sum(step_pre_grad, axis=0, keepdims=True)
     small_store(0, dot_tn(sel[:, :rank].astype(BF16), low))
     small_store(rank, dgrad_ref[...])
@@ -944,7 +952,7 @@
     pre = conv_pre(ext_ref, cw_ref, cb_ref, rows, inner)
     slope = slope_of(pre, sigmoid(pre))
     base_grad = agrad_ref[...] + skip_ref[0:1, :].astype(F32) * pgrad_ref[...]
-    advance_all((c3,))
+    advance_all((c0, c3))
     second.wait()
     selg = (sel_part[...] + sel_col[...].astype(F32)).astype(BF16)[:, :selects]
     conv_in = (base_grad + dot_nt(selg, sw_ref[...])) * slope
@@ -957,9 +965,6 @@
             line = line + taps[k : k + 1, :] * conv_in[(i - k) * spans : (i - k) * spans + 1, :]
         tails.append(line * (parents_ref[me] >= 0).astype(F32))
     tail_low = jnp.concatenate(tails, axis=0).astype(BF16)
-    for h, wi in enumerate((wi_ref, wio_ref)):
-        tpart_ref[h] = dot_nt(tail_low, wi[...])
-    tail_first = pair_copy(2, tpart_ref, tail_row, row_peer())
     last_span = lax.broadcasted_iota(jnp.int32, (spans, inner), 0) == spans - 1
     for j in range(3):
         slab = jnp.roll(conv_in[j * spans : (j + 1) * spans], -1, axis=0)
@@ -968,6 +973,13 @@
     for k in range(4):
         inner_grad = inner_grad + taps[k : k + 1, :] * cig_ref[(3 - k) * spans : (3 - k) * spans + rows, :]
     inner_low = inner_grad.astype(BF16)
+    for h in range(2):
+        store_split(igi_ref.at[h], dot_tn(hid_ref[h], inner_low) + dot_tn(hidt_ref[h], tail_low))
+    advance_all(inners)
+    for h, wi in enumerate((wi_ref, wio_ref)):
+        tpart_ref[h] = dot_nt(tail_low, wi[...])
+    tail_first = pair_copy(2, tpart_ref, tail_row, row_peer())
+    advance_all(late[1])
     natural = dot(order, inner_low).astype(BF16)
     hid_copies = []
     for h, wi in ((1, wio_ref), (0, wi_ref)):
@@ -984,9 +996,7 @@
         part_ref[1, pl.ds(mine, half), :].astype(F32) + hid_row[1].astype(F32)
     ).astype(BF16)
     hid_second = pair_copy(6, hid_low, hid_col, col_peer())
-    for h in range(2):
-        store_split(igi_ref.at[h], dot_tn(hid_ref[h], inner_low) + dot_tn(hidt_ref[h], tail_low))
-    advance_all((c4, c5, c2, c1, c3))
+    advance_all(late[2])
     tail_second.wait()
     tail_own[...] = tail_sum[0] + tail_col[...]
     tail_copies = to_all(tail_own, tails_ref, tail_send, tail_recv)
@@ -1004,9 +1014,10 @@
         a, b = place_of(at)
         small_ref[a, b, :] = jnp.zeros((8, inner), F32)
     small_chunk.next()
+    advance_all(late[3])
     hid_copies[1].wait()
     hidden = part_ref[0, pl.ds(mine, half), :].astype(F32) + hid_row[0].astype(F32)
-    advance_all((c0, c4))
+    advance_all(late[4])
 
     tok = tok_ref[...].astype(F32)
     toko = toko_ref[...].astype(F32)
@@ -1035,7 +1046,7 @@
     mean_copy = pair_copy(7, mean_out, mean_in, col_peer())
     gain_out[...] = jnp.broadcast_to(jnp.sum(hidden * normed, axis=0, keepdims=True), gain_out.shape)
     gain_copy = pair_copy(8, gain_out, gain_in, row_peer())
-    advance_all((c5, small_chunk))
+    advance_all(late[5])
     gain_copy.wait()
     gain_out[...] = gain_out[...] + gain_in[...]
     gain_copies = to_all(gain_out, gains_ref, gain_send, gain_recv)
@@ -1046,7 +1057,7 @@
     )
     mean = (mean + apart[:, 0:1]) / width
     tg_ref[...] = cot_ref[...] + inv * (scaled - normed * mean)
-    advance_all((c4, small_chunk, c5))
+    advance_all(late[6])
     for copy in gain_copies:
         copy.wait()
     gain_total = gains_ref[0]
@@ -1086,10 +1097,11 @@
         sizes, copies = stage_sizes(stages_of(count, paired), count, i % 2 == 1)
         most = max(most, copies)
         scratch += [
-            vm(size + ((small, inner) if last else (block_rows, inner)), f32 if last else bf16) for size in sizes
+            vm(size + ((small, inner) if last else (block_rows, inner if i < 4 else inner // 2)), f32 if last else bf16)
+            for size in sizes
         ]
     dma = pltpu.SemaphoreType.DMA
-    scratch += [dma((7, most))] * 2 + [dma((9,))] * 2 + [dma((count,))] * 6
+    scratch += [dma((len(chunk_plan) + 1, most))] * 2 + [dma((9,))] * 2 + [dma((count,))] * 6
     return run_kernel(
         functools.partial(backward_kernel, width=width),
         (

time: 251 us -> 230 us (0.916)
  Pallas kernels: 224 us -> 203 us
    pallas_call x9, Pallas kernels: 224 us -> 203 us  [run_kernel(): pl.pallas_call(kernel, out_shape=outs, in_specs=[smem_spec() if a.dtype =...]
  transfers between devices with their start and end apart: 2 -> 2, of which waited for: 0 -> 0; matrix products, arithmetic and copies ran while one was open for 4% -> 4% of each run, Pallas kernels for 13% -> 14%
where the time goes in v5:
time: 230 us
  Pallas kernels  203 us (88%)
  local copies, waits for them, and re-layouts  22.5 us (10%)
    pallas_call x9, Pallas kernels, run_kernel(): pl.pallas_call(kernel, out_shape=outs, in_specs=[smem_spec() if a.dtype =...  203 us
    slice x1, local copies, waits for them, and re-layouts, on_device(): wi, wg = (w_own[:, 0], w_own[:, 1])  6.52 us
  transfers between devices with their start and end apart: 2, of which 0 were waited for; matrix products, arithmetic and copies ran while one was open for 4% of the time, Pallas kernels for 14%

profile of v5, /device:TPU:0, one launch (start us, length us, event | category | flops | bytes accessed | tf_op | source)
XLA Modules:
  0.0 229.5 jit_solution(8231017008008125630)
XLA Ops:
  0.7 1.2 dynamic_slice.42
  3.2 1.4 constant_dynamic-slice_fusion.8.tail_ref
  4.6 6.5 %constant_dynamic-slice_fusion.4 = (bf16[512,1,512]{2,1,0:T(2,128)(2,1)S(1)}, bf16[512,1,512]{2,1,0:T(2,128)(2,1)S(1)}, bf16[512,1,512]{2,1,0:T(2,128)(2,1)S(1)}, bf16[512,1,512]{2,1,0:T(2,128)(2,1)S(1)}) fusion(bf16[512,2,1024]{2,1,0:T(2,128)(2,1)} %param.18, s32[]{:T(128)S(6)} %add.40, s32[]{:T(128)S(6)} %select_n.30, s32[]{:T(128)S(6)} %select_n.29), kind=kLoop, calls=%fused_computation.8 | loop fusion | bytes 4194316 | tf_op jit(solution)/shard_map/slice | solution.py:1207
  11.1 0.0 copy-start.4
  11.1 0.0 copy-start
  11.1 1.2 copy_bitcast_fusion.1
  12.4 0.6 broadcast_in_dim.8.gain_ref
  13.0 21.4 %entry_exchange.1 = (bf16[8,8,1024]{2,1,0:T(8,128)(2,1)}, bf16[512,512]{1,0:T(8,128)(2,1)}, bf16[8,512]{1,0:T(8,128)(2,1)}) custom-call(bf16[8,1024]{1,0:T(8,128)(2,1)} %constant_dynamic-slice_fusion.8.tail_ref, bf16[512,512]{1,0:T(8,128)(2,1)} %get-tuple-element.119.wi_ref, bf16[8,512]{1,0:T(8,128)(2,1)} %broadcast_in_dim.8.gain_ref), custom_call_target="tpu_custom_call" | custom-call | bytes 548864 | tf_op jit(solution)/shard_map/entry_exchange/pallas_call | solution.py:101
  34.4 0.6 collective-permute-start
  35.0 1.1 constant_dynamic-slice_fusion.9
  36.1 0.8 copy.29.sw_ref
  36.9 2.2 constant_dynamic-slice_fusion.3
  39.1 0.9 copy.44
  40.0 0.7 constant_dynamic-slice_fusion.5
  40.7 0.6 broadcast_in_dim.9.cb_ref
  41.3 4.9 %forward_in.1 = (bf16[2,512,512]{2,1,0:T(8,128)(2,1)}, bf16[2,8,512]{2,1,0:T(8,128)(2,1)}, f32[536,512]{1,0:T(8,128)}, bf16[512,512]{1,0:T(8,128)(2,1)}, f32[512,128]{1,0:T(8,128)}) custom-call(bf16[512,512]{1,0:T(8,128)(2,1)} %get-tuple-element.115.tok_ref, bf16[512,512]{1,0:T(8,128)(2,1)} %get-tuple-element.114.toko_ref, ...), custom_call_target="tpu_custom_call" | custom-call | flops 2000000000 | bytes 2355232 | tf_op jit(solution)/shard_map/forward_in/pallas_call | solution.py:101
  46.2 9.0 %select_sum.1.sel_ref = f32[512,128]{1,0:T(8,128)} custom-call(f32[512,128]{1,0:T(8,128)} %get-tuple-element.57.x_ref), custom_call_target="tpu_custom_call" | custom-call | bytes 262144 | tf_op jit(solution)/shard_map/select_sum/pallas_call | solution.py:101
  55.2 1.6 collective-permute-start.1
  56.7 0.9 copy.43
  57.7 0.6 broadcast_in_dim.10.tb_ref
  58.3 9.2 %forward_ends.1 = (f32[512,512]{1,0:T(8,128)}, f32[512,512]{1,0:T(8,128)}, f32[16,8,512]{2,1,0:T(8,128)}, f32[8,512]{1,0:T(8,128)}, bf16[24,512]{1,0:T(8,128)(2,1)}) custom-call(f32[512,128]{1,0:T(8,128)} %select_sum.1.sel_ref, bf16[64,512]{1,0:T(8,128)(2,1)} %tw_ref.3, bf16[8,512]{1,0:T(8,128)(2,1)} %broadcast_in_dim.10.tb_ref, f32[16,512]{1,0:T(8,128)} %dl_ref.5, ...), custom_call_target="tpu_custom_call" | custom-call | flops 2000000000 | bytes 892960 | tf_op jit(solution)/shard_map/forward_ends/pallas_call | solution.py:101
  67.4 8.3 %state_gather.1.table_ref = bf16[8,24,512]{2,1,0:T(8,128)(2,1)} custom-call(bf16[24,512]{1,0:T(8,128)(2,1)} %get-tuple-element.60.x_ref), custom_call_target="tpu_custom_call" | custom-call | bytes 24576 | tf_op jit(solution)/shard_map/state_gather/pallas_call | solution.py:101
  75.7 1.2 fusion
  76.9 0.0 collective-permute-done.wgo_ref
  76.9 0.0 collective-permute-done.1.owo_ref
  76.9 0.6 broadcast_in_dim.11.skip_ref
  77.6 0.1 copy-done.8
  77.7 13.4 %forward_out.1 = (f32[16,8,512]{2,1,0:T(8,128)}, f32[512,512]{1,0:T(8,128)}, f32[512,512]{1,0:T(8,128)}, bf16[512,512]{1,0:T(8,128)(2,1)}, bf16[2,512,512]{2,1,0:T(8,128)(2,1)}) custom-call(bf16[8,24,512]{2,1,0:T(8,128)(2,1)} %state_gather.1.table_ref, s32[8]{0:T(128)} %parents_ref.3, f32[16,512]{1,0:T(8,128)} %dl_ref.5, ...), custom_call_target="tpu_custom_call" | custom-call | flops 4000000000 | bytes 5496864 | tf_op jit(solution)/shard_map/forward_out/pallas_call | solution.py:101
  91.2 21.0 %middle_exchange.1 = (bf16[256,512]{1,0:T(8,128)(2,1)}, f32[256,512]{1,0:T(8,128)}, bf16[2,512,512]{2,1,0:T(8,128)(2,1)}) custom-call(bf16[2,512,512]{2,1,0:T(8,128)(2,1)} %get-tuple-element.67.part_ref, bf16[256,512]{1,0:T(8,128)(2,1)} %get-tuple-element.111.tok_ref, bf16[256,512]{1,0:T(8,128)(2,1)} %get-tuple-element.120.teach_ref, s32[8]{0:T(128)} %ints_ref.5), custom_call_target="tpu_custom_call" | custom-call | bytes 1572896 | tf_op jit(solution)/shard_map/middle_exchange/pallas_call | solution.py:101
  112.2 109.2 %backward.1 = (bf16[6,8,64,512]{3,2,1,0:T(8,128)(2,1)}, f32[8,24,512]{2,1,0:T(8,128)}, f32[256,512]{1,0:T(8,128)}, f32[8,512]{1,0:T(8,128)}) custom-call(bf16[2,512,512]{2,1,0:T(8,128)(2,1)} %get-tuple-element.68.cotangent_ref, bf16[512,512]{1,0:T(8,128)(2,1)} %get-tuple-element.69.mixed_ref, bf16[512,512]{1,0:T(8,128)(2,1)} %get-tuple-element.112.ow_ref, ...), custom_call_target="tpu_custom_call" | custom-call | flops 16000000000 | bytes 13611072 | tf_op jit(solution)/shard_map/backward/pallas_call | solution.py:101
  221.4 6.4 %final.1 = (bf16[256,512]{1,0:T(8,128)(2,1)}, f32[256,512]{1,0:T(8,128)}, f32[512]{0:T(512)}, f32[8192,128]{1,0:T(8,128)}, f32[4,512]{1,0:T(4,128)}, /*index=5*/...) custom-call(bf16[6,8,64,512]{3,2,1,0:T(8,128)(2,1)} %get-tuple-eleme, ...), custom_call_target="tpu_custom_call" | custom-call | bytes 4341760 | tf_op jit(solution)/shard_map/final/pallas_call | solution.py:101
  227.8 1.8 copy.32
  (15 shorter events, 0.0 us)
Async XLA Ops:
  11.1 1.3 copy-start.4
  11.1 23.9 %copy-start = (bf16[512,1024]{1,0:T(8,128)(2,1)S(1)}, bf16[512,1024]{1,0:T(8,128)(2,1)}, u32[]{:S(2)}) copy-start(bf16[512,1024]{1,0:T(8,128)(2,1)} %param.15) | copy-start | bytes 3145732
  12.4 23.7 %copy-start.3 = (bf16[512,96]{0,1:T(8,128)(2,1)S(1)}, bf16[512,96]{0,1:T(8,128)(2,1)}, u32[]{:S(2)}) copy-start(bf16[512,96]{0,1:T(8,128)(2,1)} %param.21) | copy-start | bytes 294916
  34.4 42.5 %collective-permute-start = (bf16[512,512]{1,0:T(8,128)(2,1)}, bf16[512,512]{1,0:T(8,128)(2,1)}, u32[]{:S(2)}, u32[]{:S(2)}) collective-permute-start(bf16[512,512]{1,0:T(8,128)(2,1)} %get-tuple-element.65), channel_id=1, source_target_pairs={{0,1},{1,0},{2,3},{3,2},{4,5},{5,4},{6,7},{7,6},{8,9},{9,8},{10,11... | collective-permute-start | bytes 1572872 | tf_op jit(solution)/shard_map/ppermute | solution.py:1217
  36.1 3.9 %copy-start.1 = (bf16[8,8,1024]{2,1,0:T(8,128)(2,1)S(1)}, bf16[8,8,1024]{2,1,0:T(8,128)(2,1)}, u32[]{:S(2)}) copy-start(bf16[8,8,1024]{2,1,0:T(8,128)(2,1)} %get-tuple-element.53) | copy-start | bytes 393220
  36.1 4.6 %copy-start.5 = (bf16[512]{0:T(512)(128)(2,1)S(1)}, bf16[512]{0:T(512)(128)(2,1)}, u32[]{:S(2)}) copy-start(bf16[512]{0:T(512)(128)(2,1)} %param.20) | copy-start | bytes 3076
  46.2 11.4 %copy-start.6 = (bf16[512]{0:T(512)(128)(2,1)S(1)}, bf16[512]{0:T(512)(128)(2,1)}, u32[]{:S(2)}) copy-start(bf16[512]{0:T(512)(128)(2,1)} %param.23) | copy-start | bytes 3076
  55.2 21.7 %collective-permute-start.1 = (bf16[512,512]{1,0:T(8,128)(2,1)}, bf16[512,512]{1,0:T(8,128)(2,1)S(1)}, u32[]{:S(2)}, u32[]{:S(2)}) collective-permute-start(bf16[512,512]{1,0:T(8,128)(2,1)} %get-tuple-element.66), channel_id=1, source_target_pairs={{0,1},{1,0},{2,3},{3,2},{4,5},{5,4},{6,7},{7,6},{8,9},{9,8},{10,11... | collective-permute-start | bytes 1572872 | tf_op jit(solution)/shard_map/ppermute | solution.py:1235
  58.2 17.5 %copy-start.2 = (bf16[512,512]{1,0:T(8,128)(2,1)S(1)}, bf16[512,512]{1,0:T(8,128)(2,1)}, u32[]{:S(2)}) copy-start(bf16[512,512]{1,0:T(8,128)(2,1)} %param.16) | copy-start | bytes 1572868
  58.2 18.7 %copy-start.7 = (bf16[512]{0:T(512)(128)(2,1)S(1)}, bf16[512]{0:T(512)(128)(2,1)}, u32[]{:S(2)}) copy-start(bf16[512]{0:T(512)(128)(2,1)} %param.25) | copy-start | bytes 3076
  76.9 0.8 copy-start.8

commit v6 on v5

--- a/solution.py
+++ b/solution.py
@@ -135,100 +135,6 @@
 
 def col_peer():
     return {"col": 1 - lax.axis_index("col")}
-
-
-def entry_kernel(tail_ref, wi_ref, gain_ref, tails_ref, wo_ref, gain_o_ref, tsend, trecv, csend, crecv):
-    count = tails_ref.shape[0]
-    me = lax.axis_index("seq")
-    peers = [{"seq": lax.rem(me + j, count)} for j in range(1, count)]
-    barrier_with([col_peer()] + peers)
-    copies = []
-    for j, peer in enumerate(peers):
-        copies.append(remote(tail_ref, tails_ref.at[me], tsend.at[j], trecv.at[j], peer))
-    copies.append(remote(gain_ref, gain_o_ref, csend.at[0], crecv.at[0], col_peer()))
-    copies.append(remote(wi_ref, wo_ref, csend.at[1], crecv.at[1], col_peer()))
-    for copy in copies:
-        copy.start()
-    tails_ref[me] = tail_ref[...]
-    for copy in copies:
-        copy.wait()
-
-
-def entry_exchange(tail, wi_send, gain_send, count):
-    return run_kernel(
-        entry_kernel,
-        (
-            struct((count,) + tail.shape, tail.dtype),
-            struct(wi_send.shape, wi_send.dtype),
-            struct(gain_send.shape, gain_send.dtype),
-        ),
-        (tail, wi_send, gain_send),
-        "entry_exchange",
-        scratch=[
-            pltpu.SemaphoreType.DMA((count,)),
-            pltpu.SemaphoreType.DMA((count,)),
-            pltpu.SemaphoreType.DMA((2,)),
-            pltpu.SemaphoreType.DMA((2,)),
-        ],
-        collective=0,
-    )
-
-
-def seq_gather_kernel(x_ref, o_ref, send, recv):
-    count = o_ref.shape[0]
-    me = lax.axis_index("seq")
-    peers = [{"seq": lax.rem(me + j, count)} for j in range(1, count)]
-    barrier_with(peers)
-    copies = [
-        remote(x_ref, o_ref.at[me], send.at[j], recv.at[j], peer) for j, peer in enumerate(peers)
-    ]
-    for copy in copies:
-        copy.start()
-    o_ref[me] = x_ref[...]
-    for copy in copies:
-        copy.wait()
-
-
-def seq_gather(x, count, collective, name):
-    return run_kernel(
-        seq_gather_kernel,
-        struct((count,) + x.shape, x.dtype),
-        (x,),
-        name,
-        scratch=[pltpu.SemaphoreType.DMA((count,)), pltpu.SemaphoreType.DMA((count,))],
-        collective=collective,
-    )
-
-
-def quad_sum_kernel(x_ref, o_ref, from_row, to_col, from_col, send, recv):
-    barrier_with([row_peer(), col_peer()])
-    first = remote(x_ref, from_row, send.at[0], recv.at[0], row_peer())
-    first.start()
-    first.wait()
-    pair = x_ref[...] + from_row[...]
-    to_col[...] = pair.astype(BF16)
-    second = remote(to_col, from_col, send.at[1], recv.at[1], col_peer())
-    second.start()
-    o_ref[...] = pair
-    second.wait()
-    o_ref[...] += from_col[...].astype(F32)
-
-
-def quad_sum(x, collective, name):
-    return run_kernel(
-        quad_sum_kernel,
-        struct(x.shape, F32),
-        (x,),
-        name,
-        scratch=[
-            pltpu.VMEM(x.shape, F32),
-            pltpu.VMEM(x.shape, BF16),
-            pltpu.VMEM(x.shape, BF16),
-            pltpu.SemaphoreType.DMA((2,)),
-            pltpu.SemaphoreType.DMA((2,)),
-        ],
-        collective=collective,
-    )
 
 
 def middle_kernel(
@@ -301,38 +207,114 @@
     )
 
 
-def forward_in_kernel(
-    tok_ref, toko_ref, tails_ref, tailso_ref, gain_ref, gaino_ref, wi_ref, wio_ref,
-    cw_ref, cb_ref, sw_ref, ints_ref,
-    hid_ref, hidt_ref, ext_ref, act_ref, sel_ref,
+def conv_pre(ext_ref, cw_ref, cb_ref, rows, half):
+    taps = cw_ref[...].astype(F32)
+    pre = jnp.broadcast_to(cb_ref[0:1, :].astype(F32), (rows, half))
+    for k in range(4):
+        pre = pre + taps[k : k + 1, :] * ext_ref[k * spans : k * spans + rows, :]
+    return pre
+
+
+def group_ds(group):
+    return pl.ds(pl.multiple_of(group * lanes, lanes), lanes)
+
+
+def step_ds(step):
+    return pl.ds(pl.multiple_of(step * spans, spans), spans)
+
+
+def decay_rows(decay_log_ref, decay_b, scale):
+    states, width = decay_log_ref.shape
+    rate = -jnp.exp(decay_log_ref[...]) * scale
+    for n in range(states):
+        decay_b[n] = jnp.broadcast_to(rate[n : n + 1, :], (spans, width))
+
+
+def span_sum_kernel_part(delta_ref, steps):
+    total = delta_ref[0:spans, :]
+    for s in range(1, steps):
+        total = total + delta_ref[s * spans : (s + 1) * spans, :]
+    return total
+
+
+def segment_sum(table_ref, index, states):
+    block = table_ref[index].astype(F32)
+    return block[:states], block[states : states + 1] + block[states + 1 : states + 2] + block[states + 2 : states + 3]
+
+
+def forward_kernel(
+    tail_ref, wi_send, wg_send, ow_send, gain_ref, tok_ref, toko_ref, wi_ref, wg_ref, ow_ref, cw_ref, cb_ref, sw_ref,
+    tw_ref, tb_ref, dl_ref, skip_ref, parents_ref, lengths_ref,
+    hid_ref, hidt_ref, ext_ref, act_ref, sel_ref, delta_ref, pre_ref, cum_ref, table_ref,
+    wio_ref, wgo_ref, owo_ref, starts_ref, mpre_ref, gate_ref, mixed_ref, part_ref,
+    tails_ref, gaino_ref, sel_row, sel_low, sel_col, drive, b_ref, c_ref, rate_ref, map_ref, reach_ref, finals,
+    pair_send, pair_recv, tail_send, tail_recv, map_send, map_recv,
 ):
+    count = table_ref.shape[0]
     rows, half = tok_ref.shape
     steps = rows // spans
     width = 2 * half
-    above = ints_ref[lax.axis_index("seq")]
+    states = dl_ref.shape[0]
+    rank = tw_ref.shape[0]
+    me = lax.axis_index("seq")
+    col = lax.axis_index("col")
+    peers = [{"seq": lax.rem(me + j, count)} for j in range(1, count)]
+    barrier_with([row_peer(), col_peer()] + peers)
+
+    def pair_copy(at, src, dst, peer):
+        copy = remote(src, dst, pair_send.at[at], pair_recv.at[at], peer)
+        copy.start()
+        return copy
+
+    def to_all(src, dst, sends, recvs):
+        copies = [
+            remote(src, dst.at[me], sends.at[j], recvs.at[j], peer) for j, peer in enumerate(peers)
+        ]
+        for copy in copies:
+            copy.start()
+        dst[me] = src[...]
+        return copies
+
+    gain_copy = pair_copy(0, gain_ref, gaino_ref, col_peer())
+    wi_copy = pair_copy(1, wi_send, wio_ref, col_peer())
+    tail_copies = to_all(tail_ref, tails_ref, tail_send, tail_recv)
+    quarter = half // 2
+    first_part, second_part = pl.ds(0, quarter), pl.ds(quarter, quarter)
+    wg_first = pair_copy(2, wg_send.at[first_part], wgo_ref.at[first_part], col_peer())
+
+    above = parents_ref[me]
     parent = jnp.maximum(above, 0)
     present = (above >= 0).astype(F32)
-    gain = gain_ref[0:1, :].astype(F32)
-    gaino = gaino_ref[0:1, :].astype(F32)
 
     def hidden_of(own, other):
         own = own.astype(F32)
         other = other.astype(F32)
         total = jnp.sum(own * own, axis=1, keepdims=True) + jnp.sum(other * other, axis=1, keepdims=True)
         inv = lax.rsqrt(total / width + norm_epsilon)
+        gain = gain_ref[0:1, :].astype(F32)
+        gaino = gaino_ref[0:1, :].astype(F32)
         return (own * inv * gain).astype(BF16), (other * inv * gaino).astype(BF16)
 
+    gain_copy.wait()
     hid, hido = hidden_of(tok_ref[...], toko_ref[...])
     order = to_steps(rows, steps)
     hid = dot(order, hid).astype(BF16)
     hido = dot(order, hido).astype(BF16)
     hid_ref[0] = hid
     hid_ref[1] = hido
-    inner = dot(hid, wi_ref[...]) + dot(hido, wio_ref[...])
-    tail, tailo = hidden_of(tails_ref[parent], tailso_ref[parent])
+    ext_ref[3 * spans :, :] = dot(hid, wi_ref[...])
+    decay_rows(dl_ref, rate_ref, log2e)
+    for copy in tail_copies:
+        copy.wait()
+    own_at = pl.ds(pl.multiple_of(col * half, half), half)
+    other_at = pl.ds(pl.multiple_of((1 - col) * half, half), half)
+    tail, tailo = hidden_of(tails_ref[parent, :, own_at], tails_ref[parent, :, other_at])
     hidt_ref[0] = tail
     hidt_ref[1] = tailo
-    tail_inner = (dot(tail, wi_ref[...]) + dot(tailo, wio_ref[...])) * present
+    tail_inner = dot(tail, wi_ref[...])
+    wi_copy.wait()
+    inner = ext_ref[3 * spans :, :] + dot(hid_ref[1], wio_ref[...])
+    tail_inner = (tail_inner + dot(tailo, wio_ref[...])) * present
     last = inner[rows - 3 * spans :]
     first_span = lax.broadcasted_iota(jnp.int32, (spans, half), 0) == 0
     for j in range(3):
@@ -341,59 +323,24 @@
             first_span, jnp.broadcast_to(tail_inner[5 + j : 6 + j, :], (spans, half)), block
         )
     ext_ref[3 * spans :, :] = inner
-    taps = cw_ref[...].astype(F32)
-    pre = jnp.broadcast_to(cb_ref[0:1, :].astype(F32), (rows, half))
-    for k in range(4):
-        pre = pre + taps[k : k + 1, :] * ext_ref[k * spans : k * spans + rows, :]
+    pre = conv_pre(ext_ref, cw_ref, cb_ref, rows, half)
     act = (pre * sigmoid(pre)).astype(BF16)
     act_ref[...] = act
     chosen = dot(act, sw_ref[...])
     sel_ref[...] = jnp.concatenate(
         [chosen, jnp.zeros((rows, sel_ref.shape[1] - chosen.shape[1]), F32)], axis=1
     )
-
-
-def conv_pre(ext_ref, cw_ref, cb_ref, rows, half):
-    taps = cw_ref[...].astype(F32)
-    pre = jnp.broadcast_to(cb_ref[0:1, :].astype(F32), (rows, half))
-    for k in range(4):
-        pre = pre + taps[k : k + 1, :] * ext_ref[k * spans : k * spans + rows, :]
-    return pre
-
-
-def group_ds(group):
-    return pl.ds(pl.multiple_of(group * lanes, lanes), lanes)
-
-
-def step_ds(step):
-    return pl.ds(pl.multiple_of(step * spans, spans), spans)
-
-
-def decay_rows(decay_log_ref, decay_b, scale):
-    states, width = decay_log_ref.shape
-    rate = -jnp.exp(decay_log_ref[...]) * scale
-    for n in range(states):
-        decay_b[n] = jnp.broadcast_to(rate[n : n + 1, :], (spans, width))
-
-
-def span_sum_kernel_part(delta_ref, steps):
-    total = delta_ref[0:spans, :]
-    for s in range(1, steps):
-        total = total + delta_ref[s * spans : (s + 1) * spans, :]
-    return total
-
-
-def forward_ends_kernel(
-    sel_ref, tw_ref, tb_ref, dl_ref, act_ref, ints_ref,
-    delta_ref, pre_ref, reach_ref, cum_ref, send_ref,
-    drive, b_ref, rate_ref,
-):
-    rows, width = act_ref.shape
-    steps = rows // spans
-    states = dl_ref.shape[0]
-    rank = tw_ref.shape[0]
-    length = ints_ref[lax.axis_index("seq")]
-    sel = sel_ref[...]
+    across = pair_copy(3, sel_ref, sel_row, row_peer())
+    across.wait()
+    pair = sel_ref[...] + sel_row[...]
+    sel_low[...] = pair.astype(BF16)
+    beside = pair_copy(4, sel_low, sel_col, col_peer())
+    wg_second = pair_copy(5, wg_send.at[second_part], wgo_ref.at[second_part], col_peer())
+    ow_copy = pair_copy(6, ow_send, owo_ref, col_peer())
+    beside.wait()
+    sel = pair + sel_col[...].astype(F32)
+    sel_ref[...] = sel
+    length = lengths_ref[me]
     step_pre = dot(sel[:, :rank].astype(BF16), tw_ref[...]) + tb_ref[0:1, :].astype(F32)
     pre_ref[...] = step_pre
     live = (step_tokens(rows, steps) < length).astype(F32)
@@ -401,9 +348,8 @@
     delta_ref[...] = delta
     drive[...] = delta * act_ref[...].astype(F32)
     b_ref[...] = spread(sel[:, rank : rank + states], states)
-    decay_rows(dl_ref, rate_ref, log2e)
-
-    for group in range(width // lanes):
+
+    for group in range(half // lanes):
         here = slice(group * lanes, (group + 1) * lanes)
 
         def advance(step, carry):
@@ -420,7 +366,7 @@
             reach_ref[n, :, here] = ends[n]
 
     total = span_sum_kernel_part(delta_ref, steps)
-    index2 = span_index((spans, width))
+    index2 = span_index((spans, half))
     part = total
     shift = 1
     while shift < spans:
@@ -438,33 +384,22 @@
     low = (sums - high.astype(F32) - mid.astype(F32)).astype(BF16)
     ends = jnp.concatenate([reach_ref[n, spans - 1 : spans, :] for n in range(states)], axis=0)
     extra = jnp.concatenate(
-        [high.astype(F32), mid.astype(F32), low.astype(F32), jnp.zeros((5, width), F32)], axis=0
-    )
-    send_ref[...] = jnp.concatenate([ends, extra], axis=0).astype(BF16)
-
-
-def segment_sum(table_ref, index, states):
-    block = table_ref[index].astype(F32)
-    return block[:states], block[states : states + 1] + block[states + 1 : states + 2] + block[states + 2 : states + 3]
-
-
-def forward_out_kernel(
-    table_ref, parents_ref, dl_ref, reach_ref, cum_ref, delta_ref, act_ref, sel_ref,
-    hid_ref, wg_ref, wgo_ref, skip_ref, ow_ref, owo_ref,
-    starts_ref, mpre_ref, gate_ref, mixed_ref, part_ref,
-    finals, drive, b_ref, c_ref, rate_ref, *, rank
-):
-    rows, width = act_ref.shape
-    steps = rows // spans
-    states = dl_ref.shape[0]
-    count = table_ref.shape[0]
-    me = lax.axis_index("seq")
-    decay_rows(dl_ref, rate_ref, log2e)
+        [high.astype(F32), mid.astype(F32), low.astype(F32), jnp.zeros((5, half), F32)], axis=0
+    )
+    map_ref[...] = jnp.concatenate([ends, extra], axis=0).astype(BF16)
+    map_copies = to_all(map_ref, table_ref, map_send, map_recv)
+    for copy in (wg_first, wg_second):
+        copy.wait()
+    gate = dot(hid_ref[0], wg_ref[...]) + dot(hid_ref[1], wgo_ref[...])
+    gate_ref[...] = gate
+    c_ref[...] = spread(sel[:, rank + states : rank + 2 * states], states)
+    for copy in map_copies:
+        copy.wait()
     rate = -jnp.exp(dl_ref[...]) * log2e
 
     def start_of(target):
-        above = parents_ref[target]
-        return finals[jnp.maximum(above, 0)] * (above >= 0).astype(F32)
+        higher = parents_ref[target]
+        return finals[jnp.maximum(higher, 0)] * (higher >= 0).astype(F32)
 
     def visit(target, carry):
         end, total = segment_sum(table_ref, target, states)
@@ -474,17 +409,12 @@
     finals[0] = jnp.zeros(finals.shape[1:], F32)
     lax.fori_loop(0, count, visit, 0)
     start = start_of(me)
-    sel = sel_ref[...]
-    drive[...] = delta_ref[...] * act_ref[...].astype(F32)
-    b_ref[...] = spread(sel[:, rank : rank + states], states)
-    c_ref[...] = spread(sel[:, rank + states : rank + 2 * states], states)
-    index2 = span_index((spans, width))
-    cum = jnp.where(index2 >= 1, shift_spans(cum_ref[...], 1), 0.0)
+    before = jnp.where(index2 >= 1, shift_spans(cum_ref[...], 1), 0.0)
     for n in range(states):
         earlier = jnp.where(index2 >= 1, shift_spans(reach_ref[n], 1), 0.0)
-        starts_ref[n] = jnp.exp2(cum * rate_ref[n]) * start[n : n + 1, :] + earlier
-
-    for group in range(width // lanes):
+        starts_ref[n] = jnp.exp2(before * rate_ref[n]) * start[n : n + 1, :] + earlier
+
+    for group in range(half // lanes):
         here = slice(group * lanes, (group + 1) * lanes)
 
         def advance(step, carry):
@@ -503,14 +433,14 @@
 
         lax.fori_loop(0, steps, advance, tuple(starts_ref[n, :, here] for n in range(states)))
 
-    gate = dot(hid_ref[0], wg_ref[...]) + dot(hid_ref[1], wgo_ref[...])
-    gate_ref[...] = gate
     mixed_pre = mpre_ref[...] + skip_ref[0:1, :].astype(F32) * act_ref[...].astype(F32)
     mpre_ref[...] = mixed_pre
+    gate = gate_ref[...]
     mixed = (mixed_pre * (gate * sigmoid(gate))).astype(BF16)
     mixed_ref[...] = mixed
     natural = dot(to_tokens(rows, steps), mixed).astype(BF16)
     part_ref[0] = dot(natural, ow_ref[...]).astype(BF16)
+    ow_copy.wait()
     part_ref[1] = dot(natural, owo_ref[...]).astype(BF16)
 
 
@@ -1191,6 +1121,7 @@
     row = lax.axis_index("row")
     col = lax.axis_index("col")
     me = lax.axis_index("seq")
+
     def halves(value, axis):
         size = value.shape[axis] // 2
         own = lax.dynamic_slice_in_dim(value, col * size, size, axis)
@@ -1200,7 +1131,6 @@
     def rows8(value):
         return jnp.broadcast_to(value[None, :], (8, value.shape[0]))
 
-    swap = [(0, 1), (1, 0)]
     tok, toko = halves(tokens_in, 1)
     tail = lax.dynamic_slice_in_dim(tokens_in, lengths[me] - 8, 8, 0)
     w_own, w_send = halves(in_weight, 2)
@@ -1212,49 +1142,25 @@
     conv_b = rows8(conv_bias)
     step_b = rows8(step_bias)
 
-    tails, wio, gaino = entry_exchange(tail, wi_send, gain, count)
-    wg_send, wio = lax.optimization_barrier((wg_send, wio))
-    wgo = lax.ppermute(wg_send, "col", swap)
-    tails_own, tails_oth = halves(tails, 2)
-
-    hid, hid_tail, ext, act, sel_part = run_kernel(
-        forward_in_kernel,
+    dma = pltpu.SemaphoreType.DMA
+    (
+        hid, hid_tail, ext, act, sel, delta, step_pre, cum, table, wio, wgo, owo,
+        starts, mixed_pre, gate, mixed, part,
+    ) = run_kernel(
+        forward_kernel,
         (
             struct((2, rows, half), BF16),
             struct((2, 8, half), BF16),
             struct((rows + 3 * spans, inner), F32),
             struct((rows, inner), BF16),
             struct((rows, padded), F32),
-        ),
-        (tok, toko, tails_own, tails_oth, gain, gaino, wi, wio, conv_weight, conv_b, select_weight, parents),
-        "forward_in",
-        flops=2e9,
-    )
-    sel = quad_sum(sel_part, 1, "select_sum")
-    ow_send, sel = lax.optimization_barrier((ow_send, sel))
-    owo = lax.ppermute(ow_send, "col", swap)
-    delta, step_pre, reach, cum, seg_map = run_kernel(
-        forward_ends_kernel,
-        (
             struct((rows, inner), F32),
             struct((rows, inner), F32),
-            struct((states, spans, inner), F32),
             struct((spans, inner), F32),
-            struct((states + 8, inner), BF16),
-        ),
-        (sel, step_weight, step_b, decay_log, act, lengths),
-        "forward_ends",
-        scratch=[
-            pltpu.VMEM((rows, inner), F32),
-            pltpu.VMEM((rows, states * lanes), F32),
-            pltpu.VMEM((states, spans, inner), F32),
-        ],
-        flops=2e9,
-    )
-    table = seq_gather(seg_map, count, 2, "state_gather")
-    starts, mixed_pre, gate, mixed, part = run_kernel(
-        functools.partial(forward_out_kernel, rank=rank),
-        (
+            struct((count, states + 8, inner), BF16),
+            struct(wi_send.shape, BF16),
+            struct(wg_send.shape, BF16),
+            struct(ow_send.shape, BF16),
             struct((states, spans, inner), F32),
             struct((rows, inner), F32),
             struct((rows, inner), F32),
@@ -1262,17 +1168,27 @@
             struct((2, rows, half), BF16),
         ),
         (
-            table, parents, decay_log, reach, cum, delta, act, sel, hid, wg, wgo, skip, ow, owo,
+            tail, wi_send, wg_send, ow_send, gain, tok, toko, wi, wg, ow, conv_weight, conv_b, select_weight,
+            step_weight, step_b, decay_log, skip, parents, lengths,
         ),
-        "forward_out",
+        "forward",
         scratch=[
-            pltpu.VMEM((count, states, inner), F32),
+            pltpu.VMEM((count,) + tail.shape, BF16),
+            pltpu.VMEM(gain.shape, BF16),
+            pltpu.VMEM((rows, padded), F32),
+            pltpu.VMEM((rows, padded), BF16),
+            pltpu.VMEM((rows, padded), BF16),
             pltpu.VMEM((rows, inner), F32),
             pltpu.VMEM((rows, states * lanes), F32),
             pltpu.VMEM((rows, states * lanes), F32),
             pltpu.VMEM((states, spans, inner), F32),
+            pltpu.VMEM((states + 8, inner), BF16),
+            pltpu.VMEM((states, spans, inner), F32),
+            pltpu.VMEM((count, states, inner), F32),
+            dma((7,)), dma((7,)), dma((count,)), dma((count,)), dma((count,)), dma((count,)),
         ],
-        flops=4e9,
+        flops=6e9,
+        collective=0,
     )
     tok_tile = lax.dynamic_slice_in_dim(tok, row * row_len, row_len, 0)
     toko_tile = lax.dynamic_slice_in_dim(toko, row * row_len, row_len, 0)

time: 230 us -> 219 us (0.952)
  Pallas kernels: 203 us -> 193 us
    pallas_call x9 -> x4, Pallas kernels: 203 us -> 193 us  [run_kernel(): pl.pallas_call(kernel, out_shape=outs, in_specs=[smem_spec() if a.dtype =...]
    broadcast_in_dim x4, local copies, waits for them, and re-layouts: 2.44 us -> 5.1 us  [rows8(): return jnp.broadcast_to(value[None, :], (8, value.shape[0]))]
  transfers between devices with their start and end apart: 2 -> 0, of which waited for: 0 -> 0; matrix products, arithmetic and copies ran while one was open for 4% -> 0% of each run, Pallas kernels for 14% -> 0%
where the time goes in v6:
time: 219 us
  Pallas kernels  193 us (88%)
  local copies, waits for them, and re-layouts  23.9 us (11%)
    pallas_call x4, Pallas kernels, run_kernel(): pl.pallas_call(kernel, out_shape=outs, in_specs=[smem_spec() if a.dtype =...  193 us
    slice x1, local copies, waits for them, and re-layouts, on_device(): wi, wg = (w_own[:, 0], w_own[:, 1])  5.12 us
    broadcast_in_dim x4, local copies, waits for them, and re-layouts, rows8(): return jnp.broadcast_to(value[None, :], (8, value.shape[0]))  5.1 us

profile of v6, /device:TPU:0, one launch (start us, length us, event | category | flops | bytes accessed | tf_op | source)
XLA Modules:
  0.0 218.8 jit_solution(260524052656696309)
XLA Ops:
  0.6 0.0 copy-start.1
  0.7 1.3 dynamic_slice.33
  3.3 1.3 broadcast_in_dim.8.gain_ref
  4.6 1.3 broadcast_in_dim.9.cb_ref
  5.9 1.3 broadcast_in_dim.11.skip_ref
  7.1 1.3 broadcast_in_dim.10.tb_ref
  8.4 1.4 constant_dynamic-slice_fusion.9.tail_ref
  9.8 1.7 copy.29.sw_ref
  11.4 2.3 %fusion = (bf16[256,512]{1,0:T(8,128)(2,1)}, bf16[256,512]{1,0:T(8,128)(2,1)}, bf16[256,512]{1,0:T(8,128)(2,1)}) fusion(bf16[512,1024]{1,0:T(8,128)(2,1)} %param.15, s32[]{:T(128)S(6)} %select_n.32, s32[]{:T(128)S(6)} %select_n.34, s32[]{:T(128)S(6)} %select_n.33, bf16[512,512]{1,0:T(8,128)(2,1)} %param.16, s32[]{:T(128)S(6)} %select_n.31), kind=kLoop, calls=%fused_computation.14 | loop fusion | bytes 1572880 | tf_op jit(solution)/shard_map/dynamic_slice | solution.py:1194
  13.7 0.0 copy-done.1
  13.7 0.0 copy-start
  13.7 2.7 %constant_dynamic-slice_fusion.3 = (bf16[512,512]{1,0:T(8,128)(2,1)}, bf16[512,512]{1,0:T(8,128)(2,1)}, bf16[512,512]{1,0:T(8,128)(2,1)}, bf16[512,512]{1,0:T(8,128)(2,1)}) fusion(bf16[1024,512]{1,0:T(8,128)(2,1)} %param.26, s32[]{:T(128)S(6)} %select_n.30, s32[]{:T(128)S(6)} %select_n.29, bf16[512,1024]{1,0:T(8,128)(2,1)S(1)} %copy-done.1), kind=kLoop, calls=%fused_computation.7 | loop fusion | bytes 4194312 | tf_op jit(solution)/shard_map/dynamic_slice | solution.py:1127
  16.5 0.0 copy-done
  16.5 5.1 %constant_dynamic-slice_fusion.4 = (bf16[512,1,512]{2,1,0:T(2,128)(2,1)S(1)}, bf16[512,1,512]{2,1,0:T(2,128)(2,1)S(1)}, bf16[512,1,512]{2,1,0:T(2,128)(2,1)S(1)}, bf16[512,1,512]{2,1,0:T(2,128)(2,1)S(1)}) fusion(bf16[512,2,1024]{2,1,0:T(2,128)(2,1)S(1)} %copy-done, s32[]{:T(128)S(6)} %add.38, s32[]{:T(128)S(6)} %select_n.30, s32[]{:T(128)S(6)} %select_n.29), kind=kLoop, calls=%fused_computation.8 | loop fusion | bytes 4194316 | tf_op jit(solution)/shard_map/slice | solution.py:1137
  21.6 1.3 copy_bitcast_fusion
  22.9 1.2 copy_bitcast_fusion.2
  24.1 54.4 %forward.1 = (bf16[2,512,512]{2,1,0:T(8,128)(2,1)}, bf16[2,8,512]{2,1,0:T(8,128)(2,1)}, f32[536,512]{1,0:T(8,128)}, bf16[512,512]{1,0:T(8,128)(2,1)}, f32[512,12...) custom-call(bf16[8,1024]{1,0:T(8,128)(2,1)} %constant_dynamic-slice_, ...), custom_call_target="tpu_custom_call" | custom-call | flops 6000000000 | bytes 4444224 | tf_op jit(solution)/shard_map/forward/pallas_call | solution.py:101
  78.5 21.1 %middle_exchange.1 = (bf16[256,512]{1,0:T(8,128)(2,1)}, f32[256,512]{1,0:T(8,128)}, bf16[2,512,512]{2,1,0:T(8,128)(2,1)}) custom-call(bf16[2,512,512]{2,1,0:T(8,128)(2,1)} %get-tuple-element.48.part_ref, bf16[256,512]{1,0:T(8,128)(2,1)} %get-tuple-element.101.tok_ref, bf16[256,512]{1,0:T(8,128)(2,1)} %get-tuple-element.112.teach_ref, s32[8]{0:T(128)} %ints_ref.1), custom_call_target="tpu_custom_call" | custom-call | bytes 1572896 | tf_op jit(solution)/shard_map/middle_exchange/pallas_call | solution.py:101
  99.6 111.1 %backward.1 = (bf16[6,8,64,512]{3,2,1,0:T(8,128)(2,1)}, f32[8,24,512]{2,1,0:T(8,128)}, f32[256,512]{1,0:T(8,128)}, f32[8,512]{1,0:T(8,128)}) custom-call(bf16[2,512,512]{2,1,0:T(8,128)(2,1)} %get-tuple-element.49.cotangent_ref, bf16[512,512]{1,0:T(8,128)(2,1)} %get-tuple-element.50.mixed_ref, bf16[512,512]{1,0:T(8,128)(2,1)} %get-tuple-element.102.ow_ref, ...), custom_call_target="tpu_custom_call" | custom-call | flops 16000000000 | bytes 13611072 | tf_op jit(solution)/shard_map/backward/pallas_call | solution.py:101
  210.6 6.4 %final.1 = (bf16[256,512]{1,0:T(8,128)(2,1)}, f32[256,512]{1,0:T(8,128)}, f32[512]{0:T(512)}, f32[8192,128]{1,0:T(8,128)}, f32[4,512]{1,0:T(4,128)}, /*index=5*/...) custom-call(bf16[6,8,64,512]{3,2,1,0:T(8,128)(2,1)} %get-tuple-eleme, ...), custom_call_target="tpu_custom_call" | custom-call | bytes 4341760 | tf_op jit(solution)/shard_map/final/pallas_call | solution.py:101
  217.1 1.8 copy.32
Async XLA Ops:
  0.6 13.1 %copy-start.1 = (bf16[512,1024]{1,0:T(8,128)(2,1)S(1)}, bf16[512,1024]{1,0:T(8,128)(2,1)}, u32[]{:S(2)}) copy-start(bf16[512,1024]{1,0:T(8,128)(2,1)} %param.15) | copy-start | bytes 3145732
  13.7 2.7 %copy-start = (bf16[512,2,1024]{2,1,0:T(2,128)(2,1)S(1)}, bf16[512,2,1024]{2,1,0:T(2,128)(2,1)}, u32[]{:S(2)}) copy-start(bf16[512,2,1024]{2,1,0:T(2,128)(2,1)} %param.18) | copy-start | bytes 6291460

commit v7 on v6

--- a/solution.py
+++ b/solution.py
@@ -1128,8 +1128,8 @@
         other = lax.dynamic_slice_in_dim(value, (1 - col) * size, size, axis)
         return own, other
 
-    def rows8(value):
-        return jnp.broadcast_to(value[None, :], (8, value.shape[0]))
+    def one_row(value):
+        return value[None, :]
 
     tok, toko = halves(tokens_in, 1)
     tail = lax.dynamic_slice_in_dim(tokens_in, lengths[me] - 8, 8, 0)
@@ -1137,10 +1137,10 @@
     wi, wg = w_own[:, 0], w_own[:, 1]
     wi_send, wg_send = w_send[:, 0], w_send[:, 1]
     ow, ow_send = halves(out_weight, 0)
-    gain = rows8(norm_gain)
-    skip = rows8(skip_gain)
-    conv_b = rows8(conv_bias)
-    step_b = rows8(step_bias)
+    gain = one_row(norm_gain)
+    skip = one_row(skip_gain)
+    conv_b = one_row(conv_bias)
+    step_b = one_row(step_bias)
 
     dma = pltpu.SemaphoreType.DMA
     (

time: 219 us -> 218 us (level)
  no operation moved by 1% of the time
where the time goes in v7:
time: 218 us
  Pallas kernels  192 us (88%)
  local copies, waits for them, and re-layouts  23.8 us (11%)
    pallas_call x4, Pallas kernels, run_kernel(): pl.pallas_call(kernel, out_shape=outs, in_specs=[smem_spec() if a.dtype =...  192 us
    slice x1, local copies, waits for them, and re-layouts, on_device(): wi, wg = (w_own[:, 0], w_own[:, 1])  5.12 us
    broadcast_in_dim x4, local copies, waits for them, and re-layouts, one_row(): return value[None, :]  5.04 us

profile of v7, /device:TPU:0, one launch (start us, length us, event | category | flops | bytes accessed | tf_op | source)
XLA Modules:
  0.0 217.6 jit_solution(6646623465628997123)
XLA Ops:
  0.6 0.0 copy-start.1
  0.7 1.3 dynamic_slice.33
  3.3 1.3 broadcast_in_dim.12.gain_ref
  4.6 1.3 broadcast_in_dim.13.cb_ref
  5.8 1.3 broadcast_in_dim.15.skip_ref
  7.1 1.3 broadcast_in_dim.14.tb_ref
  8.3 1.4 constant_dynamic-slice_fusion.9.tail_ref
  9.7 1.7 copy.29.sw_ref
  11.4 2.3 %fusion = (bf16[256,512]{1,0:T(8,128)(2,1)}, bf16[256,512]{1,0:T(8,128)(2,1)}, bf16[256,512]{1,0:T(8,128)(2,1)}) fusion(bf16[512,1024]{1,0:T(8,128)(2,1)} %param.15, s32[]{:T(128)S(6)} %select_n.32, s32[]{:T(128)S(6)} %select_n.34, s32[]{:T(128)S(6)} %select_n.33, bf16[512,512]{1,0:T(8,128)(2,1)} %param.16, s32[]{:T(128)S(6)} %select_n.31), kind=kLoop, calls=%fused_computation.14 | loop fusion | bytes 1572880 | tf_op jit(solution)/shard_map/dynamic_slice | solution.py:1194
  13.6 0.0 copy-done.1
  13.7 0.0 copy-start
  13.7 2.7 %constant_dynamic-slice_fusion.3 = (bf16[512,512]{1,0:T(8,128)(2,1)}, bf16[512,512]{1,0:T(8,128)(2,1)}, bf16[512,512]{1,0:T(8,128)(2,1)}, bf16[512,512]{1,0:T(8,128)(2,1)}) fusion(bf16[1024,512]{1,0:T(8,128)(2,1)} %param.26, s32[]{:T(128)S(6)} %select_n.30, s32[]{:T(128)S(6)} %select_n.29, bf16[512,1024]{1,0:T(8,128)(2,1)S(1)} %copy-done.1), kind=kLoop, calls=%fused_computation.7 | loop fusion | bytes 4194312 | tf_op jit(solution)/shard_map/dynamic_slice | solution.py:1127
  16.4 0.0 copy-done
  16.4 5.1 %constant_dynamic-slice_fusion.4 = (bf16[512,1,512]{2,1,0:T(2,128)(2,1)S(1)}, bf16[512,1,512]{2,1,0:T(2,128)(2,1)S(1)}, bf16[512,1,512]{2,1,0:T(2,128)(2,1)S(1)}, bf16[512,1,512]{2,1,0:T(2,128)(2,1)S(1)}) fusion(bf16[512,2,1024]{2,1,0:T(2,128)(2,1)S(1)} %copy-done, s32[]{:T(128)S(6)} %add.38, s32[]{:T(128)S(6)} %select_n.30, s32[]{:T(128)S(6)} %select_n.29), kind=kLoop, calls=%fused_computation.8 | loop fusion | bytes 4194316 | tf_op jit(solution)/shard_map/slice | solution.py:1137
  21.5 1.3 copy_bitcast_fusion
  22.8 1.2 copy_bitcast_fusion.2
  24.0 53.2 %forward.1 = (bf16[2,512,512]{2,1,0:T(8,128)(2,1)}, bf16[2,8,512]{2,1,0:T(8,128)(2,1)}, f32[536,512]{1,0:T(8,128)}, bf16[512,512]{1,0:T(8,128)(2,1)}, f32[512,12...) custom-call(bf16[8,1024]{1,0:T(8,128)(2,1)} %constant_dynamic-slice_, ...), custom_call_target="tpu_custom_call" | custom-call | flops 6000000000 | bytes 4415552 | tf_op jit(solution)/shard_map/forward/pallas_call | solution.py:101
  77.3 21.1 %middle_exchange.1 = (bf16[256,512]{1,0:T(8,128)(2,1)}, f32[256,512]{1,0:T(8,128)}, bf16[2,512,512]{2,1,0:T(8,128)(2,1)}) custom-call(bf16[2,512,512]{2,1,0:T(8,128)(2,1)} %get-tuple-element.48.part_ref, bf16[256,512]{1,0:T(8,128)(2,1)} %get-tuple-element.101.tok_ref, bf16[256,512]{1,0:T(8,128)(2,1)} %get-tuple-element.112.teach_ref, s32[8]{0:T(128)} %ints_ref.1), custom_call_target="tpu_custom_call" | custom-call | bytes 1572896 | tf_op jit(solution)/shard_map/middle_exchange/pallas_call | solution.py:101
  98.3 111.1 %backward.1 = (bf16[6,8,64,512]{3,2,1,0:T(8,128)(2,1)}, f32[8,24,512]{2,1,0:T(8,128)}, f32[256,512]{1,0:T(8,128)}, f32[8,512]{1,0:T(8,128)}) custom-call(bf16[2,512,512]{2,1,0:T(8,128)(2,1)} %get-tuple-element.49.cotangent_ref, bf16[512,512]{1,0:T(8,128)(2,1)} %get-tuple-element.50.mixed_ref, bf16[512,512]{1,0:T(8,128)(2,1)} %get-tuple-element.102.ow_ref, ...), custom_call_target="tpu_custom_call" | custom-call | flops 16000000000 | bytes 13589568 | tf_op jit(solution)/shard_map/backward/pallas_call | solution.py:101
  209.4 6.4 %final.1 = (bf16[256,512]{1,0:T(8,128)(2,1)}, f32[256,512]{1,0:T(8,128)}, f32[512]{0:T(512)}, f32[8192,128]{1,0:T(8,128)}, f32[4,512]{1,0:T(4,128)}, /*index=5*/...) custom-call(bf16[6,8,64,512]{3,2,1,0:T(8,128)(2,1)} %get-tuple-eleme, ...), custom_call_target="tpu_custom_call" | custom-call | bytes 4341760 | tf_op jit(solution)/shard_map/final/pallas_call | solution.py:101
  215.8 1.8 copy.32
Async XLA Ops:
  0.6 13.0 %copy-start.1 = (bf16[512,1024]{1,0:T(8,128)(2,1)S(1)}, bf16[512,1024]{1,0:T(8,128)(2,1)}, u32[]{:S(2)}) copy-start(bf16[512,1024]{1,0:T(8,128)(2,1)} %param.15) | copy-start | bytes 3145732
  13.7 2.7 %copy-start = (bf16[512,2,1024]{2,1,0:T(2,128)(2,1)S(1)}, bf16[512,2,1024]{2,1,0:T(2,128)(2,1)}, u32[]{:S(2)}) copy-start(bf16[512,2,1024]{2,1,0:T(2,128)(2,1)} %param.18) | copy-start | bytes 6291460
